TPU v7x, 128 devices: a whole 4x4x4 slice. The times are simulated.
128 devices in a mesh: inner: 8 (over z, core), outer: 16 (over x, y).
Axes of the slice: x: 4, y: 4, z: 4, core: 2. Of those that a mesh axis runs over, the one named last changes fastest.
Arguments:
- inner_state: float32 [2, 32, 2048], P(None, 'inner', 'outer'), may hold values from -6 to 6
- outer_state: float32 [2, 1280, 8192], P(None, 'inner', 'outer'), may hold values from -6 to 6
- energies: float32 [32, 2048], P('inner', 'outer'), may hold values from -2 to 2
- dipole: float32 [32, 2048, 2048], P('inner', 'outer'), may hold values from -0.125 to 0.125
- surface: float32 [32, 40, 2048], P('inner', None, 'outer'), may hold values from -0.125 to 0.125
- thresholds: float32 [1280], P('inner'), may hold values from 0 to 2
- coupling_coef: float32 [32, 40, 40], P('inner'), may hold values from -1 to 1
- coupling_pattern: int32 [32, 40, 40], P('inner'), may hold values 0 or 1
- block_sizes: int32 [32], P('inner'), may hold values from 1 to 2048, 61440 in all
- field_strength: float32 [2], replicated, may hold values from 0.5 to 2
Outputs:
- inner_final: float32 [2, 32, 2048], P(None, 'inner', 'outer')
- outer_final: float32 [2, 1280, 8192], P(None, 'inner', 'outer')
All inputs are finite; a program needn't handle non-finite values. No bound on the sum of `coupling_pattern` or of `block_sizes` on one device may be relied on, other than what follows from the above.
Results may differ from a plain program's by a relative error of at most 0.0001.
Values sent between devices are 32-bit elements; how exact they have to be, the bound alone decides.
No kernel may reach another device: no remote copies, remote signals or barrier semaphores. Data moves between devices by JAX's collectives and lax.ppermute only.
A program may use at most 128 MiB of HBM per device.

v0:
```python
import functools

import jax
import jax.numpy as jnp
from jax import lax
from jax.sharding import Mesh
from jax.sharding import PartitionSpec as P

STEPS = 2
ORDER = 4
OUTER = ("outer_0", "outer_1")


kinetic_scale = 3.125
time_step = 0.1


def cut_along(shard, dim, length):
    dims = shard.shape
    tiles = shard.reshape(*dims[:dim], length, dims[dim] // length, *dims[dim + 1 :])
    return jnp.moveaxis(tiles, dim, 0)


def sum_at_owner(shard, axis, dim):
    tiles = cut_along(shard, dim, lax.axis_size(axis))
    arrived = lax.all_to_all(tiles, axis, split_axis=0, concat_axis=0, tiled=True)
    return arrived.sum(axis=0)


def one_axis_at_a_time(shard, axes):
    return functools.reduce(lax.psum, axes, shard)


def from_behind(block, axis, distance):
    devices = range(lax.axis_size(axis))
    route = [(i - distance, i) for i in devices if i - distance in devices]
    return lax.ppermute(block, axis, route)


def laid_out(tiles, dim):
    tiles = jnp.moveaxis(tiles, 0, dim)
    dims = tiles.shape
    return tiles.reshape(*dims[:dim], dims[dim] * dims[dim + 1], *dims[dim + 2 :])


def from_everyone(shard, axis):
    copies = jnp.broadcast_to(shard, (lax.axis_size(axis), *shard.shape))
    return lax.all_to_all(copies, axis, split_axis=0, concat_axis=0, tiled=True)


def gathered_copies(shard, axis, dim):
    return laid_out(from_everyone(shard, axis), dim)


def broadcast_by_axis(shard, axes, root):
    shard = jnp.where(lax.axis_index(axes) == root, shard, jnp.zeros_like(shard))
    for axis in axes:
        shard = lax.psum(shard, axis)
    return shard


def with_halo(cells, sides, width):
    for axis, dim in sides:
        count = lax.axis_size(axis)
        ends = count - 1
        head = lax.slice_in_dim(cells, 0, width, axis=dim)
        tail = lax.slice_in_dim(cells, cells.shape[dim] - width, cells.shape[dim], axis=dim)
        cells = jnp.concatenate(
            [
                lax.ppermute(tail, axis, [(i, (i + 1) % count) for i in range(ends)]),
                cells,
                lax.ppermute(head, axis, [((i + 1) % count, i) for i in range(ends)]),
            ],
            axis=dim,
        )
    return cells


def reduce_partials(partial_terms, partial_boundary):
    own_terms = sum_at_owner(partial_terms, OUTER, 2)
    boundary = one_axis_at_a_time(partial_boundary, OUTER)
    return (own_terms, boundary)


def local(
    inner_state,
    outer_state,
    energies,
    dipole,
    surface,
    thresholds,
    coupling_coef,
    coupling_pattern,
    block_sizes,
    field_strength,
):
    highest = lax.Precision.HIGHEST
    blocks = dipole.shape[0]
    row_count = dipole.shape[1]
    channels = coupling_coef.shape[1]
    radial = outer_state.shape[2]
    sector_index = lax.axis_index(OUTER)
    row_index = sector_index * row_count + jnp.arange(row_count, dtype=jnp.int32)
    live_rows = (row_index[None, :] < block_sizes[:, None]).astype(jnp.float32)
    coupling = coupling_coef * coupling_pattern.astype(jnp.float32)
    first_sector = jnp.where(sector_index == 0, 1.0, 0.0).astype(jnp.float32)
    edge_mask = first_sector * (jnp.arange(radial, dtype=jnp.int32) == 0).astype(jnp.float32)
    current = (inner_state * live_rows, outer_state)
    for time_index in range(STEPS):
        strength = field_strength[time_index]
        taylor_term = current
        accumulated = current
        for power in range(1, ORDER + 1):
            inner_part = taylor_term[0]
            outer_part = taylor_term[1]
            channel_grid = outer_part.reshape(2, blocks, channels, radial)
            next_first, next_channels = from_behind(
                (inner_part[:, 0], channel_grid[:, 0]), "inner", -1
            )
            extended = jnp.concatenate([inner_part, next_first[:, None]], axis=1)
            gathered = gathered_copies(extended, OUTER, 2)
            edge_values = broadcast_by_axis(outer_part[:, :, 0], OUTER, 0)
            forward = jnp.einsum("lij,plj->pli", dipole, gathered[:, 1:], precision=highest)
            grid_next = jnp.concatenate([channel_grid[:, 1:], next_channels[:, None]], axis=1)
            upward = jnp.einsum("lab,plbr->plar", coupling, grid_next, precision=highest)
            partial_boundary = jnp.einsum("lcs,pls->plc", surface, inner_part, precision=highest)
            partial_terms = jnp.einsum("lji,plj->pli", dipole, inner_part, precision=highest)
            summed_terms, boundary = reduce_partials(partial_terms, partial_boundary)
            lowered = jnp.einsum("lba,plbr->plar", coupling, channel_grid, precision=highest)
            carried, carried_grid = from_behind(
                (summed_terms[:, blocks - 1], lowered[:, blocks - 1]), "inner", 1
            )
            backward = jnp.concatenate([carried[:, None], summed_terms[:, : blocks - 1]], axis=1)
            downward = jnp.concatenate([carried_grid[:, None], lowered[:, : blocks - 1]], axis=1)
            first_point = edge_values.reshape(2, blocks, channels)
            surf_term = jnp.einsum("lcs,plc->pls", surface, first_point, precision=highest)
            inner_image = live_rows * (
                energies * inner_part + strength * (forward + backward) - kinetic_scale * surf_term
            )
            padded = with_halo(outer_part, ((OUTER, 2),), 1)
            left_cells = (
                padded[:, :, :radial]
                + edge_mask[None, None, :] * boundary.reshape(2, blocks * channels)[:, :, None]
            )
            right_cells = padded[:, :, 2:]
            kinetic = kinetic_scale * (2.0 * outer_part - left_cells - right_cells)
            outer_image = (
                kinetic
                + thresholds[None, :, None] * outer_part
                + strength * (upward + downward).reshape(2, blocks * channels, radial)
            )
            inner_image, outer_image = (inner_image, outer_image)
            factor = time_step / power
            taylor_term = (
                factor * jnp.stack([inner_image[1], -inner_image[0]]),
                factor * jnp.stack([outer_image[1], -outer_image[0]]),
            )
            accumulated = (accumulated[0] + taylor_term[0], accumulated[1] + taylor_term[1])
        current = accumulated
    return (current[0], current[1])


def solution(mesh):
    torus = Mesh(mesh.devices.reshape(mesh.shape["inner"], 4, 4), ("inner", "outer_0", "outer_1"))
    placed = (
        P(None, "inner", OUTER),
        P(None, "inner", OUTER),
        P("inner", OUTER),
        P("inner", OUTER, None),
        P("inner", None, OUTER),
        P("inner"),
        P("inner", None, None),
        P("inner", None, None),
        P("inner"),
        P(),
    )
    return jax.shard_map(
        local,
        mesh=torus,
        in_specs=placed,
        out_specs=(P(None, "inner", OUTER), P(None, "inner", OUTER)),
        check_vma=False,
    )
```

profile of v0, /device:TPU:88, one launch (start us, length us, event | category | flops | bytes accessed | tf_op | source)
XLA Modules:
  0.0 597.7 jit_solution(16005529261771589149)
XLA Ops:
  4.3 4.3 convolution_bitcast_fusion.23
  9.2 7.2 %all-to-all-start.1 = ((f32[16,2,4,128]{3,1,2,0:T(2,128)}), f32[16,2,4,128]{3,1,2,0:T(2,128)S(1)}, u32[]{:S(2)}, u32[]{:S(2)}) async-start(f32[16,2,4,128]{3,1,2,0:T(2,128)} %bitcast.496), calls=%async_computation.1 | async-start | bytes 131072 | tf_op jit(solution)/shard_map/all_to_all | solution.py:26
  19.1 3.4 collective-permute-start.4
  29.9 10.5 %all-reduce.15 = (f32[2,4,40]{2,0,1:T(2,128)S(1)}, f32[2,160]{1,0:T(2,128)S(1)}) all-reduce(f32[2,4,40]{2,0,1:T(2,128)S(1)} %convolution_bitcast_fusion.39, f32[2,160]{1,0:T(2,128)S(1)} %get-tuple-element.77), channel_id=1, replica_groups=mesh['inner'=8,'outer_0'=4,'outer_1'=4] {'outer_0'}, use_global_device_ids=true, to_apply=%region_4.5 | all-reduce | flops 640 | bytes 5120 | tf_op jit(solution)/shard_map/psum | solution.py:31
  40.6 9.3 %all-reduce.7 = (f32[2,160]{1,0:T(2,128)S(1)}, f32[2,4,40]{2,0,1:T(2,128)S(1)}) all-reduce(f32[2,160]{1,0:T(2,128)S(1)} %mul.604, f32[2,4,40]{2,0,1:T(2,128)S(1)} %copy.65), channel_id=1, replica_groups=mesh['inner'=8,'outer_0'=4,'outer_1'=4] {'outer_1'}, use_global_device_ids=true, to_apply=%region_5.6 | all-reduce | flops 640 | bytes 5120 | tf_op jit(solution)/shard_map/psum | solution.py:31
  50.6 5.1 all-to-all-start
  57.7 3.9 all-to-all-done
  61.5 5.4 convolution_bitcast_fusion.31
  72.9 5.4 all-to-all-start.3
  78.3 5.8 all-to-all-done.3
  84.7 5.3 all-to-all-start.2
  92.2 3.6 all-to-all-done.2
  95.8 5.2 convolution_bitcast_fusion.30
  105.0 8.8 %all-reduce.14 = (f32[2,4,40]{2,0,1:T(2,128)S(1)}, f32[2,160]{1,0:T(2,128)S(1)}) all-reduce(f32[2,4,40]{2,0,1:T(2,128)S(1)} %convolution_bitcast_fusion.38, f32[2,160]{1,0:T(2,128)S(1)} %get-tuple-element.72), channel_id=1, replica_groups=mesh['inner'=8,'outer_0'=4,'outer_1'=4] {'outer_0'}, use_global_device_ids=true, to_apply=%region_9.10 | all-reduce | flops 640 | bytes 5120 | tf_op jit(solution)/shard_map/psum | solution.py:31
  114.0 9.2 %all-reduce.6 = (f32[2,160]{1,0:T(2,128)}, f32[2,4,40]{2,0,1:T(2,128)S(1)}) all-reduce(f32[2,160]{1,0:T(2,128)S(1)} %mul.626, f32[2,4,40]{2,0,1:T(2,128)S(1)} %copy.74), channel_id=1, replica_groups=mesh['inner'=8,'outer_0'=4,'outer_1'=4] {'outer_1'}, use_global_device_ids=true, to_apply=%region_10.11 | all-reduce | flops 640 | bytes 5120 | tf_op jit(solution)/shard_map/psum | solution.py:31
  124.0 4.3 convolution_bitcast_fusion.21
  134.9 3.3 collective-permute-start.12
  138.9 5.7 all-to-all-start.5
  144.6 3.4 collective-permute-start.10
  151.1 7.3 %all-to-all-start.4 = ((f32[16,2,5,128]{3,1,2,0:T(2,128)}), f32[16,2,5,128]{3,1,2,0:T(2,128)S(1)}, u32[]{:S(2)}, u32[]{:S(2)}) async-start(f32[16,2,5,128]{3,1,2,0:T(2,128)} %broadcast_in_dim.164), calls=%async_computation.4 | async-start | bytes 163840 | tf_op jit(solution)/shard_map/all_to_all | solution.py:48
  160.5 3.8 all-to-all-done.4
  164.3 5.2 convolution_bitcast_fusion.29
  176.1 8.9 %all-reduce.13 = (f32[2,4,40]{2,0,1:T(2,128)S(1)}, f32[2,160]{1,0:T(2,128)S(1)}) all-reduce(f32[2,4,40]{2,0,1:T(2,128)S(1)} %convolution_bitcast_fusion.37, f32[2,160]{1,0:T(2,128)S(1)} %get-tuple-element.67), channel_id=1, replica_groups=mesh['inner'=8,'outer_0'=4,'outer_1'=4] {'outer_0'}, use_global_device_ids=true, to_apply=%region_14.15 | all-reduce | flops 640 | bytes 5120 | tf_op jit(solution)/shard_map/psum | solution.py:31
  185.2 9.6 %all-reduce.5 = (f32[2,160]{1,0:T(2,128)}, f32[2,4,40]{2,0,1:T(2,128)S(1)}) all-reduce(f32[2,160]{1,0:T(2,128)S(1)} %mul.648, f32[2,4,40]{2,0,1:T(2,128)S(1)} %copy.80), channel_id=1, replica_groups=mesh['inner'=8,'outer_0'=4,'outer_1'=4] {'outer_1'}, use_global_device_ids=true, to_apply=%region_15.16 | all-reduce | flops 640 | bytes 5120 | tf_op jit(solution)/shard_map/psum | solution.py:31
  195.7 4.3 convolution_bitcast_fusion.20
  210.4 5.7 all-to-all-start.7
  216.1 3.4 collective-permute-start.16
  223.9 7.4 %all-to-all-start.6 = ((f32[16,2,5,128]{3,1,2,0:T(2,128)}), f32[16,2,5,128]{3,1,2,0:T(2,128)S(1)}, u32[]{:S(2)}, u32[]{:S(2)}) async-start(f32[16,2,5,128]{3,1,2,0:T(2,128)} %broadcast_in_dim.169), calls=%async_computation.6 | async-start | bytes 163840 | tf_op jit(solution)/shard_map/all_to_all | solution.py:48
  233.2 3.8 all-to-all-done.6
  237.1 5.3 convolution_bitcast_fusion.28
  249.8 8.9 %all-reduce.12 = (f32[2,4,40]{2,0,1:T(2,128)S(1)}, f32[2,160]{1,0:T(2,128)S(1)}) all-reduce(f32[2,4,40]{2,0,1:T(2,128)S(1)} %copy-done.81, f32[2,160]{1,0:T(2,128)S(1)} %get-tuple-element.62), channel_id=1, replica_groups=mesh['inner'=8,'outer_0'=4,'outer_1'=4] {'outer_0'}, use_global_device_ids=true, to_apply=%region_19.20 | all-reduce | flops 640 | bytes 5120 | tf_op jit(solution)/shard_map/psum | solution.py:31
  258.9 9.2 %all-reduce.4 = (f32[2,160]{1,0:T(2,128)}, f32[2,4,40]{2,0,1:T(2,128)S(1)}) all-reduce(f32[2,160]{1,0:T(2,128)S(1)} %mul.669, f32[2,4,40]{2,0,1:T(2,128)S(1)} %copy.86), channel_id=1, replica_groups=mesh['inner'=8,'outer_0'=4,'outer_1'=4] {'outer_1'}, use_global_device_ids=true, to_apply=%region_20.21 | all-reduce | flops 640 | bytes 5120 | tf_op jit(solution)/shard_map/psum | solution.py:31
  269.1 4.3 convolution_bitcast_fusion.19
  283.6 5.7 all-to-all-start.9
  289.4 3.4 collective-permute-start.22
  297.1 7.4 %all-to-all-start.8 = ((f32[16,2,5,128]{3,1,2,0:T(2,128)}), f32[16,2,5,128]{3,1,2,0:T(2,128)S(1)}, u32[]{:S(2)}, u32[]{:S(2)}) async-start(f32[16,2,5,128]{3,1,2,0:T(2,128)} %broadcast_in_dim.174), calls=%async_computation.8 | async-start | bytes 163840 | tf_op jit(solution)/shard_map/all_to_all | solution.py:48
  310.3 5.9 convolution_bitcast_fusion.27
  322.2 9.5 %all-reduce.11 = (f32[2,4,40]{2,0,1:T(2,128)S(1)}, f32[2,160]{1,0:T(2,128)S(1)}) all-reduce(f32[2,4,40]{2,0,1:T(2,128)S(1)} %copy-done.82, f32[2,160]{1,0:T(2,128)S(1)} %get-tuple-element.57), channel_id=1, replica_groups=mesh['inner'=8,'outer_0'=4,'outer_1'=4] {'outer_0'}, use_global_device_ids=true, to_apply=%region_24.25 | all-reduce | flops 640 | bytes 5120 | tf_op jit(solution)/shard_map/psum | solution.py:31
  331.9 8.6 %all-reduce.3 = (f32[2,160]{1,0:T(2,128)}, f32[2,4,40]{2,0,1:T(2,128)S(1)}) all-reduce(f32[2,160]{1,0:T(2,128)S(1)} %mul.688, f32[2,4,40]{2,0,1:T(2,128)S(1)} %copy.92), channel_id=1, replica_groups=mesh['inner'=8,'outer_0'=4,'outer_1'=4] {'outer_1'}, use_global_device_ids=true, to_apply=%region_25.26 | all-reduce | flops 640 | bytes 5120 | tf_op jit(solution)/shard_map/psum | solution.py:31
  342.0 4.3 convolution_bitcast_fusion.18
  354.7 6.3 %all-to-all-start.11 = ((f32[16,2,4,128]{3,1,2,0:T(2,128)}), f32[16,2,4,128]{3,1,2,0:T(2,128)S(1)}, u32[]{:S(2)}, u32[]{:S(2)}) async-start(f32[16,2,4,128]{3,1,2,0:T(2,128)} %bitcast.527), calls=%async_computation.11 | async-start | bytes 131072 | tf_op jit(solution)/shard_map/all_to_all | solution.py:26
  361.0 3.4 collective-permute-start.28
  372.6 7.4 %all-to-all-start.10 = ((f32[16,2,5,128]{3,1,2,0:T(2,128)}), f32[16,2,5,128]{3,1,2,0:T(2,128)S(1)}, u32[]{:S(2)}, u32[]{:S(2)}) async-start(f32[16,2,5,128]{3,1,2,0:T(2,128)} %broadcast_in_dim.179), calls=%async_computation.10 | async-start | bytes 163840 | tf_op jit(solution)/shard_map/all_to_all | solution.py:48
  382.7 3.4 collective-permute-start.27
  386.1 5.9 convolution_bitcast_fusion.26
  400.3 10.7 %all-reduce.10 = (f32[2,4,40]{2,0,1:T(2,128)S(1)}, f32[2,160]{1,0:T(2,128)S(1)}) all-reduce(f32[2,4,40]{2,0,1:T(2,128)S(1)} %copy-done.79, f32[2,160]{1,0:T(2,128)S(1)} %get-tuple-element.52), channel_id=1, replica_groups=mesh['inner'=8,'outer_0'=4,'outer_1'=4] {'outer_0'}, use_global_device_ids=true, to_apply=%region_29.30 | all-reduce | flops 640 | bytes 5120 | tf_op jit(solution)/shard_map/psum | solution.py:31
  411.1 8.1 %all-reduce.2 = (f32[2,160]{1,0:T(2,128)}, f32[2,4,40]{2,0,1:T(2,128)S(1)}) all-reduce(f32[2,160]{1,0:T(2,128)S(1)} %mul.704, f32[2,4,40]{2,0,1:T(2,128)S(1)} %copy.101), channel_id=1, replica_groups=mesh['inner'=8,'outer_0'=4,'outer_1'=4] {'outer_1'}, use_global_device_ids=true, to_apply=%region_30.31 | all-reduce | flops 640 | bytes 5120 | tf_op jit(solution)/shard_map/psum | solution.py:31
  421.0 4.3 convolution_bitcast_fusion.17
  435.6 6.8 %all-to-all-start.13 = ((f32[16,2,4,128]{3,1,2,0:T(2,128)}), f32[16,2,4,128]{3,1,2,0:T(2,128)S(1)}, u32[]{:S(2)}, u32[]{:S(2)}) async-start(f32[16,2,4,128]{3,1,2,0:T(2,128)} %bitcast.528), calls=%async_computation.13 | async-start | bytes 131072 | tf_op jit(solution)/shard_map/all_to_all | solution.py:26
  442.4 3.4 collective-permute-start.34
  450.1 7.4 %all-to-all-start.12 = ((f32[16,2,5,128]{3,1,2,0:T(2,128)}), f32[16,2,5,128]{3,1,2,0:T(2,128)S(1)}, u32[]{:S(2)}, u32[]{:S(2)}) async-start(f32[16,2,5,128]{3,1,2,0:T(2,128)} %broadcast_in_dim.184), calls=%async_computation.12 | async-start | bytes 163840 | tf_op jit(solution)/shard_map/all_to_all | solution.py:48
  463.3 6.0 convolution_bitcast_fusion.25
  477.0 9.3 %all-reduce.9 = (f32[2,4,40]{2,0,1:T(2,128)S(1)}, f32[2,160]{1,0:T(2,128)S(1)}) all-reduce(f32[2,4,40]{2,0,1:T(2,128)S(1)} %copy-done.80, f32[2,160]{1,0:T(2,128)S(1)} %get-tuple-element.47), channel_id=1, replica_groups=mesh['inner'=8,'outer_0'=4,'outer_1'=4] {'outer_0'}, use_global_device_ids=true, to_apply=%region_34.35 | all-reduce | flops 640 | bytes 5120 | tf_op jit(solution)/shard_map/psum | solution.py:31
  486.5 8.7 %all-reduce.1 = (f32[2,160]{1,0:T(2,128)}, f32[2,4,40]{2,0,1:T(2,128)S(1)}) all-reduce(f32[2,160]{1,0:T(2,128)S(1)} %mul.720, f32[2,4,40]{2,0,1:T(2,128)S(1)} %copy.107), channel_id=1, replica_groups=mesh['inner'=8,'outer_0'=4,'outer_1'=4] {'outer_1'}, use_global_device_ids=true, to_apply=%region_35.36 | all-reduce | flops 640 | bytes 5120 | tf_op jit(solution)/shard_map/psum | solution.py:31
  496.9 4.3 convolution_bitcast_fusion.16
  511.5 6.2 %all-to-all-start.15 = ((f32[16,2,4,128]{3,1,2,0:T(2,128)}), f32[16,2,4,128]{3,1,2,0:T(2,128)S(1)}, u32[]{:S(2)}, u32[]{:S(2)}) async-start(f32[16,2,4,128]{3,1,2,0:T(2,128)} %bitcast.529), calls=%async_computation.15 | async-start | bytes 131072 | tf_op jit(solution)/shard_map/all_to_all | solution.py:26
  517.7 3.4 collective-permute-start.40
  525.4 7.4 %all-to-all-start.14 = ((f32[16,2,5,128]{3,1,2,0:T(2,128)}), f32[16,2,5,128]{3,1,2,0:T(2,128)S(1)}, u32[]{:S(2)}, u32[]{:S(2)}) async-start(f32[16,2,5,128]{3,1,2,0:T(2,128)} %broadcast_in_dim.189), calls=%async_computation.14 | async-start | bytes 163840 | tf_op jit(solution)/shard_map/all_to_all | solution.py:48
  538.6 6.0 %convolution_bitcast_fusion.24 = f32[2,4,128]{2,0,1:T(2,128)} fusion(f32[4,128,2048]{2,1,0:T(8,128)} %param.13, f32[16,2,5,128]{3,1,2,0:T(2,128)S(1)} %all-to-all-done.14), kind=kOutput, calls=%fused_computation.40 | convolution fusion | flops 25165824 | bytes 4280320 | tf_op jit(solution)/shard_map/lij,plj->pli/dot_general | solution.py:123
  554.7 3.6 collective-permute-start.46
  559.2 9.6 %all-reduce.8 = (f32[2,160]{1,0:T(2,128)S(1)}, f32[2,4,40]{2,0,1:T(2,128)S(1)}) all-reduce(f32[2,160]{1,0:T(2,128)S(1)} %get-tuple-element.43, f32[2,4,40]{2,0,1:T(2,128)S(1)} %copy-done.78), channel_id=1, replica_groups=mesh['inner'=8,'outer_0'=4,'outer_1'=4] {'outer_0'}, use_global_device_ids=true, to_apply=%region_36.37 | all-reduce | flops 640 | bytes 5120 | tf_op jit(solution)/shard_map/psum | solution.py:58
  569.0 7.9 %all-reduce = (f32[2,4,40]{2,0,1:T(2,128)S(1)}, f32[2,160]{1,0:T(2,128)S(1)}) all-reduce(f32[2,4,40]{2,0,1:T(2,128)S(1)} %copy.113, f32[2,160]{1,0:T(2,128)S(1)} %mul.734), channel_id=1, replica_groups=mesh['inner'=8,'outer_0'=4,'outer_1'=4] {'outer_1'}, use_global_device_ids=true, to_apply=%region_37.38 | all-reduce | flops 640 | bytes 5120 | tf_op jit(solution)/shard_map/psum | solution.py:58
  579.3 4.7 collective-permute-start.44
  588.7 4.9 collective-permute-done.45
  (528 shorter events, 204.3 us)
Async XLA Ops:
  2.2 47.7 %collective-permute-start = (f32[2,128]{1,0:T(2,128)S(1)}, f32[2,128]{1,0:T(2,128)S(1)}, u32[]{:S(2)}, u32[]{:S(2)}) collective-permute-start(f32[2,128]{1,0:T(2,128)S(1)} %slice_bitcast_fusion.31), channel_id=1, source_target_pairs={{16,0},{32,16},{48,32},{64,48},{80,64},{96,80},{112,96},{17,1},{33... | collective-permute-start | bytes 3080 | tf_op jit(solution)/shard_map/ppermute | solution.py:37
  9.2 40.7 %all-to-all-start.1 = ((f32[16,2,4,128]{3,1,2,0:T(2,128)}), f32[16,2,4,128]{3,1,2,0:T(2,128)S(1)}, u32[]{:S(2)}, u32[]{:S(2)}) async-start(f32[16,2,4,128]{3,1,2,0:T(2,128)} %bitcast.496), calls=%async_computation.1 | async-start | bytes 131072 | tf_op jit(solution)/shard_map/all_to_all | solution.py:26
  16.4 84.7 %collective-permute-start.6 = (f32[2,40,512]{2,1,0:T(8,128)S(1)}, f32[2,40,512]{2,1,0:T(8,128)S(1)}, u32[]{:S(2)}, u32[]{:S(2)}) collective-permute-start(f32[2,40,512]{2,1,0:T(8,128)S(1)} %slice_bitcast_fusion.15), channel_id=1, source_target_pairs={{16,0},{32,16},{48,32},{64,48},{80,64},{96,80},{112,96},{17,1},{33... | collective-permute-start | bytes 491528 | tf_op jit(solution)/shard_map/ppermute | solution.py:37
  19.1 83.4 %collective-permute-start.4 = (f32[2,160,1]{2,1,0:T(8,128)}, f32[2,160,1]{2,1,0:T(8,128)S(1)}, u32[]{:S(2)}, u32[]{:S(2)}) collective-permute-start(f32[2,160,1]{2,1,0:T(8,128)} %get-tuple-element.78), channel_id=1, source_target_pairs={{0,1},{1,2},{2,3},{3,4},{4,5},{5,6},{6,7},{7,8},{8,9},{9,10},{10,1... | collective-permute-start | bytes 3848 | tf_op jit(solution)/shard_map/ppermute | solution.py:70
  22.4 80.1 %collective-permute-start.5 = (f32[2,160,1]{2,1,0:T(8,128)}, f32[2,160,1]{2,1,0:T(8,128)S(1)}, u32[]{:S(2)}, u32[]{:S(2)}) collective-permute-start(f32[2,160,1]{2,1,0:T(8,128)} %get-tuple-element.79), channel_id=1, source_target_pairs={{1,0},{2,1},{3,2},{4,3},{5,4},{6,5},{7,6},{8,7},{9,8},{10,9},{11,1... | collective-permute-start | bytes 3848 | tf_op jit(solution)/shard_map/ppermute | solution.py:72
  26.4 74.7 %collective-permute-start.7 = (f32[2,40,512]{2,1,0:T(8,128)}, f32[2,40,512]{2,1,0:T(8,128)S(1)}, u32[]{:S(2)}, u32[]{:S(2)}) collective-permute-start(f32[2,40,512]{2,1,0:T(8,128)} %slice_bitcast_fusion.14), channel_id=1, source_target_pairs={{0,16},{16,32},{32,48},{48,64},{64,80},{80,96},{96,112},{1,17},{17... | collective-permute-start | bytes 491528 | tf_op jit(solution)/shard_map/ppermute | solution.py:37
  50.6 11.0 %all-to-all-start = ((f32[16,2,5,128]{3,1,2,0:T(2,128)}), f32[16,2,5,128]{3,1,2,0:T(2,128)S(1)}, u32[]{:S(2)}, u32[]{:S(2)}) async-start(f32[16,2,5,128]{3,1,2,0:T(2,128)} %broadcast_in_dim.156), calls=%async_computation | async-start | bytes 163840 | tf_op jit(solution)/shard_map/all_to_all | solution.py:48
  55.7 11.2 %collective-permute-start.1 = (f32[2,128]{1,0:T(2,128)S(1)}, f32[2,128]{1,0:T(2,128)S(1)}, u32[]{:S(2)}, u32[]{:S(2)}) collective-permute-start(f32[2,128]{1,0:T(2,128)S(1)} %slice_bitcast_fusion.30), channel_id=1, source_target_pairs={{0,16},{16,32},{32,48},{48,64},{64,80},{80,96},{96,112},{1,17},{17... | collective-permute-start | bytes 3080 | tf_op jit(solution)/shard_map/ppermute | solution.py:37
  69.9 8.4 %collective-permute-start.2 = (f32[2,128]{1,0:T(2,128)S(1)}, f32[2,128]{1,0:T(2,128)S(1)}, u32[]{:S(2)}, u32[]{:S(2)}) collective-permute-start(f32[2,128]{1,0:T(2,128)S(1)} %slice_bitcast_fusion.29), channel_id=1, source_target_pairs={{16,0},{32,16},{48,32},{64,48},{80,64},{96,80},{112,96},{17,1},{33... | collective-permute-start | bytes 3080 | tf_op jit(solution)/shard_map/ppermute | solution.py:37
  72.9 11.2 %all-to-all-start.3 = ((f32[16,2,4,128]{3,1,2,0:T(2,128)}), f32[16,2,4,128]{3,1,2,0:T(2,128)S(1)}, u32[]{:S(2)}, u32[]{:S(2)}) async-start(f32[16,2,4,128]{3,1,2,0:T(2,128)} %bitcast.494), calls=%async_computation.3 | async-start | bytes 131072 | tf_op jit(solution)/shard_map/all_to_all | solution.py:26
  84.7 11.2 %all-to-all-start.2 = ((f32[16,2,5,128]{3,1,2,0:T(2,128)}), f32[16,2,5,128]{3,1,2,0:T(2,128)S(1)}, u32[]{:S(2)}, u32[]{:S(2)}) async-start(f32[16,2,5,128]{3,1,2,0:T(2,128)} %broadcast_in_dim.159), calls=%async_computation.2 | async-start | bytes 163840 | tf_op jit(solution)/shard_map/all_to_all | solution.py:48
  90.0 33.2 %collective-permute-start.3 = (f32[2,128]{1,0:T(2,128)S(1)}, f32[2,128]{1,0:T(2,128)S(1)}, u32[]{:S(2)}, u32[]{:S(2)}) collective-permute-start(f32[2,128]{1,0:T(2,128)S(1)} %slice_bitcast_fusion.28), channel_id=1, source_target_pairs={{0,16},{16,32},{32,48},{48,64},{64,80},{80,96},{96,112},{1,17},{17... | collective-permute-start | bytes 3080 | tf_op jit(solution)/shard_map/ppermute | solution.py:37
  130.2 20.2 %collective-permute-start.8 = (f32[2,128]{1,0:T(2,128)}, f32[2,128]{1,0:T(2,128)S(1)}, u32[]{:S(2)}, u32[]{:S(2)}) collective-permute-start(f32[2,128]{1,0:T(2,128)} %slice_bitcast_fusion.27), channel_id=1, source_target_pairs={{16,0},{32,16},{48,32},{64,48},{80,64},{96,80},{112,96},{17,1},{33... | collective-permute-start | bytes 3080 | tf_op jit(solution)/shard_map/ppermute | solution.py:37
  132.4 37.2 %collective-permute-start.13 = (f32[2,40,512]{2,1,0:T(8,128)}, f32[2,40,512]{2,1,0:T(8,128)S(1)}, u32[]{:S(2)}, u32[]{:S(2)}) collective-permute-start(f32[2,40,512]{2,1,0:T(8,128)} %slice_bitcast_fusion.12), channel_id=1, source_target_pairs={{0,16},{16,32},{32,48},{48,64},{64,80},{80,96},{96,112},{1,17},{17... | collective-permute-start | bytes 491528 | tf_op jit(solution)/shard_map/ppermute | solution.py:37
  134.9 34.6 %collective-permute-start.12 = (f32[2,40,512]{2,1,0:T(8,128)}, f32[2,40,512]{2,1,0:T(8,128)}, u32[]{:S(2)}, u32[]{:S(2)}) collective-permute-start(f32[2,40,512]{2,1,0:T(8,128)} %slice_bitcast_fusion.13), channel_id=1, source_target_pairs={{16,0},{32,16},{48,32},{64,48},{80,64},{96,80},{112,96},{17,1},{33... | collective-permute-start | bytes 491528 | tf_op jit(solution)/shard_map/ppermute | solution.py:37
  138.9 11.6 %all-to-all-start.5 = ((f32[16,2,4,128]{3,1,2,0:T(2,128)}), f32[16,2,4,128]{3,1,2,0:T(2,128)S(1)}, u32[]{:S(2)}, u32[]{:S(2)}) async-start(f32[16,2,4,128]{3,1,2,0:T(2,128)} %bitcast.492), calls=%async_computation.5 | async-start | bytes 131072 | tf_op jit(solution)/shard_map/all_to_all | solution.py:26
  144.6 27.3 %collective-permute-start.10 = (f32[2,160,1]{2,1,0:T(8,128)}, f32[2,160,1]{2,1,0:T(8,128)}, u32[]{:S(2)}, u32[]{:S(2)}) collective-permute-start(f32[2,160,1]{2,1,0:T(8,128)} %get-tuple-element.73), channel_id=1, source_target_pairs={{0,1},{1,2},{2,3},{3,4},{4,5},{5,6},{6,7},{7,8},{8,9},{9,10},{10,1... | collective-permute-start | bytes 3848 | tf_op jit(solution)/shard_map/ppermute | solution.py:70
  148.0 23.9 %collective-permute-start.11 = (f32[2,160,1]{2,1,0:T(8,128)}, f32[2,160,1]{2,1,0:T(8,128)}, u32[]{:S(2)}, u32[]{:S(2)}) collective-permute-start(f32[2,160,1]{2,1,0:T(8,128)} %get-tuple-element.74), channel_id=1, source_target_pairs={{1,0},{2,1},{3,2},{4,3},{5,4},{6,5},{7,6},{8,7},{9,8},{10,9},{11,1... | collective-permute-start | bytes 3848 | tf_op jit(solution)/shard_map/ppermute | solution.py:72
  151.1 13.2 %all-to-all-start.4 = ((f32[16,2,5,128]{3,1,2,0:T(2,128)}), f32[16,2,5,128]{3,1,2,0:T(2,128)S(1)}, u32[]{:S(2)}, u32[]{:S(2)}) async-start(f32[16,2,5,128]{3,1,2,0:T(2,128)} %broadcast_in_dim.164), calls=%async_computation.4 | async-start | bytes 163840 | tf_op jit(solution)/shard_map/all_to_all | solution.py:48
  158.5 36.2 %collective-permute-start.9 = (f32[2,128]{1,0:T(2,128)S(1)}, f32[2,128]{1,0:T(2,128)S(1)}, u32[]{:S(2)}, u32[]{:S(2)}) collective-permute-start(f32[2,128]{1,0:T(2,128)S(1)} %slice_bitcast_fusion.26), channel_id=1, source_target_pairs={{0,16},{16,32},{32,48},{48,64},{64,80},{80,96},{96,112},{1,17},{17... | collective-permute-start | bytes 3080 | tf_op jit(solution)/shard_map/ppermute | solution.py:37
  201.3 20.7 %collective-permute-start.14 = (f32[2,128]{1,0:T(2,128)S(1)}, f32[2,128]{1,0:T(2,128)S(1)}, u32[]{:S(2)}, u32[]{:S(2)}) collective-permute-start(f32[2,128]{1,0:T(2,128)S(1)} %slice_bitcast_fusion.25), channel_id=1, source_target_pairs={{16,0},{32,16},{48,32},{64,48},{80,64},{96,80},{112,96},{17,1},{33... | collective-permute-start | bytes 3080 | tf_op jit(solution)/shard_map/ppermute | solution.py:37
  204.0 38.4 %collective-permute-start.19 = (f32[2,40,512]{2,1,0:T(8,128)}, f32[2,40,512]{2,1,0:T(8,128)}, u32[]{:S(2)}, u32[]{:S(2)}) collective-permute-start(f32[2,40,512]{2,1,0:T(8,128)} %slice_bitcast_fusion.10), channel_id=1, source_target_pairs={{0,16},{16,32},{32,48},{48,64},{64,80},{80,96},{96,112},{1,17},{17... | collective-permute-start | bytes 491528 | tf_op jit(solution)/shard_map/ppermute | solution.py:37
  206.5 35.9 %collective-permute-start.18 = (f32[2,40,512]{2,1,0:T(8,128)}, f32[2,40,512]{2,1,0:T(8,128)}, u32[]{:S(2)}, u32[]{:S(2)}) collective-permute-start(f32[2,40,512]{2,1,0:T(8,128)} %slice_bitcast_fusion.11), channel_id=1, source_target_pairs={{16,0},{32,16},{48,32},{64,48},{80,64},{96,80},{112,96},{17,1},{33... | collective-permute-start | bytes 491528 | tf_op jit(solution)/shard_map/ppermute | solution.py:37
  210.4 12.8 %all-to-all-start.7 = ((f32[16,2,4,128]{3,1,2,0:T(2,128)}), f32[16,2,4,128]{3,1,2,0:T(2,128)S(1)}, u32[]{:S(2)}, u32[]{:S(2)}) async-start(f32[16,2,4,128]{3,1,2,0:T(2,128)} %bitcast.490), calls=%async_computation.7 | async-start | bytes 131072 | tf_op jit(solution)/shard_map/all_to_all | solution.py:26
  216.1 28.7 %collective-permute-start.16 = (f32[2,160,1]{2,1,0:T(8,128)}, f32[2,160,1]{2,1,0:T(8,128)}, u32[]{:S(2)}, u32[]{:S(2)}) collective-permute-start(f32[2,160,1]{2,1,0:T(8,128)} %get-tuple-element.68), channel_id=1, source_target_pairs={{0,1},{1,2},{2,3},{3,4},{4,5},{5,6},{6,7},{7,8},{8,9},{9,10},{10,1... | collective-permute-start | bytes 3848 | tf_op jit(solution)/shard_map/ppermute | solution.py:70
  219.5 25.3 %collective-permute-start.17 = (f32[2,160,1]{2,1,0:T(8,128)}, f32[2,160,1]{2,1,0:T(8,128)}, u32[]{:S(2)}, u32[]{:S(2)}) collective-permute-start(f32[2,160,1]{2,1,0:T(8,128)} %get-tuple-element.69), channel_id=1, source_target_pairs={{1,0},{2,1},{3,2},{4,3},{5,4},{6,5},{7,6},{8,7},{9,8},{10,9},{11,1... | collective-permute-start | bytes 3848 | tf_op jit(solution)/shard_map/ppermute | solution.py:72
  223.9 13.2 %all-to-all-start.6 = ((f32[16,2,5,128]{3,1,2,0:T(2,128)}), f32[16,2,5,128]{3,1,2,0:T(2,128)S(1)}, u32[]{:S(2)}, u32[]{:S(2)}) async-start(f32[16,2,5,128]{3,1,2,0:T(2,128)} %broadcast_in_dim.169), calls=%async_computation.6 | async-start | bytes 163840 | tf_op jit(solution)/shard_map/all_to_all | solution.py:48
  231.3 36.7 %collective-permute-start.15 = (f32[2,128]{1,0:T(2,128)S(1)}, f32[2,128]{1,0:T(2,128)S(1)}, u32[]{:S(2)}, u32[]{:S(2)}) collective-permute-start(f32[2,128]{1,0:T(2,128)S(1)} %slice_bitcast_fusion.24), channel_id=1, source_target_pairs={{0,16},{16,32},{32,48},{48,64},{64,80},{80,96},{96,112},{1,17},{17... | collective-permute-start | bytes 3080 | tf_op jit(solution)/shard_map/ppermute | solution.py:37
  274.7 20.6 %collective-permute-start.20 = (f32[2,128]{1,0:T(2,128)S(1)}, f32[2,128]{1,0:T(2,128)S(1)}, u32[]{:S(2)}, u32[]{:S(2)}) collective-permute-start(f32[2,128]{1,0:T(2,128)S(1)} %slice_bitcast_fusion.23), channel_id=1, source_target_pairs={{16,0},{32,16},{48,32},{64,48},{80,64},{96,80},{112,96},{17,1},{33... | collective-permute-start | bytes 3080 | tf_op jit(solution)/shard_map/ppermute | solution.py:37
  277.4 38.8 %collective-permute-start.25 = (f32[2,40,512]{2,1,0:T(8,128)}, f32[2,40,512]{2,1,0:T(8,128)}, u32[]{:S(2)}, u32[]{:S(2)}) collective-permute-start(f32[2,40,512]{2,1,0:T(8,128)} %slice_bitcast_fusion.8), channel_id=1, source_target_pairs={{0,16},{16,32},{32,48},{48,64},{64,80},{80,96},{96,112},{1,17},{17... | collective-permute-start | bytes 491528 | tf_op jit(solution)/shard_map/ppermute | solution.py:37
  279.8 36.4 %collective-permute-start.24 = (f32[2,40,512]{2,1,0:T(8,128)}, f32[2,40,512]{2,1,0:T(8,128)}, u32[]{:S(2)}, u32[]{:S(2)}) collective-permute-start(f32[2,40,512]{2,1,0:T(8,128)} %slice_bitcast_fusion.9), channel_id=1, source_target_pairs={{16,0},{32,16},{48,32},{64,48},{80,64},{96,80},{112,96},{17,1},{33... | collective-permute-start | bytes 491528 | tf_op jit(solution)/shard_map/ppermute | solution.py:37
  283.6 12.8 %all-to-all-start.9 = ((f32[16,2,4,128]{3,1,2,0:T(2,128)}), f32[16,2,4,128]{3,1,2,0:T(2,128)S(1)}, u32[]{:S(2)}, u32[]{:S(2)}) async-start(f32[16,2,4,128]{3,1,2,0:T(2,128)} %bitcast.530), calls=%async_computation.9 | async-start | bytes 131072 | tf_op jit(solution)/shard_map/all_to_all | solution.py:26
  289.4 29.3 %collective-permute-start.22 = (f32[2,160,1]{2,1,0:T(8,128)}, f32[2,160,1]{2,1,0:T(8,128)}, u32[]{:S(2)}, u32[]{:S(2)}) collective-permute-start(f32[2,160,1]{2,1,0:T(8,128)} %get-tuple-element.63), channel_id=1, source_target_pairs={{0,1},{1,2},{2,3},{3,4},{4,5},{5,6},{6,7},{7,8},{8,9},{9,10},{10,1... | collective-permute-start | bytes 3848 | tf_op jit(solution)/shard_map/ppermute | solution.py:70
  292.7 25.9 %collective-permute-start.23 = (f32[2,160,1]{2,1,0:T(8,128)}, f32[2,160,1]{2,1,0:T(8,128)}, u32[]{:S(2)}, u32[]{:S(2)}) collective-permute-start(f32[2,160,1]{2,1,0:T(8,128)} %get-tuple-element.64), channel_id=1, source_target_pairs={{1,0},{2,1},{3,2},{4,3},{5,4},{6,5},{7,6},{8,7},{9,8},{10,9},{11,1... | collective-permute-start | bytes 3848 | tf_op jit(solution)/shard_map/ppermute | solution.py:72
  297.1 13.2 %all-to-all-start.8 = ((f32[16,2,5,128]{3,1,2,0:T(2,128)}), f32[16,2,5,128]{3,1,2,0:T(2,128)S(1)}, u32[]{:S(2)}, u32[]{:S(2)}) async-start(f32[16,2,5,128]{3,1,2,0:T(2,128)} %broadcast_in_dim.174), calls=%async_computation.8 | async-start | bytes 163840 | tf_op jit(solution)/shard_map/all_to_all | solution.py:48
  307.2 33.3 %collective-permute-start.21 = (f32[2,128]{1,0:T(2,128)}, f32[2,128]{1,0:T(2,128)}, u32[]{:S(2)}, u32[]{:S(2)}) collective-permute-start(f32[2,128]{1,0:T(2,128)} %slice_bitcast_fusion.22), channel_id=1, source_target_pairs={{0,16},{16,32},{32,48},{48,64},{64,80},{80,96},{96,112},{1,17},{17... | collective-permute-start | bytes 3080 | tf_op jit(solution)/shard_map/ppermute | solution.py:37
  347.7 23.0 %collective-permute-start.26 = (f32[2,128]{1,0:T(2,128)S(1)}, f32[2,128]{1,0:T(2,128)S(1)}, u32[]{:S(2)}, u32[]{:S(2)}) collective-permute-start(f32[2,128]{1,0:T(2,128)S(1)} %slice_bitcast_fusion.21), channel_id=1, source_target_pairs={{16,0},{32,16},{48,32},{64,48},{80,64},{96,80},{112,96},{17,1},{33... | collective-permute-start | bytes 3080 | tf_op jit(solution)/shard_map/ppermute | solution.py:37
  351.9 40.1 %collective-permute-start.30 = (f32[2,40,512]{2,1,0:T(8,128)}, f32[2,40,512]{2,1,0:T(8,128)}, u32[]{:S(2)}, u32[]{:S(2)}) collective-permute-start(f32[2,40,512]{2,1,0:T(8,128)} %slice_bitcast_fusion.7), channel_id=1, source_target_pairs={{16,0},{32,16},{48,32},{64,48},{80,64},{96,80},{112,96},{17,1},{33... | collective-permute-start | bytes 491528 | tf_op jit(solution)/shard_map/ppermute | solution.py:37
  354.7 17.3 %all-to-all-start.11 = ((f32[16,2,4,128]{3,1,2,0:T(2,128)}), f32[16,2,4,128]{3,1,2,0:T(2,128)S(1)}, u32[]{:S(2)}, u32[]{:S(2)}) async-start(f32[16,2,4,128]{3,1,2,0:T(2,128)} %bitcast.527), calls=%async_computation.11 | async-start | bytes 131072 | tf_op jit(solution)/shard_map/all_to_all | solution.py:26
  361.0 33.5 %collective-permute-start.28 = (f32[2,160,1]{2,1,0:T(8,128)}, f32[2,160,1]{2,1,0:T(8,128)}, u32[]{:S(2)}, u32[]{:S(2)}) collective-permute-start(f32[2,160,1]{2,1,0:T(8,128)} %get-tuple-element.58), channel_id=1, source_target_pairs={{0,1},{1,2},{2,3},{3,4},{4,5},{5,6},{6,7},{7,8},{8,9},{9,10},{10,1... | collective-permute-start | bytes 3848 | tf_op jit(solution)/shard_map/ppermute | solution.py:70
  364.4 30.1 %collective-permute-start.29 = (f32[2,160,1]{2,1,0:T(8,128)}, f32[2,160,1]{2,1,0:T(8,128)}, u32[]{:S(2)}, u32[]{:S(2)}) collective-permute-start(f32[2,160,1]{2,1,0:T(8,128)} %get-tuple-element.59), channel_id=1, source_target_pairs={{1,0},{2,1},{3,2},{4,3},{5,4},{6,5},{7,6},{8,7},{9,8},{10,9},{11,1... | collective-permute-start | bytes 3848 | tf_op jit(solution)/shard_map/ppermute | solution.py:72
  368.7 23.3 %collective-permute-start.31 = (f32[2,40,512]{2,1,0:T(8,128)}, f32[2,40,512]{2,1,0:T(8,128)}, u32[]{:S(2)}, u32[]{:S(2)}) collective-permute-start(f32[2,40,512]{2,1,0:T(8,128)} %slice_bitcast_fusion.6), channel_id=1, source_target_pairs={{0,16},{16,32},{32,48},{48,64},{64,80},{80,96},{96,112},{1,17},{17... | collective-permute-start | bytes 491528 | tf_op jit(solution)/shard_map/ppermute | solution.py:37
  372.6 13.5 %all-to-all-start.10 = ((f32[16,2,5,128]{3,1,2,0:T(2,128)}), f32[16,2,5,128]{3,1,2,0:T(2,128)S(1)}, u32[]{:S(2)}, u32[]{:S(2)}) async-start(f32[16,2,5,128]{3,1,2,0:T(2,128)} %broadcast_in_dim.179), calls=%async_computation.10 | async-start | bytes 163840 | tf_op jit(solution)/shard_map/all_to_all | solution.py:48
  382.7 36.6 %collective-permute-start.27 = (f32[2,128]{1,0:T(2,128)}, f32[2,128]{1,0:T(2,128)}, u32[]{:S(2)}, u32[]{:S(2)}) collective-permute-start(f32[2,128]{1,0:T(2,128)} %slice_bitcast_fusion.20), channel_id=1, source_target_pairs={{0,16},{16,32},{32,48},{48,64},{64,80},{80,96},{96,112},{1,17},{17... | collective-permute-start | bytes 3080 | tf_op jit(solution)/shard_map/ppermute | solution.py:37
  426.6 21.6 %collective-permute-start.32 = (f32[2,128]{1,0:T(2,128)S(1)}, f32[2,128]{1,0:T(2,128)S(1)}, u32[]{:S(2)}, u32[]{:S(2)}) collective-permute-start(f32[2,128]{1,0:T(2,128)S(1)} %slice_bitcast_fusion.19), channel_id=1, source_target_pairs={{16,0},{32,16},{48,32},{64,48},{80,64},{96,80},{112,96},{17,1},{33... | collective-permute-start | bytes 3080 | tf_op jit(solution)/shard_map/ppermute | solution.py:37
  429.4 40.0 %collective-permute-start.37 = (f32[2,40,512]{2,1,0:T(8,128)}, f32[2,40,512]{2,1,0:T(8,128)}, u32[]{:S(2)}, u32[]{:S(2)}) collective-permute-start(f32[2,40,512]{2,1,0:T(8,128)} %slice_bitcast_fusion.4), channel_id=1, source_target_pairs={{0,16},{16,32},{32,48},{48,64},{64,80},{80,96},{96,112},{1,17},{17... | collective-permute-start | bytes 491528 | tf_op jit(solution)/shard_map/ppermute | solution.py:37
  431.8 37.6 %collective-permute-start.36 = (f32[2,40,512]{2,1,0:T(8,128)}, f32[2,40,512]{2,1,0:T(8,128)}, u32[]{:S(2)}, u32[]{:S(2)}) collective-permute-start(f32[2,40,512]{2,1,0:T(8,128)} %slice_bitcast_fusion.5), channel_id=1, source_target_pairs={{16,0},{32,16},{48,32},{64,48},{80,64},{96,80},{112,96},{17,1},{33... | collective-permute-start | bytes 491528 | tf_op jit(solution)/shard_map/ppermute | solution.py:37
  435.6 13.9 %all-to-all-start.13 = ((f32[16,2,4,128]{3,1,2,0:T(2,128)}), f32[16,2,4,128]{3,1,2,0:T(2,128)S(1)}, u32[]{:S(2)}, u32[]{:S(2)}) async-start(f32[16,2,4,128]{3,1,2,0:T(2,128)} %bitcast.528), calls=%async_computation.13 | async-start | bytes 131072 | tf_op jit(solution)/shard_map/all_to_all | solution.py:26
  442.4 29.4 %collective-permute-start.34 = (f32[2,160,1]{2,1,0:T(8,128)}, f32[2,160,1]{2,1,0:T(8,128)}, u32[]{:S(2)}, u32[]{:S(2)}) collective-permute-start(f32[2,160,1]{2,1,0:T(8,128)} %get-tuple-element.53), channel_id=1, source_target_pairs={{0,1},{1,2},{2,3},{3,4},{4,5},{5,6},{6,7},{7,8},{8,9},{9,10},{10,1... | collective-permute-start | bytes 3848 | tf_op jit(solution)/shard_map/ppermute | solution.py:70
  445.7 26.0 %collective-permute-start.35 = (f32[2,160,1]{2,1,0:T(8,128)}, f32[2,160,1]{2,1,0:T(8,128)}, u32[]{:S(2)}, u32[]{:S(2)}) collective-permute-start(f32[2,160,1]{2,1,0:T(8,128)} %get-tuple-element.54), channel_id=1, source_target_pairs={{1,0},{2,1},{3,2},{4,3},{5,4},{6,5},{7,6},{8,7},{9,8},{10,9},{11,1... | collective-permute-start | bytes 3848 | tf_op jit(solution)/shard_map/ppermute | solution.py:72
  450.1 13.2 %all-to-all-start.12 = ((f32[16,2,5,128]{3,1,2,0:T(2,128)}), f32[16,2,5,128]{3,1,2,0:T(2,128)S(1)}, u32[]{:S(2)}, u32[]{:S(2)}) async-start(f32[16,2,5,128]{3,1,2,0:T(2,128)} %broadcast_in_dim.184), calls=%async_computation.12 | async-start | bytes 163840 | tf_op jit(solution)/shard_map/all_to_all | solution.py:48
  460.2 35.0 %collective-permute-start.33 = (f32[2,128]{1,0:T(2,128)}, f32[2,128]{1,0:T(2,128)}, u32[]{:S(2)}, u32[]{:S(2)}) collective-permute-start(f32[2,128]{1,0:T(2,128)} %slice_bitcast_fusion.18), channel_id=1, source_target_pairs={{0,16},{16,32},{32,48},{48,64},{64,80},{80,96},{96,112},{1,17},{17... | collective-permute-start | bytes 3080 | tf_op jit(solution)/shard_map/ppermute | solution.py:37
  502.5 21.0 %collective-permute-start.38 = (f32[2,128]{1,0:T(2,128)S(1)}, f32[2,128]{1,0:T(2,128)S(1)}, u32[]{:S(2)}, u32[]{:S(2)}) collective-permute-start(f32[2,128]{1,0:T(2,128)S(1)} %slice_bitcast_fusion.17), channel_id=1, source_target_pairs={{16,0},{32,16},{48,32},{64,48},{80,64},{96,80},{112,96},{17,1},{33... | collective-permute-start | bytes 3080 | tf_op jit(solution)/shard_map/ppermute | solution.py:37
  505.2 39.4 %collective-permute-start.43 = (f32[2,40,512]{2,1,0:T(8,128)}, f32[2,40,512]{2,1,0:T(8,128)}, u32[]{:S(2)}, u32[]{:S(2)}) collective-permute-start(f32[2,40,512]{2,1,0:T(8,128)} %slice_bitcast_fusion.2), channel_id=1, source_target_pairs={{0,16},{16,32},{32,48},{48,64},{64,80},{80,96},{96,112},{1,17},{17... | collective-permute-start | bytes 491528 | tf_op jit(solution)/shard_map/ppermute | solution.py:37
  507.6 37.0 %collective-permute-start.42 = (f32[2,40,512]{2,1,0:T(8,128)}, f32[2,40,512]{2,1,0:T(8,128)}, u32[]{:S(2)}, u32[]{:S(2)}) collective-permute-start(f32[2,40,512]{2,1,0:T(8,128)} %slice_bitcast_fusion.3), channel_id=1, source_target_pairs={{16,0},{32,16},{48,32},{64,48},{80,64},{96,80},{112,96},{17,1},{33... | collective-permute-start | bytes 491528 | tf_op jit(solution)/shard_map/ppermute | solution.py:37
  511.5 13.3 %all-to-all-start.15 = ((f32[16,2,4,128]{3,1,2,0:T(2,128)}), f32[16,2,4,128]{3,1,2,0:T(2,128)S(1)}, u32[]{:S(2)}, u32[]{:S(2)}) async-start(f32[16,2,4,128]{3,1,2,0:T(2,128)} %bitcast.529), calls=%async_computation.15 | async-start | bytes 131072 | tf_op jit(solution)/shard_map/all_to_all | solution.py:26
  517.7 29.4 %collective-permute-start.40 = (f32[2,160,1]{2,1,0:T(8,128)}, f32[2,160,1]{2,1,0:T(8,128)}, u32[]{:S(2)}, u32[]{:S(2)}) collective-permute-start(f32[2,160,1]{2,1,0:T(8,128)} %get-tuple-element.48), channel_id=1, source_target_pairs={{0,1},{1,2},{2,3},{3,4},{4,5},{5,6},{6,7},{7,8},{8,9},{9,10},{10,1... | collective-permute-start | bytes 3848 | tf_op jit(solution)/shard_map/ppermute | solution.py:70
  521.0 26.1 %collective-permute-start.41 = (f32[2,160,1]{2,1,0:T(8,128)}, f32[2,160,1]{2,1,0:T(8,128)}, u32[]{:S(2)}, u32[]{:S(2)}) collective-permute-start(f32[2,160,1]{2,1,0:T(8,128)} %get-tuple-element.49), channel_id=1, source_target_pairs={{1,0},{2,1},{3,2},{4,3},{5,4},{6,5},{7,6},{8,7},{9,8},{10,9},{11,1... | collective-permute-start | bytes 3848 | tf_op jit(solution)/shard_map/ppermute | solution.py:72
  525.4 13.2 %all-to-all-start.14 = ((f32[16,2,5,128]{3,1,2,0:T(2,128)}), f32[16,2,5,128]{3,1,2,0:T(2,128)S(1)}, u32[]{:S(2)}, u32[]{:S(2)}) async-start(f32[16,2,5,128]{3,1,2,0:T(2,128)} %broadcast_in_dim.189), calls=%async_computation.14 | async-start | bytes 163840 | tf_op jit(solution)/shard_map/all_to_all | solution.py:48
  535.5 41.4 %collective-permute-start.39 = (f32[2,128]{1,0:T(2,128)}, f32[2,128]{1,0:T(2,128)}, u32[]{:S(2)}, u32[]{:S(2)}) collective-permute-start(f32[2,128]{1,0:T(2,128)} %slice_bitcast_fusion.16), channel_id=1, source_target_pairs={{0,16},{16,32},{32,48},{48,64},{64,80},{80,96},{96,112},{1,17},{17... | collective-permute-start | bytes 3080 | tf_op jit(solution)/shard_map/ppermute | solution.py:37
  552.8 33.2 %collective-permute-start.47 = (f32[2,40,512]{2,1,0:T(8,128)}, f32[2,40,512]{2,1,0:T(8,128)}, u32[]{:S(2)}, u32[]{:S(2)}) collective-permute-start(f32[2,40,512]{2,1,0:T(8,128)} %slice_bitcast_fusion), channel_id=1, source_target_pairs={{0,16},{16,32},{32,48},{48,64},{64,80},{80,96},{96,112},{1,17},{17... | collective-permute-start | bytes 491528 | tf_op jit(solution)/shard_map/ppermute | solution.py:37
  554.7 31.2 %collective-permute-start.46 = (f32[2,40,512]{2,1,0:T(8,128)}, f32[2,40,512]{2,1,0:T(8,128)}, u32[]{:S(2)}, u32[]{:S(2)}) collective-permute-start(f32[2,40,512]{2,1,0:T(8,128)} %slice_bitcast_fusion.1), channel_id=1, source_target_pairs={{16,0},{32,16},{48,32},{64,48},{80,64},{96,80},{112,96},{17,1},{33... | collective-permute-start | bytes 491528 | tf_op jit(solution)/shard_map/ppermute | solution.py:37
  579.3 9.4 %collective-permute-start.44 = (f32[2,160,1]{2,1,0:T(8,128)}, f32[2,160,1]{2,1,0:T(8,128)S(1)}, u32[]{:S(2)}, u32[]{:S(2)}) collective-permute-start(f32[2,160,1]{2,1,0:T(8,128)} %get-tuple-element.42), channel_id=1, source_target_pairs={{0,1},{1,2},{2,3},{3,4},{4,5},{5,6},{6,7},{7,8},{8,9},{9,10},{10,1... | collective-permute-start | bytes 3848 | tf_op jit(solution)/shard_map/ppermute | solution.py:70
  584.0 9.5 %collective-permute-start.45 = (f32[2,160,1]{2,1,0:T(8,128)}, f32[2,160,1]{2,1,0:T(8,128)S(1)}, u32[]{:S(2)}, u32[]{:S(2)}) collective-permute-start(f32[2,160,1]{2,1,0:T(8,128)} %get-tuple-element.44), channel_id=1, source_target_pairs={{1,0},{2,1},{3,2},{4,3},{5,4},{6,5},{7,6},{8,7},{9,8},{10,9},{11,1... | collective-permute-start | bytes 3848 | tf_op jit(solution)/shard_map/ppermute | solution.py:72
  (113 other events, 2677.7 us)
where the time goes:
time: 608 us; the launch traced here: 598 us
  starting transfers between devices  226 us (37%)
  blocking collectives  147 us (24%)
  matrix products  118 us (19%)
  local copies, waits for them, and re-layouts  38.2 us (6%)
  other arithmetic  35.6 us (6%)
  waiting for transfers between devices  29.2 us (5%)
    psum x14, blocking collectives, one_axis_at_a_time(): return functools.reduce(lax.psum, axes, shard)  129 us
    ppermute x32, starting transfers between devices, from_behind(): return lax.ppermute(block, axis, route)  74.6 us
    all_to_all x8, starting transfers between devices, from_everyone(): return lax.all_to_all(copies, axis, split_axis=0, concat_axis=0, tiled=True)  54.6 us
    all_to_all x8, starting transfers between devices, sum_at_owner(): lax.all_to_all(tiles, axis, split_axis=0, concat_axis=0, tiled=True)  49.1 us
    dot_general x8, matrix products, local(): jnp.einsum('lij,plj->pli', dipole, gathered[:, 1:], precision=highest)  45 us
    dot_general x8, matrix products, local(): jnp.einsum('lji,plj->pli', dipole, inner_part, precision=highest)  31.9 us
    ppermute x8, starting transfers between devices, with_halo(): lax.ppermute(tail, axis, [(i, (i + 1) % count) for i in range(ends)])  28.3 us
    ppermute x8, starting transfers between devices, with_halo(): lax.ppermute(head, axis, [((i + 1) % count, i) for i in range(ends)])  19.2 us
  transfers between devices with their start and end apart: 64, of which 9 were waited for; matrix products, arithmetic and copies ran while one was open for 24% of the time, Pallas kernels for 0%

commit v1 on v0

v1 whole, which is shorter than its diff:
```python
import functools

import jax
import jax.numpy as jnp
from jax import lax
from jax.experimental import pallas as pl
from jax.experimental.pallas import tpu as pltpu
from jax.sharding import PartitionSpec as P

STEPS = 2
ORDER = 4
kinetic_scale = 3.125
time_step = 0.1

F32 = jnp.float32
BF16 = jnp.bfloat16
HIGHEST = lax.Precision.HIGHEST
VM = pl.BlockSpec(memory_space=pltpu.VMEM)
SM = pl.BlockSpec(memory_space=pltpu.SMEM)

LB = 4
CH = 40
OWN = LB * CH
PTS = 16
HALO = 8
WIDTH = 640
EDGE = 64 + OWN
NT = (((1,), (1,)), ((), ()))


def sds(*shape):
    return jax.ShapeDtypeStruct(shape, F32)


def call(kernel, outs, smem=1, scratch=(), limit=48):
    def run(*args):
        return pl.pallas_call(
            kernel,
            out_shape=outs,
            in_specs=[SM] * smem + [VM] * (len(args) - smem),
            out_specs=[VM] * len(outs),
            scratch_shapes=list(scratch),
            compiler_params=pltpu.CompilerParams(vmem_limit_bytes=limit << 20),
        )(*args)

    return run


def rows_of(lines, shape):
    return lax.broadcasted_iota(jnp.int32, shape, lines)


def block_mask():
    lanes = rows_of(1, (8, 256))
    first = (rows_of(0, (8, 256)) % LB) * CH
    return jnp.where((lanes >= first) & (lanes < first + CH), 1.0, 0.0).astype(F32)


def edge_tiles(strip):
    lanes = rows_of(1, (2 * PTS, 128))
    up = pltpu.roll(strip, 80, 1)[:, 128:]
    down = pltpu.roll(strip, 160, 1)[:, 128:]
    zero = jnp.zeros_like(up)
    up = jnp.where((lanes >= 72) & (lanes < 112), up, zero)
    down = jnp.where((lanes >= 32) & (lanes < 72), down, zero)
    return up, down


def emit(parity, c, strip, dipole, surface, q_ref, a_ref, b_ref, up_ref, down_ref):
    for s in range(16):
        q_ref[s, 0:8, :] = jnp.zeros((8, 128), F32)
    ahead = jnp.concatenate([c[1:4], c[0:1], c[5:8], c[4:5]], axis=0)
    partial = lax.dot_general(c, surface[...], NT, precision=HIGHEST, preferred_element_type=F32)
    partial = partial * block_mask()
    b_re = jnp.sum(partial[0:4], axis=0, keepdims=True)
    b_im = jnp.sum(partial[4:8], axis=0, keepdims=True)
    tail = jnp.concatenate(
        [b_re[:, :128], b_re[:, 128:], b_im[:, :128], b_im[:, 128:], jnp.zeros((4, 128), F32)], axis=0
    )
    for s in range(16):
        q_ref[s, 0:8, :] = ahead
        q_ref[s, 8:16, :] = jnp.zeros((8, 128), F32)
        q_ref[s, 16:24, :] = tail
    for l in range(LB):
        re = jnp.broadcast_to(c[l : l + 1], (128, 128)).T
        im = jnp.broadcast_to(c[4 + l : 5 + l], (128, 128)).T

        def body(s, carry):
            tile = dipole[l, :, pl.ds(pl.multiple_of(s * 128, 128), 128)]
            sum_re = jnp.sum(tile * re, axis=0, keepdims=True)
            sum_im = jnp.sum(tile * im, axis=0, keepdims=True)
            if l < LB - 1:
                q_ref[s, 9 + l : 10 + l, :] = sum_re
                q_ref[s, 13 + l : 14 + l, :] = sum_im
            else:
                up_ref[pl.ds(s, 1), :] = sum_re
                up_ref[pl.ds(16 + s, 1), :] = sum_im
            return carry

        lax.fori_loop(0, 16, body, 0, unroll=4)
    up, down = edge_tiles(strip)
    up_ref[32:64, :] = up
    down_ref[0:8, :] = c
    down_ref[8:32, :] = jnp.zeros((24, 128), F32)
    down_ref[32:64, :] = down

    @pl.when(parity == 0)
    def _():
        a_ref[0:64, :] = up_ref[...]
        b_ref[0:64, :] = down_ref[...]

    @pl.when(parity != 0)
    def _():
        a_ref[0:64, :] = down_ref[...]
        b_ref[0:64, :] = up_ref[...]


def first_kernel(where, inner, live, strip, dipole, surface, pack, c_ref, q_ref, a_ref, b_ref, up_ref, down_ref):
    c = inner[...] * live[...]
    c_ref[...] = c
    a_ref[64:EDGE, :] = pack[...]
    b_ref[64:EDGE, :] = pack[...]
    emit(where[0], c, strip[...], dipole, surface, q_ref, a_ref, b_ref, up_ref, down_ref)


def received(parity, a, b):
    flag = jnp.full(a.shape, parity, jnp.int32) == 0
    return jnp.where(flag, b, a), jnp.where(flag, a, b)


def assemble_kernel(first, where, *refs):
    if first:
        q, a, b, strip, out_ref, low_ref, high_ref = refs
    else:
        q, a, b, out_ref, ghost_ref = refs
    up, down = received(where[0], a[...], b[...])
    out_ref[:, 0:24, :] = q[...]
    for s in range(16):
        out_ref[s, 3:4, :] = down[0:1]
        out_ref[s, 7:8, :] = down[4:5]
        out_ref[s, 8:9, :] = up[s : s + 1]
        out_ref[s, 12:13, :] = up[16 + s : 17 + s]
    ghost = up[32:64] + down[32:64]
    if first:
        whole = strip[...]
        near, far = whole[:, :128], whole[:, 128:] + ghost
        for s in range(16):
            out_ref[s, 24:56, :] = near
            out_ref[s, 56:88, :] = far
        low_ref[...] = up[64:EDGE]
        high_ref[...] = down[64:EDGE]
    else:
        ghost_ref[...] = ghost


def advance(first, last_power, factor, field, dipole, surface, levels, pairs, thresholds, arrived, cs, fs, ghost):
    sums = []
    for l in range(LB):

        def body(s, carry):
            tile = dipole[l, :, pl.ds(pl.multiple_of(s * 128, 128), 128)]
            return (
                carry[0] + tile * arrived[s, l : l + 1, :],
                carry[1] + tile * arrived[s, 4 + l : 5 + l, :],
            )

        zero = jnp.zeros((128, 128), F32)
        re, im = lax.fori_loop(0, 16, body, (zero, zero), unroll=4)
        sums.append((jnp.sum(re.T, axis=0, keepdims=True), jnp.sum(im.T, axis=0, keepdims=True)))
    forward = jnp.concatenate([a for a, _ in sums] + [b for _, b in sums], axis=0)
    backward = arrived[0, 8:16, :]
    tail = arrived[0, 16:24, :]
    for s in range(1, 16):
        backward = backward + arrived[s, 8:16, :]
        tail = tail + arrived[s, 16:24, :]
    lanes = rows_of(1, (2 * PTS, 256))
    if first:
        whole = jnp.concatenate([arrived[0, 24:56, :], arrived[0, 56:88, :]], axis=1)
        own = jnp.where(lanes < OWN, whole, 0.0)
        strip_sum = own
    else:
        own = fs[0:32, :]
        strip_sum = fs[32:64, :]
        whole = jnp.concatenate([own[:, :128], own[:, 128:] + ghost[...]], axis=1)
    c = cs[0:8, :]
    c_sum = c if first else cs[8:16, :]
    edge = jnp.concatenate(
        [jnp.broadcast_to(own[0:1], (4, 256)), jnp.broadcast_to(own[PTS : PTS + 1], (4, 256))], axis=0
    )
    surf = jnp.dot(edge * block_mask(), surface[...], precision=HIGHEST, preferred_element_type=F32)
    image = levels[8:16, :] * (levels[0:8, :] * c + field * (forward + backward) - kinetic_scale * surf)
    c_new = jnp.concatenate([factor * image[4:8], -factor * image[0:4]], axis=0)
    coupled = lax.dot_general(whole, pairs[...], NT, precision=HIGHEST, preferred_element_type=F32)
    b_re = jnp.concatenate([tail[0:1], tail[1:2]], axis=1)
    b_im = jnp.concatenate([tail[2:3], tail[3:4]], axis=1)
    points = rows_of(0, (2 * PTS, 256))
    left = pltpu.roll(own, 1, 0)
    left = jnp.where(points == 0, b_re, jnp.where(points == PTS, b_im, left))
    right = pltpu.roll(own, 2 * PTS - 1, 0)
    right = jnp.where((points == PTS - 1) | (points == 2 * PTS - 1), 0.0, right)
    grid = kinetic_scale * (2.0 * own - left - right) + thresholds[...] * own + field * coupled
    grid = jnp.where(lanes < OWN, grid, 0.0)
    f_new = jnp.concatenate([factor * grid[PTS:], -factor * grid[:PTS]], axis=0)
    c_sum = c_sum + c_new
    strip_sum = strip_sum + f_new
    if last_power:
        return c_sum, c_sum, strip_sum, strip_sum
    return c_new, c_sum, f_new, strip_sum


def middle_kernel(first, last_power, factor, step, where, strengths, *refs):
    dipole, surface, levels, pairs, thresholds, arrived, cs = refs[:7]
    rest = refs[7:]
    fs = ghost = None
    if not first:
        fs, ghost = rest[:2]
        rest = rest[2:]
    cs_ref, fs_ref, q_ref, a_ref, b_ref, up_ref, down_ref = rest
    c, c_sum, f, f_sum = advance(
        first, last_power, factor, strengths[step], dipole, surface, levels, pairs, thresholds, arrived, cs, fs, ghost
    )
    cs_ref[0:8, :] = c
    cs_ref[8:16, :] = c_sum
    fs_ref[0:32, :] = f
    fs_ref[32:64, :] = f_sum
    emit(where[0], c, f, dipole, surface, q_ref, a_ref, b_ref, up_ref, down_ref)


def last_kernel(
    factor, step, where, strengths, dipole, surface, levels, pairs, thresholds, arrived, cs, fs, ghost, bulk, c_ref, out_ref
):
    _, c_sum, _, f_sum = advance(
        False, True, factor, strengths[step], dipole, surface, levels, pairs, thresholds, arrived, cs, fs, ghost
    )
    c_ref[...] = c_sum
    lanes = rows_of(1, (OWN, 128))
    low = jnp.full((OWN, 128), where[1], jnp.int32) == 0
    fixed = (lanes < HALO) & low
    for part in range(2):
        corner = f_sum[part * PTS : (part + 1) * PTS]
        corner = jnp.concatenate([corner, jnp.zeros((128 - PTS, 256), F32)], axis=0).T[:OWN]
        base = part * WIDTH
        out_ref[part, :, 0:128] = jnp.where(fixed, corner, bulk[:, base : base + 128])
        out_ref[part, :, 128:512] = bulk[:, base + 128 : base + 512]


def window_kernel(outer, left, right, out_ref):
    lanes = rows_of(1, (OWN, 128))
    for part in range(2):
        base = part * WIDTH
        out_ref[:, base : base + 512] = outer[part]
        out_ref[:, base + 512 : base + WIDTH] = jnp.where(
            lanes < HALO, right[part], jnp.where(lanes >= 128 - HALO, left[part], 0.0)
        )


GROUPS = ((160, 320, 120, 360), (40, 160, 0, 200), (320, 440, 280, 480))


def bulk_kernel(step, powers, begin, where, strengths, *refs):
    if begin:
        low, own, high, couplings, pack, win_ref, sum_ref, old_ref = refs
        old_ref[0:160, :] = low[...]
        old_ref[160:320, :] = own[...]
        old_ref[320:480, :] = high[...]
        sum_ref[...] = own[...]
    else:
        given, given_sum, couplings, pack, sum_ref, old_ref, win_ref = refs
        old_ref[...] = given[...]
        sum_ref[...] = given_sum[...]
    field = strengths[step]
    lanes = rows_of(1, (1, WIDTH))
    past = (lanes >= 512) & (lanes < 512 + 64) & (jnp.full((1, WIDTH), where[1], jnp.int32) == 15)
    keep = jnp.where(past, 0.0, 1.0).astype(F32)
    source, target = old_ref, win_ref
    for power in powers:
        factor = time_step / power
        for out0, out1, in0, in1 in GROUPS if power < ORDER else GROUPS[:1]:
            matrix = couplings[out0:out1, in0:in1]
            m_hi = matrix.astype(BF16)
            m_lo = (matrix - m_hi.astype(F32)).astype(BF16)
            images = []
            for part in range(2):
                cols = slice(part * WIDTH, (part + 1) * WIDTH)
                f = source[in0:in1, cols]
                f_hi = f.astype(BF16)
                f_lo = (f - f_hi.astype(F32)).astype(BF16)
                coupled = jnp.dot(m_hi, f_hi, preferred_element_type=F32)
                coupled = coupled + jnp.dot(m_hi, f_lo, preferred_element_type=F32)
                coupled = coupled + jnp.dot(m_lo, f_hi, preferred_element_type=F32)
                own = source[out0:out1, cols]
                left = pltpu.roll(own, 1, 1)
                right = pltpu.roll(own, WIDTH - 1, 1)
                level = pack[out0:out1, CH : CH + 1]
                image = kinetic_scale * (2.0 * own - left - right) + level * own + field * coupled
                images.append(image * keep)
            new_re = factor * images[1]
            new_im = -factor * images[0]
            target[out0:out1, 0:WIDTH] = new_re
            target[out0:out1, WIDTH : 2 * WIDTH] = new_im
            if out0 == 160:
                sum_ref[:, 0:WIDTH] = sum_ref[:, 0:WIDTH] + new_re
                sum_ref[:, WIDTH : 2 * WIDTH] = sum_ref[:, WIDTH : 2 * WIDTH] + new_im
        if power == powers[0]:
            target[0:40, :] = source[0:40, :]
            target[440:480, :] = source[440:480, :]
        source, target = target, source
    if begin and source is not win_ref:
        win_ref[...] = old_ref[...]


def pair_up(lower, upper):
    return [(a, b) for a, b in zip(lower, upper)] + [(b, a) for a, b in zip(lower, upper)]


def coupling_matrix(blocks):
    count = blocks.shape[0]
    up = blocks[:, :, None, :]
    before = jnp.concatenate([jnp.zeros_like(blocks[:1]), blocks[:-1]], axis=0)
    down = jnp.swapaxes(before, 1, 2)[:, :, None, :]
    here = jnp.arange(count)[:, None, None, None]
    there = jnp.arange(count)[None, None, :, None]
    whole = jnp.where(there == here + 1, up, 0.0) + jnp.where(there == here - 1, down, 0.0)
    return whole.reshape(count * CH, count * CH)


def local(
    inner_state,
    outer_state,
    energies,
    dipole,
    surface,
    thresholds,
    coupling_coef,
    coupling_pattern,
    block_sizes,
    field_strength,
):
    inner_count = lax.axis_size("inner")
    outer_count = lax.axis_size("outer")
    i = lax.axis_index("inner")
    o = lax.axis_index("outer")
    where = jnp.stack([i % 2, o]).astype(jnp.int32)
    swap = pair_up(range(0, inner_count, 2), range(1, inner_count, 2))
    chips = pair_up(range(1, inner_count - 1, 2), range(2, inner_count, 2))
    even = pair_up(range(0, outer_count, 2), range(1, outer_count, 2))
    odd = pair_up(range(1, outer_count - 1, 2), range(2, outer_count, 2))

    rows = o * 128 + jnp.arange(128, dtype=jnp.int32)
    live = (rows[None, :] < block_sizes[:, None]).astype(F32)
    live = jnp.concatenate([live, live], axis=0)
    levels = jnp.concatenate([energies, energies, live], axis=0)
    coupling = coupling_coef * coupling_pattern.astype(F32)
    has_next = (i * LB + jnp.arange(LB) < inner_count * LB - 1).astype(F32)
    coupling = coupling * has_next[:, None, None]
    pack = jnp.concatenate([coupling.reshape(OWN, CH), thresholds[:, None], jnp.zeros((OWN, 128 - CH - 1), F32)], axis=1)
    surface_all = jnp.pad(surface.reshape(OWN, 128), ((0, 256 - OWN), (0, 0)))
    strip = jnp.swapaxes(outer_state[:, :, :PTS], 1, 2).reshape(2 * PTS, OWN)
    strip = jnp.pad(strip, ((0, 0), (0, 256 - OWN)))
    strip_levels = jnp.pad(thresholds[None, :], ((0, 0), (0, 256 - OWN)))

    edges = (pltpu.VMEM((64, 128), F32), pltpu.VMEM((64, 128), F32))
    c, q, to_a, to_b = call(
        first_kernel, [sds(8, 128), sds(16, 24, 128), sds(EDGE, 128), sds(EDGE, 128)], scratch=edges
    )(where, inner_state.reshape(8, 128), live, strip, dipole, surface_all, pack)

    fs = ghost = cs = None
    window = total = None
    low_pack = high_pack = None
    for index in range(STEPS * ORDER):
        step, power = index // ORDER, index % ORDER + 1
        first = index == 0
        factor = time_step / power
        from_a = lax.ppermute(to_a, "inner", swap)
        from_b = lax.ppermute(to_b, "inner", chips)
        if first:
            q, low_pack, high_pack = call(
                functools.partial(assemble_kernel, True), [sds(16, 88, 128), sds(OWN, 128), sds(OWN, 128)]
            )(where, q, from_a, from_b, strip)
            cs = c
        else:
            q, ghost = call(functools.partial(assemble_kernel, False), [sds(16, 24, 128), sds(32, 128)])(
                where, q, from_a, from_b
            )
        arrived = lax.all_to_all(q, "outer", split_axis=0, concat_axis=0, tiled=True)

        if first:
            tail, head, _ = lax.optimization_barrier((outer_state[:, :, 384:], outer_state[:, :, :128], q[0, 0, 0]))
            is_odd = (o % 2) == 1
            by_even = lax.ppermute(jnp.where(is_odd, head, tail), "outer", even)
            by_odd = lax.ppermute(jnp.where(is_odd, tail, head), "outer", odd)
            right = jnp.where(is_odd, by_odd, by_even)
            left = jnp.where(is_odd, by_even, by_odd)
            (bulk,) = call(window_kernel, [sds(OWN, 2 * WIDTH)], smem=0)(outer_state, left, right)
            packs = jnp.concatenate([low_pack, pack, high_pack], axis=0)
            couplings = coupling_matrix(packs[:, :CH].reshape(3 * LB, CH, CH))
            own = couplings[OWN : 2 * OWN]
            pairs = jnp.concatenate(
                [own[:, OWN : 2 * OWN], own[:, 2 * OWN : 2 * OWN + CH], own[:, OWN - CH : OWN]], axis=1
            )
            pairs = jnp.pad(pairs, ((0, 256 - OWN), (0, 16)))
        phase = index % ORDER
        if phase == 0:
            sent, _ = lax.optimization_barrier((bulk, q[0, 0, 0]))
            by_swap = lax.ppermute(sent, "inner", swap)
            by_chip = lax.ppermute(sent, "inner", chips)
            is_upper = (i % 2) == 1
            window = (by_swap, by_chip, is_upper)
        elif phase == 1:
            by_swap, by_chip, is_upper = window
            low = jnp.where(is_upper, by_swap, by_chip)
            high = jnp.where(is_upper, by_chip, by_swap)
            low, high, _ = lax.optimization_barrier((low, high, q[0, 0, 0]))
            window, total = call(
                functools.partial(bulk_kernel, step, (1, 2), True),
                [sds(3 * OWN, 2 * WIDTH), sds(OWN, 2 * WIDTH)],
                smem=2,
                scratch=(pltpu.VMEM((3 * OWN, 2 * WIDTH), F32),),
            )(where, field_strength, low, bulk, high, couplings, packs)
        elif phase == 2:
            window, total, _ = lax.optimization_barrier((window, total, q[0, 0, 0]))
            (bulk,) = call(
                functools.partial(bulk_kernel, step, (3, 4), False),
                [sds(OWN, 2 * WIDTH)],
                smem=2,
                scratch=(pltpu.VMEM((3 * OWN, 2 * WIDTH), F32), pltpu.VMEM((3 * OWN, 2 * WIDTH), F32)),
            )(where, field_strength, window, total, couplings, packs)

        given = (where, field_strength, dipole, surface_all, levels, pairs, strip_levels, arrived, cs)
        if not first:
            given = given + (fs, ghost)
        if index < STEPS * ORDER - 1:
            cs, fs, q, to_a, to_b = call(
                functools.partial(middle_kernel, first, power == ORDER, factor, step),
                [sds(16, 128), sds(64, 256), sds(16, 24, 128), sds(64, 128), sds(64, 128)],
                smem=2,
                scratch=edges,
            )(*given)
        else:
            c, grid = call(functools.partial(last_kernel, factor, step), [sds(8, 128), sds(2, OWN, 512)], smem=2)(
                *given, bulk
            )
    return c.reshape(2, LB, 128), grid


def solution(mesh):
    placed = (
        P(None, "inner", "outer"),
        P(None, "inner", "outer"),
        P("inner", "outer"),
        P("inner", "outer", None),
        P("inner", None, "outer"),
        P("inner"),
        P("inner", None, None),
        P("inner", None, None),
        P("inner"),
        P(),
    )
    return jax.shard_map(
        local,
        mesh=mesh,
        in_specs=placed,
        out_specs=(P(None, "inner", "outer"), P(None, "inner", "outer")),
        check_vma=False,
    )
```

time: 608 us -> 233 us (0.38); the launches traced: 598 us -> 229 us
  starting transfers between devices: 226 us -> 55.6 us
  matrix products: 118 us -> 0 us
  blocking collectives: 147 us -> 60.3 us
  Pallas kernels: 0 us -> 56.7 us
  other arithmetic: 35.6 us -> 6.24 us
  local copies, waits for them, and re-layouts: 38.2 us -> 24.1 us
    psum x16 -> x0, blocking collectives: 147 us -> none  [the longest x14 129 us: one_axis_at_a_time(): return functools.reduce(lax.psum, axes, shard)]
    dot_general x48 -> x0, matrix products: 118 us -> none  [the longest x8 45 us: local(): jnp.einsum('lij,plj->pli', dipole, gathered[:, 1:], precision=highest)]
    all_to_all x16 -> x3, starting transfers between devices: 104 us -> 18.5 us  [local(): lax.all_to_all(q, 'outer', split_axis=0, concat_axis=0, tiled=True)]
    ppermute x48 -> x22, starting transfers between devices: 122 us -> 37.2 us  [the longest x8 28 us: local(): from_b = lax.ppermute(to_b, 'inner', chips)]
    all_to_all x0 -> x5, blocking collectives: none -> 60.3 us  [local(): lax.all_to_all(q, 'outer', split_axis=0, concat_axis=0, tiled=True)]
    pallas_call x0 -> x22, Pallas kernels: none -> 56.7 us  [run(): pl.pallas_call(kernel, out_shape=outs, in_specs=[SM] * smem + [VM] * (len...]
    all_to_all x16 -> x3, waiting for transfers between devices: 24.2 us -> 0.01 us  [local(): lax.all_to_all(q, 'outer', split_axis=0, concat_axis=0, tiled=True)]
    ppermute x48 -> x22, waiting for transfers between devices: 5.04 us -> 25.1 us  [the longest x8 13.7 us: local(): from_b = lax.ppermute(to_b, 'inner', chips)]
  transfers between devices with their start and end apart: 64 -> 25, of which waited for: 9 -> 8; matrix products, arithmetic and copies ran while one was open for 24% -> 5% of each run, Pallas kernels for 0% -> 22%
where the time goes in v1:
time: 233 us; the launch traced here: 229 us
  blocking collectives  60.3 us (26%)
  Pallas kernels  56.7 us (24%)
  starting transfers between devices  55.6 us (24%)
  waiting for transfers between devices  25.1 us (11%)
  local copies, waits for them, and re-layouts  24.1 us (10%)
  other arithmetic  6.24 us (3%)
    all_to_all x5, blocking collectives, local(): lax.all_to_all(q, 'outer', split_axis=0, concat_axis=0, tiled=True)  60.3 us
    pallas_call x22, Pallas kernels, run(): pl.pallas_call(kernel, out_shape=outs, in_specs=[SM] * smem + [VM] * (len...  56.7 us
    ppermute x8, starting transfers between devices, local(): from_b = lax.ppermute(to_b, 'inner', chips)  28 us
    all_to_all x3, starting transfers between devices, local(): lax.all_to_all(q, 'outer', split_axis=0, concat_axis=0, tiled=True)  18.5 us
    unnamed x28, local copies, waits for them, and re-layouts  14.7 us
    ppermute x8, waiting for transfers between devices, local(): from_b = lax.ppermute(to_b, 'inner', chips)  13.7 us
    ppermute x1, waiting for transfers between devices, local(): by_odd = lax.ppermute(jnp.where(is_odd, tail, head), 'outer', odd)  11.4 us
  transfers between devices with their start and end apart: 25, of which 8 were waited for; matrix products, arithmetic and copies ran while one was open for 5% of the time, Pallas kernels for 22%

profile of v1, /device:TPU:88, one launch (start us, length us, event | category | flops | bytes accessed | tf_op | source)
XLA Modules:
  0.0 229.4 jit_solution(4949094581057721225)
XLA Ops:
  0.7 0.8 compare_convert_fusion.1
  1.5 0.9 slice_bitcast_fusion
  2.5 0.9 pad.17.surface.refs_1_
  3.4 0.8 copy.15
  4.3 1.0 multiply_multiply_fusion
  5.5 2.2 copy-done
  7.6 0.7 copy-done.10
  8.3 2.1 shard_map.113
  10.6 2.1 collective-permute-start.1
  12.9 3.8 %collective-permute-done.1.refs_2_ = f32[224,128]{1,0:T(8,128)S(1)} collective-permute-done((f32[224,128]{1,0:T(8,128)S(1)}, f32[224,128]{1,0:T(8,128)S(1)}, u32[]{:S(2)}, u32[]{:S(2)}) %collective-permute-start.1) | collective-permute-done | bytes 114720 | tf_op jit(solution)/shard_map/ppermute | solution.py:375
  16.7 1.5 shard_map.114
  18.2 7.2 %all-to-all-start = ((f32[16,88,128]{2,1,0:T(8,128)}), f32[16,88,128]{2,1,0:T(8,128)S(1)}, u32[]{:S(2)}, u32[]{:S(2)}) async-start(f32[16,88,128]{2,1,0:T(8,128)} %get-tuple-element.76), calls=%async_computation | async-start | bytes 1441792 | tf_op jit(solution)/shard_map/all_to_all | solution.py:385
  25.4 3.4 %collective-permute-start.17 = (f32[2,160,128]{2,1,0:T(8,128)S(1)}, f32[2,160,128]{2,1,0:T(8,128)S(1)}, u32[]{:S(2)}, u32[]{:S(2)}) collective-permute-start(f32[2,160,128]{2,1,0:T(8,128)S(1)} %get-tuple-element.148), channel_id=1, source_target_pairs={{1,2},{3,4},{5,6},{7,8},{9,10},{11,12},{13,14},{2,1},{4,3},{6,5},{... | collective-permute-start | bytes 491528 | tf_op jit(solution)/shard_map/ppermute | solution.py:391
  29.2 11.4 %collective-permute-done.17 = f32[2,160,128]{2,1,0:T(8,128)S(1)} collective-permute-done((f32[2,160,128]{2,1,0:T(8,128)S(1)}, f32[2,160,128]{2,1,0:T(8,128)S(1)}, u32[]{:S(2)}, u32[]{:S(2)}) %collective-permute-start.17) | collective-permute-done | bytes 163872 | tf_op jit(solution)/shard_map/ppermute | solution.py:391
  40.7 1.9 collective-permute-start.19
  42.7 0.9 select_add_fusion
  43.6 1.9 copy-done.11
  45.5 1.2 slice.55
  46.7 1.7 reshape.110
  48.7 2.2 copy-done.1
  50.9 3.7 %shard_map.115 = (f32[16,128]{1,0:T(8,128)S(1)}, f32[64,256]{1,0:T(8,128)S(1)}, f32[16,24,128]{2,1,0:T(8,128)S(1)}, f32[64,128]{1,0:T(8,128)S(1)}, f32[64,128]{1,0:T(8,128)S(1)}) custom-call(s32[2]{0:T(128)S(1)} %pad_add_fusion.where, f32[2]{0:T(128)S(1)} %copy-done.9, f32[4,128,2048]{2,1,0:T(8,128)S(1)} %copy-done.1, f32[256,128]{1,0:T(8,128)S(1)} %pad.17.surface.refs_1_, ...), custom_call_target="tpu_custom_call" | custom-call | tf_op jit(solution)/shard_map/pallas_call | solution.py:37
  55.2 3.6 %collective-permute-start.3 = (f32[64,128]{1,0:T(8,128)S(1)}, f32[64,128]{1,0:T(8,128)S(1)}, u32[]{:S(2)}, u32[]{:S(2)}) collective-permute-start(f32[64,128]{1,0:T(8,128)S(1)} %get-tuple-element.80), channel_id=1, source_target_pairs={{16,32},{48,64},{80,96},{32,16},{64,48},{96,80},{17,33},{49,65},{8... | collective-permute-start | bytes 98312 | tf_op jit(solution)/shard_map/ppermute | solution.py:375
  58.9 1.6 collective-permute-done.3.refs_2_
  60.4 0.6 shard_map.116
  61.0 11.8 %all_to_all.40.refs_5_ = f32[16,24,128]{2,1,0:T(8,128)S(1)} all-to-all(f32[16,24,128]{2,1,0:T(8,128)S(1)} %get-tuple-element.81), channel_id=1, replica_groups=mesh['inner'=8,'outer'=16] {'outer'}, dimensions={0} | all-to-all | bytes 393216 | tf_op jit(solution)/shard_map/all_to_all | solution.py:385
  72.8 3.8 %shard_map.117 = (f32[16,128]{1,0:T(8,128)S(1)}, f32[64,256]{1,0:T(8,128)S(1)}, f32[16,24,128]{2,1,0:T(8,128)S(1)}, f32[64,128]{1,0:T(8,128)S(1)}, f32[64,128]{1,0:T(8,128)S(1)}) custom-call(s32[2]{0:T(128)S(1)} %pad_add_fusion.where, f32[2]{0:T(128)S(1)} %copy-done.9, f32[4,128,2048]{2,1,0:T(8,128)S(1)} %copy-done.2, f32[256,128]{1,0:T(8,128)S(1)} %pad.17.surface.refs_1_, ...), custom_call_target="tpu_custom_call" | custom-call | tf_op jit(solution)/shard_map/pallas_call | solution.py:37
  76.6 3.9 %collective-permute-start.5 = (f32[64,128]{1,0:T(8,128)S(1)}, f32[64,128]{1,0:T(8,128)S(1)}, u32[]{:S(2)}, u32[]{:S(2)}) collective-permute-start(f32[64,128]{1,0:T(8,128)S(1)} %get-tuple-element.87), channel_id=1, source_target_pairs={{16,32},{48,64},{80,96},{32,16},{64,48},{96,80},{17,33},{49,65},{8... | collective-permute-start | bytes 98312 | tf_op jit(solution)/shard_map/ppermute | solution.py:375
  80.6 1.6 collective-permute-done.5.refs_2_
  82.7 11.6 %all_to_all.41.refs_5_ = f32[16,24,128]{2,1,0:T(8,128)S(1)} all-to-all(f32[16,24,128]{2,1,0:T(8,128)S(1)} %get-tuple-element.88), channel_id=1, replica_groups=mesh['inner'=8,'outer'=16] {'outer'}, dimensions={0} | all-to-all | bytes 393216 | tf_op jit(solution)/shard_map/all_to_all | solution.py:385
  94.3 3.8 %shard_map.119 = (f32[16,128]{1,0:T(8,128)S(1)}, f32[64,256]{1,0:T(8,128)S(1)}, f32[16,24,128]{2,1,0:T(8,128)S(1)}, f32[64,128]{1,0:T(8,128)S(1)}, f32[64,128]{1,0:T(8,128)S(1)}) custom-call(s32[2]{0:T(128)S(1)} %pad_add_fusion.where, f32[2]{0:T(128)S(1)} %copy-done.9, f32[4,128,2048]{2,1,0:T(8,128)S(1)} %copy-done.2, f32[256,128]{1,0:T(8,128)S(1)} %pad.17.surface.refs_1_, ...), custom_call_target="tpu_custom_call" | custom-call | tf_op jit(solution)/shard_map/pallas_call | solution.py:37
  98.2 3.9 %collective-permute-start.7 = (f32[64,128]{1,0:T(8,128)S(1)}, f32[64,128]{1,0:T(8,128)S(1)}, u32[]{:S(2)}, u32[]{:S(2)}) collective-permute-start(f32[64,128]{1,0:T(8,128)S(1)} %get-tuple-element.94), channel_id=1, source_target_pairs={{16,32},{48,64},{80,96},{32,16},{64,48},{96,80},{17,33},{49,65},{8... | collective-permute-start | bytes 98312 | tf_op jit(solution)/shard_map/ppermute | solution.py:375
  102.1 3.3 %add.68.refs_3_.refs_2_ = f32[480,480]{1,0:T(8,128)S(1)} reshape(f32[12,40,12,40]{3,2,1,0:T(8,128)} %copy-done.11) | data formatting | bytes 1843200 | tf_op jit(solution)/shard_map/add | solution.py:323
  105.5 1.2 shard_map.120
  106.7 5.7 %all-to-all-start.3 = ((f32[16,24,128]{2,1,0:T(8,128)}), f32[16,24,128]{2,1,0:T(8,128)S(1)}, u32[]{:S(2)}, u32[]{:S(2)}) async-start(f32[16,24,128]{2,1,0:T(8,128)} %get-tuple-element.95), calls=%async_computation.3 | async-start | bytes 393216 | tf_op jit(solution)/shard_map/all_to_all | solution.py:385
  112.4 1.5 broadcast_select_fusion.2
  113.9 6.0 %shard_map.130 = (f32[480,1280]{1,0:T(8,128)}, f32[160,1280]{1,0:T(8,128)S(1)}) custom-call(s32[2]{0:T(128)S(1)} %pad_add_fusion.where, f32[2]{0:T(128)S(1)} %copy-done.9, f32[160,1280]{1,0:T(8,128)S(1)} %get-tuple-element.130.refs_0_, f32[160,1280]{1,0:T(8,128)S(1)} %shard_map.129.refs_1_, f32[160,1280]{1,0:T(8,128)S(1)} %get-tuple-element.131.refs_2_, ...), custom_call_target="tpu_custom_call" | custom-call | tf_op jit(solution)/shard_map/pallas_call | solution.py:37
  119.9 1.7 copy-done.7
  121.6 3.2 %shard_map.131.refs_1_ = f32[160,1280]{1,0:T(8,128)S(1)} custom-call(s32[2]{0:T(128)S(1)} %pad_add_fusion.where, f32[2]{0:T(128)S(1)} %copy-done.9, f32[480,1280]{1,0:T(8,128)S(1)} %copy-done.7, f32[160,1280]{1,0:T(8,128)S(1)} %get-tuple-element.133.refs_1_, f32[480,480]{1,0:T(8,128)S(1)} %add.68.refs_3_.refs_2_, f32[480,128]{1,0:T(8,128)S(1)} %pad_maximum_fusion.refs_4_.refs_3_), custom_call_target="tpu_custom_call" | custom-call | tf_op jit(solution)/shard_map/pallas_call | solution.py:37
  124.8 1.9 collective-permute-start.21
  127.0 2.2 copy-done.3
  129.2 3.7 %shard_map.121 = (f32[16,128]{1,0:T(8,128)S(1)}, f32[64,256]{1,0:T(8,128)S(1)}, f32[16,24,128]{2,1,0:T(8,128)S(1)}, f32[64,128]{1,0:T(8,128)S(1)}, f32[64,128]{1,0:T(8,128)S(1)}) custom-call(s32[2]{0:T(128)S(1)} %pad_add_fusion.where, f32[2]{0:T(128)S(1)} %copy-done.9, f32[4,128,2048]{2,1,0:T(8,128)S(1)} %copy-done.3, f32[256,128]{1,0:T(8,128)S(1)} %pad.17.surface.refs_1_, ...), custom_call_target="tpu_custom_call" | custom-call | tf_op jit(solution)/shard_map/pallas_call | solution.py:37
  133.2 3.6 %collective-permute-start.9 = (f32[64,128]{1,0:T(8,128)S(1)}, f32[64,128]{1,0:T(8,128)S(1)}, u32[]{:S(2)}, u32[]{:S(2)}) collective-permute-start(f32[64,128]{1,0:T(8,128)S(1)} %get-tuple-element.101), channel_id=1, source_target_pairs={{16,32},{48,64},{80,96},{32,16},{64,48},{96,80},{17,33},{49,65},{8... | collective-permute-start | bytes 98312 | tf_op jit(solution)/shard_map/ppermute | solution.py:375
  136.9 1.9 collective-permute-done.9.refs_2_
  139.4 13.2 %all_to_all.42.refs_5_ = f32[16,24,128]{2,1,0:T(8,128)S(1)} all-to-all(f32[16,24,128]{2,1,0:T(8,128)S(1)} %get-tuple-element.102), channel_id=1, replica_groups=mesh['inner'=8,'outer'=16] {'outer'}, dimensions={0} | all-to-all | bytes 393216 | tf_op jit(solution)/shard_map/all_to_all | solution.py:385
  152.5 3.8 %shard_map.123 = (f32[16,128]{1,0:T(8,128)S(1)}, f32[64,256]{1,0:T(8,128)S(1)}, f32[16,24,128]{2,1,0:T(8,128)S(1)}, f32[64,128]{1,0:T(8,128)S(1)}, f32[64,128]{1,0:T(8,128)S(1)}) custom-call(s32[2]{0:T(128)S(1)} %pad_add_fusion.where, f32[2]{0:T(128)S(1)} %copy-done.9, f32[4,128,2048]{2,1,0:T(8,128)S(1)} %copy-done.4, f32[256,128]{1,0:T(8,128)S(1)} %pad.17.surface.refs_1_, ...), custom_call_target="tpu_custom_call" | custom-call | tf_op jit(solution)/shard_map/pallas_call | solution.py:37
  156.4 3.6 %collective-permute-start.11 = (f32[64,128]{1,0:T(8,128)S(1)}, f32[64,128]{1,0:T(8,128)S(1)}, u32[]{:S(2)}, u32[]{:S(2)}) collective-permute-start(f32[64,128]{1,0:T(8,128)S(1)} %get-tuple-element.108), channel_id=1, source_target_pairs={{16,32},{48,64},{80,96},{32,16},{64,48},{96,80},{17,33},{49,65},{8... | collective-permute-start | bytes 98312 | tf_op jit(solution)/shard_map/ppermute | solution.py:375
  160.0 1.6 collective-permute-done.11.refs_2_
  161.6 0.6 shard_map.124
  162.2 11.9 %all_to_all.43.refs_5_ = f32[16,24,128]{2,1,0:T(8,128)S(1)} all-to-all(f32[16,24,128]{2,1,0:T(8,128)S(1)} %get-tuple-element.109), channel_id=1, replica_groups=mesh['inner'=8,'outer'=16] {'outer'}, dimensions={0} | all-to-all | bytes 393216 | tf_op jit(solution)/shard_map/all_to_all | solution.py:385
  174.1 3.8 %shard_map.125 = (f32[16,128]{1,0:T(8,128)S(1)}, f32[64,256]{1,0:T(8,128)S(1)}, f32[16,24,128]{2,1,0:T(8,128)S(1)}, f32[64,128]{1,0:T(8,128)S(1)}, f32[64,128]{1,0:T(8,128)S(1)}) custom-call(s32[2]{0:T(128)S(1)} %pad_add_fusion.where, f32[2]{0:T(128)S(1)} %copy-done.9, f32[4,128,2048]{2,1,0:T(8,128)S(1)} %copy-done.4, f32[256,128]{1,0:T(8,128)S(1)} %pad.17.surface.refs_1_, ...), custom_call_target="tpu_custom_call" | custom-call | tf_op jit(solution)/shard_map/pallas_call | solution.py:37
  177.9 3.6 %collective-permute-start.13 = (f32[64,128]{1,0:T(8,128)S(1)}, f32[64,128]{1,0:T(8,128)S(1)}, u32[]{:S(2)}, u32[]{:S(2)}) collective-permute-start(f32[64,128]{1,0:T(8,128)S(1)} %get-tuple-element.115), channel_id=1, source_target_pairs={{16,32},{48,64},{80,96},{32,16},{64,48},{96,80},{17,33},{49,65},{8... | collective-permute-start | bytes 98312 | tf_op jit(solution)/shard_map/ppermute | solution.py:375
  181.6 1.6 collective-permute-done.13.refs_2_
  183.7 11.9 %all_to_all.44.refs_5_ = f32[16,24,128]{2,1,0:T(8,128)S(1)} all-to-all(f32[16,24,128]{2,1,0:T(8,128)S(1)} %get-tuple-element.116), channel_id=1, replica_groups=mesh['inner'=8,'outer'=16] {'outer'}, dimensions={0} | all-to-all | bytes 393216 | tf_op jit(solution)/shard_map/all_to_all | solution.py:385
  195.6 3.8 %shard_map.127 = (f32[16,128]{1,0:T(8,128)S(1)}, f32[64,256]{1,0:T(8,128)S(1)}, f32[16,24,128]{2,1,0:T(8,128)S(1)}, f32[64,128]{1,0:T(8,128)S(1)}, f32[64,128]{1,0:T(8,128)S(1)}) custom-call(s32[2]{0:T(128)S(1)} %pad_add_fusion.where, f32[2]{0:T(128)S(1)} %copy-done.9, f32[4,128,2048]{2,1,0:T(8,128)S(1)} %copy-done.4, f32[256,128]{1,0:T(8,128)S(1)} %pad.17.surface.refs_1_, ...), custom_call_target="tpu_custom_call" | custom-call | tf_op jit(solution)/shard_map/pallas_call | solution.py:37
  199.5 3.6 %collective-permute-start.15 = (f32[64,128]{1,0:T(8,128)S(1)}, f32[64,128]{1,0:T(8,128)S(1)}, u32[]{:S(2)}, u32[]{:S(2)}) collective-permute-start(f32[64,128]{1,0:T(8,128)S(1)} %get-tuple-element.122), channel_id=1, source_target_pairs={{16,32},{48,64},{80,96},{32,16},{64,48},{96,80},{17,33},{49,65},{8... | collective-permute-start | bytes 98312 | tf_op jit(solution)/shard_map/ppermute | solution.py:375
  203.1 1.6 collective-permute-done.15.refs_2_
  204.7 1.2 shard_map.128
  205.9 5.7 %all-to-all-start.7 = ((f32[16,24,128]{2,1,0:T(8,128)}), f32[16,24,128]{2,1,0:T(8,128)S(1)}, u32[]{:S(2)}, u32[]{:S(2)}) async-start(f32[16,24,128]{2,1,0:T(8,128)} %get-tuple-element.123), calls=%async_computation.7 | async-start | bytes 393216 | tf_op jit(solution)/shard_map/all_to_all | solution.py:385
  211.6 1.5 broadcast_select_fusion
  213.1 6.0 %shard_map.132 = (f32[480,1280]{1,0:T(8,128)}, f32[160,1280]{1,0:T(8,128)S(1)}) custom-call(s32[2]{0:T(128)S(1)} %pad_add_fusion.where, f32[2]{0:T(128)S(1)} %copy-done.9, f32[160,1280]{1,0:T(8,128)S(1)} %get-tuple-element.134.refs_0_, f32[160,1280]{1,0:T(8,128)S(1)} %shard_map.131.refs_1_, f32[160,1280]{1,0:T(8,128)S(1)} %get-tuple-element.135.refs_2_, ...), custom_call_target="tpu_custom_call" | custom-call | tf_op jit(solution)/shard_map/pallas_call | solution.py:37
  219.1 1.7 copy-done.6
  220.8 3.2 %shard_map.133.bulk = f32[160,1280]{1,0:T(8,128)S(1)} custom-call(s32[2]{0:T(128)S(1)} %pad_add_fusion.where, f32[2]{0:T(128)S(1)} %copy-done.9, f32[480,1280]{1,0:T(8,128)S(1)} %copy-done.6, f32[160,1280]{1,0:T(8,128)S(1)} %get-tuple-element.137.refs_1_, f32[480,480]{1,0:T(8,128)S(1)} %add.68.refs_3_.refs_2_, f32[480,128]{1,0:T(8,128)S(1)} %pad_maximum_fusion.refs_4_.refs_3_), custom_call_target="tpu_custom_call" | custom-call | tf_op jit(solution)/shard_map/pallas_call | solution.py:37
  224.0 2.2 copy-done.5
  226.2 3.2 %shard_map.134 = (f32[8,128]{1,0:T(8,128)}, f32[2,160,512]{2,1,0:T(8,128)}) custom-call(s32[2]{0:T(128)S(1)} %pad_add_fusion.where, f32[2]{0:T(128)S(1)} %copy-done.9, f32[4,128,2048]{2,1,0:T(8,128)S(1)} %copy-done.5, f32[256,128]{1,0:T(8,128)S(1)} %pad.17.surface.refs_1_, f32[16,128]{1,0:T(8,128)S(1)} %pad_maximum_fusion.2.refs_2_.levels, ...), custom_call_target="tpu_custom_call" | custom-call | tf_op jit(solution)/shard_map/pallas_call | solution.py:37
  (75 shorter events, 4.8 us)
Async XLA Ops:
  0.6 12.1 %copy-start.8 = (f32[2,160,512]{2,1,0:T(8,128)S(1)}, f32[2,160,512]{2,1,0:T(8,128)}, u32[]{:S(2)}) copy-start(f32[2,160,512]{2,1,0:T(8,128)} %outer.1) | copy-start | bytes 1966084
  0.6 12.2 %copy-start.12 = (f32[160]{0:T(256)S(1)}, f32[160]{0:T(256)}, u32[]{:S(2)}) copy-start(f32[160]{0:T(256)} %param.15) | copy-start | bytes 1924
  0.7 12.2 %copy-start.13 = (f32[4,128]{1,0:T(4,128)S(1)}, f32[4,128]{1,0:T(4,128)}, u32[]{:S(2)}) copy-start(f32[4,128]{1,0:T(4,128)} %param.12) | copy-start | bytes 6148
  5.4 2.2 copy-start
  7.6 0.7 copy-start.10
  10.5 2.4 %collective-permute-start = (f32[224,128]{1,0:T(8,128)S(1)}, f32[224,128]{1,0:T(8,128)S(1)}, u32[]{:S(2)}, u32[]{:S(2)}) collective-permute-start(f32[224,128]{1,0:T(8,128)S(1)} %get-tuple-element.72), channel_id=1, source_target_pairs={{0,16},{32,48},{64,80},{96,112},{16,0},{48,32},{80,64},{112,96},{1... | collective-permute-start | bytes 344072 | tf_op jit(solution)/shard_map/ppermute | solution.py:374
  10.6 6.1 %collective-permute-start.1 = (f32[224,128]{1,0:T(8,128)S(1)}, f32[224,128]{1,0:T(8,128)S(1)}, u32[]{:S(2)}, u32[]{:S(2)}) collective-permute-start(f32[224,128]{1,0:T(8,128)S(1)} %get-tuple-element.73), channel_id=1, source_target_pairs={{16,32},{48,64},{80,96},{32,16},{64,48},{96,80},{17,33},{49,65},{8... | collective-permute-start | bytes 344072 | tf_op jit(solution)/shard_map/ppermute | solution.py:375
  18.2 30.5 %all-to-all-start = ((f32[16,88,128]{2,1,0:T(8,128)}), f32[16,88,128]{2,1,0:T(8,128)S(1)}, u32[]{:S(2)}, u32[]{:S(2)}) async-start(f32[16,88,128]{2,1,0:T(8,128)} %get-tuple-element.76), calls=%async_computation | async-start | bytes 1441792 | tf_op jit(solution)/shard_map/all_to_all | solution.py:385
  25.4 15.2 %collective-permute-start.17 = (f32[2,160,128]{2,1,0:T(8,128)S(1)}, f32[2,160,128]{2,1,0:T(8,128)S(1)}, u32[]{:S(2)}, u32[]{:S(2)}) collective-permute-start(f32[2,160,128]{2,1,0:T(8,128)S(1)} %get-tuple-element.148), channel_id=1, source_target_pairs={{1,2},{3,4},{5,6},{7,8},{9,10},{11,12},{13,14},{2,1},{4,3},{6,5},{... | collective-permute-start | bytes 491528 | tf_op jit(solution)/shard_map/ppermute | solution.py:391
  28.8 11.8 %collective-permute-start.16 = (f32[2,160,128]{2,1,0:T(8,128)S(1)}, f32[2,160,128]{2,1,0:T(8,128)S(1)}, u32[]{:S(2)}, u32[]{:S(2)}) collective-permute-start(f32[2,160,128]{2,1,0:T(8,128)S(1)} %get-tuple-element.149), channel_id=1, source_target_pairs={{0,1},{2,3},{4,5},{6,7},{8,9},{10,11},{12,13},{14,15},{1,0},{3,2},... | collective-permute-start | bytes 491528 | tf_op jit(solution)/shard_map/ppermute | solution.py:390
  40.7 71.8 %collective-permute-start.19 = (f32[160,1280]{1,0:T(8,128)S(1)}, f32[160,1280]{1,0:T(8,128)}, u32[]{:S(2)}, u32[]{:S(2)}) collective-permute-start(f32[160,1280]{1,0:T(8,128)S(1)} %shard_map.129.refs_1_), channel_id=1, source_target_pairs={{16,32},{48,64},{80,96},{32,16},{64,48},{96,80},{17,33},{49,65},{8... | collective-permute-start | bytes 2457608 | tf_op jit(solution)/shard_map/ppermute | solution.py:406
  42.6 69.8 %collective-permute-start.18 = (f32[160,1280]{1,0:T(8,128)S(1)}, f32[160,1280]{1,0:T(8,128)}, u32[]{:S(2)}, u32[]{:S(2)}) collective-permute-start(f32[160,1280]{1,0:T(8,128)S(1)} %shard_map.129.refs_1_), channel_id=1, source_target_pairs={{0,16},{32,48},{64,80},{96,112},{16,0},{48,32},{80,64},{112,96},{1... | collective-permute-start | bytes 2457608 | tf_op jit(solution)/shard_map/ppermute | solution.py:405
  42.7 6.0 %copy-start.9 = (f32[2]{0:T(128)S(1)}, f32[2]{0:T(128)}, u32[]{:S(2)}) copy-start(f32[2]{0:T(128)} %strengths.23) | copy-start | bytes 28
  43.6 1.9 copy-start.11
  48.7 2.2 copy-start.1
  50.9 21.9 %copy-start.2 = (f32[4,128,2048]{2,1,0:T(8,128)S(1)}, f32[4,128,2048]{2,1,0:T(8,128)}, u32[]{:S(2)}) copy-start(f32[4,128,2048]{2,1,0:T(8,128)} %dipole.3) | copy-start | bytes 12582916
  54.7 4.2 %collective-permute-start.2 = (f32[64,128]{1,0:T(8,128)S(1)}, f32[64,128]{1,0:T(8,128)S(1)}, u32[]{:S(2)}, u32[]{:S(2)}) collective-permute-start(f32[64,128]{1,0:T(8,128)S(1)} %get-tuple-element.79), channel_id=1, source_target_pairs={{0,16},{32,48},{64,80},{96,112},{16,0},{48,32},{80,64},{112,96},{1... | collective-permute-start | bytes 98312 | tf_op jit(solution)/shard_map/ppermute | solution.py:374
  55.2 5.2 %collective-permute-start.3 = (f32[64,128]{1,0:T(8,128)S(1)}, f32[64,128]{1,0:T(8,128)S(1)}, u32[]{:S(2)}, u32[]{:S(2)}) collective-permute-start(f32[64,128]{1,0:T(8,128)S(1)} %get-tuple-element.80), channel_id=1, source_target_pairs={{16,32},{48,64},{80,96},{32,16},{64,48},{96,80},{17,33},{49,65},{8... | collective-permute-start | bytes 98312 | tf_op jit(solution)/shard_map/ppermute | solution.py:375
  76.6 4.0 %collective-permute-start.4 = (f32[64,128]{1,0:T(8,128)S(1)}, f32[64,128]{1,0:T(8,128)S(1)}, u32[]{:S(2)}, u32[]{:S(2)}) collective-permute-start(f32[64,128]{1,0:T(8,128)S(1)} %get-tuple-element.86), channel_id=1, source_target_pairs={{0,16},{32,48},{64,80},{96,112},{16,0},{48,32},{80,64},{112,96},{1... | collective-permute-start | bytes 98312 | tf_op jit(solution)/shard_map/ppermute | solution.py:374
  76.6 5.5 %collective-permute-start.5 = (f32[64,128]{1,0:T(8,128)S(1)}, f32[64,128]{1,0:T(8,128)S(1)}, u32[]{:S(2)}, u32[]{:S(2)}) collective-permute-start(f32[64,128]{1,0:T(8,128)S(1)} %get-tuple-element.87), channel_id=1, source_target_pairs={{16,32},{48,64},{80,96},{32,16},{64,48},{96,80},{17,33},{49,65},{8... | collective-permute-start | bytes 98312 | tf_op jit(solution)/shard_map/ppermute | solution.py:375
  98.1 7.4 %collective-permute-start.6 = (f32[64,128]{1,0:T(8,128)S(1)}, f32[64,128]{1,0:T(8,128)S(1)}, u32[]{:S(2)}, u32[]{:S(2)}) collective-permute-start(f32[64,128]{1,0:T(8,128)S(1)} %get-tuple-element.93), channel_id=1, source_target_pairs={{0,16},{32,48},{64,80},{96,112},{16,0},{48,32},{80,64},{112,96},{1... | collective-permute-start | bytes 98312 | tf_op jit(solution)/shard_map/ppermute | solution.py:374
  98.2 7.3 %collective-permute-start.7 = (f32[64,128]{1,0:T(8,128)S(1)}, f32[64,128]{1,0:T(8,128)S(1)}, u32[]{:S(2)}, u32[]{:S(2)}) collective-permute-start(f32[64,128]{1,0:T(8,128)S(1)} %get-tuple-element.94), channel_id=1, source_target_pairs={{16,32},{48,64},{80,96},{32,16},{64,48},{96,80},{17,33},{49,65},{8... | collective-permute-start | bytes 98312 | tf_op jit(solution)/shard_map/ppermute | solution.py:375
  106.7 20.2 %all-to-all-start.3 = ((f32[16,24,128]{2,1,0:T(8,128)}), f32[16,24,128]{2,1,0:T(8,128)S(1)}, u32[]{:S(2)}, u32[]{:S(2)}) async-start(f32[16,24,128]{2,1,0:T(8,128)} %get-tuple-element.95), calls=%async_computation.3 | async-start | bytes 393216 | tf_op jit(solution)/shard_map/all_to_all | solution.py:385
  119.9 1.7 copy-start.7
  124.8 86.8 %collective-permute-start.21 = (f32[160,1280]{1,0:T(8,128)S(1)}, f32[160,1280]{1,0:T(8,128)}, u32[]{:S(2)}, u32[]{:S(2)}) collective-permute-start(f32[160,1280]{1,0:T(8,128)S(1)} %shard_map.131.refs_1_), channel_id=1, source_target_pairs={{16,32},{48,64},{80,96},{32,16},{64,48},{96,80},{17,33},{49,65},{8... | collective-permute-start | bytes 2457608 | tf_op jit(solution)/shard_map/ppermute | solution.py:406
  126.7 84.9 %collective-permute-start.20 = (f32[160,1280]{1,0:T(8,128)S(1)}, f32[160,1280]{1,0:T(8,128)}, u32[]{:S(2)}, u32[]{:S(2)}) collective-permute-start(f32[160,1280]{1,0:T(8,128)S(1)} %shard_map.131.refs_1_), channel_id=1, source_target_pairs={{0,16},{32,48},{64,80},{96,112},{16,0},{48,32},{80,64},{112,96},{1... | collective-permute-start | bytes 2457608 | tf_op jit(solution)/shard_map/ppermute | solution.py:405
  127.0 2.2 copy-start.3
  129.2 23.3 %copy-start.4 = (f32[4,128,2048]{2,1,0:T(8,128)S(1)}, f32[4,128,2048]{2,1,0:T(8,128)}, u32[]{:S(2)}) copy-start(f32[4,128,2048]{2,1,0:T(8,128)} %dipole.3) | copy-start | bytes 12582916
  132.9 4.0 %collective-permute-start.8 = (f32[64,128]{1,0:T(8,128)S(1)}, f32[64,128]{1,0:T(8,128)S(1)}, u32[]{:S(2)}, u32[]{:S(2)}) collective-permute-start(f32[64,128]{1,0:T(8,128)S(1)} %get-tuple-element.100), channel_id=1, source_target_pairs={{0,16},{32,48},{64,80},{96,112},{16,0},{48,32},{80,64},{112,96},{1... | collective-permute-start | bytes 98312 | tf_op jit(solution)/shard_map/ppermute | solution.py:374
  133.2 5.5 %collective-permute-start.9 = (f32[64,128]{1,0:T(8,128)S(1)}, f32[64,128]{1,0:T(8,128)S(1)}, u32[]{:S(2)}, u32[]{:S(2)}) collective-permute-start(f32[64,128]{1,0:T(8,128)S(1)} %get-tuple-element.101), channel_id=1, source_target_pairs={{16,32},{48,64},{80,96},{32,16},{64,48},{96,80},{17,33},{49,65},{8... | collective-permute-start | bytes 98312 | tf_op jit(solution)/shard_map/ppermute | solution.py:375
  156.3 3.7 %collective-permute-start.10 = (f32[64,128]{1,0:T(8,128)S(1)}, f32[64,128]{1,0:T(8,128)S(1)}, u32[]{:S(2)}, u32[]{:S(2)}) collective-permute-start(f32[64,128]{1,0:T(8,128)S(1)} %get-tuple-element.107), channel_id=1, source_target_pairs={{0,16},{32,48},{64,80},{96,112},{16,0},{48,32},{80,64},{112,96},{1... | collective-permute-start | bytes 98312 | tf_op jit(solution)/shard_map/ppermute | solution.py:374
  156.4 5.2 %collective-permute-start.11 = (f32[64,128]{1,0:T(8,128)S(1)}, f32[64,128]{1,0:T(8,128)S(1)}, u32[]{:S(2)}, u32[]{:S(2)}) collective-permute-start(f32[64,128]{1,0:T(8,128)S(1)} %get-tuple-element.108), channel_id=1, source_target_pairs={{16,32},{48,64},{80,96},{32,16},{64,48},{96,80},{17,33},{49,65},{8... | collective-permute-start | bytes 98312 | tf_op jit(solution)/shard_map/ppermute | solution.py:375
  177.8 3.7 %collective-permute-start.12 = (f32[64,128]{1,0:T(8,128)S(1)}, f32[64,128]{1,0:T(8,128)S(1)}, u32[]{:S(2)}, u32[]{:S(2)}) collective-permute-start(f32[64,128]{1,0:T(8,128)S(1)} %get-tuple-element.114), channel_id=1, source_target_pairs={{0,16},{32,48},{64,80},{96,112},{16,0},{48,32},{80,64},{112,96},{1... | collective-permute-start | bytes 98312 | tf_op jit(solution)/shard_map/ppermute | solution.py:374
  177.9 5.2 %collective-permute-start.13 = (f32[64,128]{1,0:T(8,128)S(1)}, f32[64,128]{1,0:T(8,128)S(1)}, u32[]{:S(2)}, u32[]{:S(2)}) collective-permute-start(f32[64,128]{1,0:T(8,128)S(1)} %get-tuple-element.115), channel_id=1, source_target_pairs={{16,32},{48,64},{80,96},{32,16},{64,48},{96,80},{17,33},{49,65},{8... | collective-permute-start | bytes 98312 | tf_op jit(solution)/shard_map/ppermute | solution.py:375
  199.4 3.7 %collective-permute-start.14 = (f32[64,128]{1,0:T(8,128)S(1)}, f32[64,128]{1,0:T(8,128)S(1)}, u32[]{:S(2)}, u32[]{:S(2)}) collective-permute-start(f32[64,128]{1,0:T(8,128)S(1)} %get-tuple-element.121), channel_id=1, source_target_pairs={{0,16},{32,48},{64,80},{96,112},{16,0},{48,32},{80,64},{112,96},{1... | collective-permute-start | bytes 98312 | tf_op jit(solution)/shard_map/ppermute | solution.py:374
  199.5 5.2 %collective-permute-start.15 = (f32[64,128]{1,0:T(8,128)S(1)}, f32[64,128]{1,0:T(8,128)S(1)}, u32[]{:S(2)}, u32[]{:S(2)}) collective-permute-start(f32[64,128]{1,0:T(8,128)S(1)} %get-tuple-element.122), channel_id=1, source_target_pairs={{16,32},{48,64},{80,96},{32,16},{64,48},{96,80},{17,33},{49,65},{8... | collective-permute-start | bytes 98312 | tf_op jit(solution)/shard_map/ppermute | solution.py:375
  205.9 18.0 %all-to-all-start.7 = ((f32[16,24,128]{2,1,0:T(8,128)}), f32[16,24,128]{2,1,0:T(8,128)S(1)}, u32[]{:S(2)}, u32[]{:S(2)}) async-start(f32[16,24,128]{2,1,0:T(8,128)} %get-tuple-element.123), calls=%async_computation.7 | async-start | bytes 393216 | tf_op jit(solution)/shard_map/all_to_all | solution.py:385
  219.1 1.7 copy-start.6
  224.0 2.2 copy-start.5

commit v2 on v1

v2 whole, which is shorter than its diff:
```python
import functools

import jax
import jax.numpy as jnp
from jax import lax
from jax.experimental import pallas as pl
from jax.experimental.pallas import tpu as pltpu
from jax.sharding import PartitionSpec as P

STEPS = 2
ORDER = 4
kinetic_scale = 3.125
time_step = 0.1

F32 = jnp.float32
BF16 = jnp.bfloat16
HIGHEST = lax.Precision.HIGHEST
VM = pl.BlockSpec(memory_space=pltpu.VMEM)
SM = pl.BlockSpec(memory_space=pltpu.SMEM)
HBM = pl.BlockSpec(memory_space=pltpu.HBM)
DIPOLE = (pltpu.VMEM((4, 128, 2048), jnp.float32), pltpu.SemaphoreType.DMA((4,)))

LB = 4
CH = 40
OWN = LB * CH
PTS = 16
HALO = 8
WIDTH = 640
EDGE = 64 + OWN
NT = (((1,), (1,)), ((), ()))


def sds(*shape):
    return jax.ShapeDtypeStruct(shape, F32)


def call(kernel, outs, smem=1, scratch=(), limit=20, hbm=()):
    def run(*args):
        return pl.pallas_call(
            kernel,
            out_shape=outs,
            in_specs=[SM] * smem + [HBM if n in hbm else VM for n in range(smem, len(args))],
            out_specs=[VM] * len(outs),
            scratch_shapes=list(scratch),
            compiler_params=pltpu.CompilerParams(vmem_limit_bytes=limit << 20),
        )(*args)

    return run


def rows_of(lines, shape):
    return lax.broadcasted_iota(jnp.int32, shape, lines)


def block_mask():
    lanes = rows_of(1, (8, 256))
    first = (rows_of(0, (8, 256)) % LB) * CH
    return jnp.where((lanes >= first) & (lanes < first + CH), 1.0, 0.0).astype(F32)


def edge_tiles(strip):
    lanes = rows_of(1, (2 * PTS, 128))
    up = pltpu.roll(strip, 80, 1)[:, 128:]
    down = pltpu.roll(strip, 160, 1)[:, 128:]
    zero = jnp.zeros_like(up)
    up = jnp.where((lanes >= 72) & (lanes < 112), up, zero)
    down = jnp.where((lanes >= 32) & (lanes < 72), down, zero)
    return up, down


def emit(parity, c, strip, dipole, surface, q_ref, a_ref, b_ref, up_ref, down_ref, copies=None):
    ahead = jnp.concatenate([c[1:4], c[0:1], c[5:8], c[4:5]], axis=0)
    partial = lax.dot_general(c, surface[...], NT, precision=HIGHEST, preferred_element_type=F32)
    partial = partial * block_mask()
    b_re = jnp.sum(partial[0:4], axis=0, keepdims=True)
    b_im = jnp.sum(partial[4:8], axis=0, keepdims=True)
    tail = jnp.concatenate(
        [b_re[:, :128], b_re[:, 128:], b_im[:, :128], b_im[:, 128:], jnp.zeros((4, 128), F32)], axis=0
    )
    for s in range(16):
        q_ref[s, 0:8, :] = ahead
        q_ref[s, 8:16, :] = jnp.zeros((8, 128), F32)
        q_ref[s, 16:24, :] = tail
    for l in range(LB):
        re = jnp.broadcast_to(c[l : l + 1], (128, 128)).T
        im = jnp.broadcast_to(c[4 + l : 5 + l], (128, 128)).T
        if copies is not None:
            copies[l].wait()

        def body(s, carry):
            tile = dipole[l, :, pl.ds(pl.multiple_of(s * 128, 128), 128)]
            sum_re = jnp.sum(tile * re, axis=0, keepdims=True)
            sum_im = jnp.sum(tile * im, axis=0, keepdims=True)
            if l < LB - 1:
                q_ref[s, 9 + l : 10 + l, :] = sum_re
                q_ref[s, 13 + l : 14 + l, :] = sum_im
            else:
                up_ref[pl.ds(s, 1), :] = sum_re
                up_ref[pl.ds(16 + s, 1), :] = sum_im
            return carry

        lax.fori_loop(0, 16, body, 0, unroll=16)
    up, down = edge_tiles(strip)
    up_ref[32:64, :] = up
    down_ref[0:8, :] = c
    down_ref[8:32, :] = jnp.zeros((24, 128), F32)
    down_ref[32:64, :] = down

    @pl.when(parity == 0)
    def _():
        a_ref[0:64, :] = up_ref[...]
        b_ref[0:64, :] = down_ref[...]

    @pl.when(parity != 0)
    def _():
        a_ref[0:64, :] = down_ref[...]
        b_ref[0:64, :] = up_ref[...]


def fetch(dipole, target, arrivals):
    copies = [pltpu.make_async_copy(dipole.at[l], target.at[l], arrivals.at[l]) for l in range(LB)]
    for copy in copies:
        copy.start()
    return copies


def first_kernel(
    where,
    sizes,
    inner,
    energies,
    surface,
    coef,
    pattern,
    thresholds,
    dipole,
    outer,
    cs_ref,
    fs_ref,
    q_ref,
    a_ref,
    b_ref,
    levels_ref,
    surface_ref,
    pack_ref,
    strip_levels_ref,
    up_ref,
    down_ref,
    dipole_ref,
    dipole_arrivals,
    inner_v,
    energies_v,
    surface_v,
    coef_v,
    pattern_v,
    thresholds_v,
    corner_v,
    arrivals,
):
    copies = [
        pltpu.make_async_copy(source, target, arrivals.at[n])
        for n, (source, target) in enumerate(
            [
                (inner, inner_v),
                (energies, energies_v),
                (surface, surface_v),
                (coef, coef_v),
                (pattern, pattern_v),
                (thresholds, thresholds_v),
                (outer.at[:, :, pl.ds(0, 128)], corner_v),
            ]
        )
    ]
    for copy in copies:
        copy.start()
    fetched = fetch(dipole, dipole_ref, dipole_arrivals)
    for copy in copies:
        copy.wait()
    position = where[1] * 128 + rows_of(1, (1, 128))
    for l in range(LB):
        live = jnp.where(position < sizes[l], 1.0, 0.0).astype(F32)
        levels_ref[8 + l : 9 + l, :] = live
        levels_ref[12 + l : 13 + l, :] = live
        surface_ref[l * CH : (l + 1) * CH, :] = surface_v[l]
    levels_ref[0:4, :] = energies_v[...]
    levels_ref[4:8, :] = energies_v[...]
    surface_ref[OWN:256, :] = jnp.zeros((256 - OWN, 128), F32)
    level_lane = jnp.concatenate([thresholds_v[...], jnp.zeros((1, 256 - OWN), F32)], axis=1)
    strip_levels_ref[...] = level_lane
    column = jnp.broadcast_to(level_lane, (128, 256)).T[:OWN]
    pack_ref[...] = jnp.where(rows_of(1, (OWN, 128)) == CH, column, 0.0)
    for l in range(LB):
        block = coef_v[l] * pattern_v[l].astype(F32)
        if l == LB - 1:
            block = block * jnp.where(where[2] != 0, 1.0, 0.0).astype(F32)
        pack_ref[l * CH : (l + 1) * CH, 0:CH] = block
    for part in range(2):
        corner = jnp.concatenate([corner_v[part], jnp.zeros((256 - OWN, 128), F32)], axis=0).T[:PTS]
        fs_ref[part * PTS : (part + 1) * PTS, :] = corner
    fs_ref[32:64, :] = jnp.zeros((32, 256), F32)
    c = jnp.concatenate([inner_v[0], inner_v[1]], axis=0) * levels_ref[8:16, :]
    cs_ref[0:8, :] = c
    cs_ref[8:16, :] = c
    a_ref[64:EDGE, :] = pack_ref[...]
    b_ref[64:EDGE, :] = pack_ref[...]
    emit(where[0], c, fs_ref[0:32, :], dipole_ref, surface_ref, q_ref, a_ref, b_ref, up_ref, down_ref, fetched)


def received(parity, a, b):
    flag = jnp.full(a.shape, parity, jnp.int32) == 0
    return jnp.where(flag, b, a), jnp.where(flag, a, b)


def assemble_kernel(first, where, *refs):
    if first:
        q, a, b, strip, out_ref, low_ref, high_ref, ghost_ref = refs
    else:
        q, a, b, out_ref, ghost_ref = refs
    up, down = received(where[0], a[...], b[...])
    out_ref[:, 0:24, :] = q[...]
    for s in range(16):
        out_ref[s, 3:4, :] = down[0:1]
        out_ref[s, 7:8, :] = down[4:5]
        out_ref[s, 8:9, :] = up[s : s + 1]
        out_ref[s, 12:13, :] = up[16 + s : 17 + s]
    ghost = up[32:64] + down[32:64]
    if first:
        whole = strip[0:32, :]
        near, far = whole[:, :128], whole[:, 128:] + ghost
        for s in range(16):
            for at, value in ((24, near), (40, far)):
                out_ref[s, at : at + 8, :] = value[0:8]
                out_ref[s, at + 8 : at + 16, :] = value[PTS : PTS + 8]
        ghost_ref[...] = ghost
        low_ref[...] = up[64:EDGE]
        high_ref[...] = down[64:EDGE]
    else:
        ghost_ref[...] = ghost


def advance(copies, first, last_power, factor, field, dipole, surface, levels, pairs, thresholds, arrived, cs, fs, ghost):
    sums = []
    for l in range(LB):
        if copies is not None:
            copies[l].wait()

        def body(s, carry):
            tile = dipole[l, :, pl.ds(pl.multiple_of(s * 128, 128), 128)]
            return (
                carry[0] + tile * arrived[s, l : l + 1, :],
                carry[1] + tile * arrived[s, 4 + l : 5 + l, :],
            )

        zero = jnp.zeros((128, 128), F32)
        re, im = lax.fori_loop(0, 16, body, (zero, zero), unroll=16)
        sums.append((jnp.sum(re.T, axis=0, keepdims=True), jnp.sum(im.T, axis=0, keepdims=True)))
    forward = jnp.concatenate([a for a, _ in sums] + [b for _, b in sums], axis=0)
    backward = arrived[0, 8:16, :]
    tail = arrived[0, 16:24, :]
    for s in range(1, 16):
        backward = backward + arrived[s, 8:16, :]
        tail = tail + arrived[s, 16:24, :]
    lanes = rows_of(1, (2 * PTS, 256))
    own = fs[0:32, :]
    strip_sum = fs[32:64, :]
    near, far = own[:, :128], own[:, 128:] + ghost[...]
    if first:
        near = jnp.concatenate(
            [arrived[0, 24:32, :], near[8:16], arrived[0, 32:40, :], near[PTS + 8 : PTS + 16]], axis=0
        )
        far = jnp.concatenate([arrived[0, 40:48, :], far[8:16], arrived[0, 48:56, :], far[PTS + 8 : PTS + 16]], axis=0)
    whole = jnp.concatenate([near, far], axis=1)
    if first:
        own = jnp.where(lanes < OWN, whole, 0.0)
        strip_sum = own
    c = cs[0:8, :]
    c_sum = cs[8:16, :]
    edge = jnp.concatenate(
        [jnp.broadcast_to(own[0:1], (4, 256)), jnp.broadcast_to(own[PTS : PTS + 1], (4, 256))], axis=0
    )
    surf = jnp.dot(edge * block_mask(), surface[...], precision=HIGHEST, preferred_element_type=F32)
    image = levels[8:16, :] * (levels[0:8, :] * c + field * (forward + backward) - kinetic_scale * surf)
    c_new = jnp.concatenate([factor * image[4:8], -factor * image[0:4]], axis=0)
    coupled = lax.dot_general(whole, pairs[...], NT, precision=HIGHEST, preferred_element_type=F32)
    b_re = jnp.concatenate([tail[0:1], tail[1:2]], axis=1)
    b_im = jnp.concatenate([tail[2:3], tail[3:4]], axis=1)
    points = rows_of(0, (2 * PTS, 256))
    left = pltpu.roll(own, 1, 0)
    left = jnp.where(points == 0, b_re, jnp.where(points == PTS, b_im, left))
    right = pltpu.roll(own, 2 * PTS - 1, 0)
    right = jnp.where((points == PTS - 1) | (points == 2 * PTS - 1), 0.0, right)
    grid = kinetic_scale * (2.0 * own - left - right) + thresholds[...] * own + field * coupled
    grid = jnp.where(lanes < OWN, grid, 0.0)
    f_new = jnp.concatenate([factor * grid[PTS:], -factor * grid[:PTS]], axis=0)
    c_sum = c_sum + c_new
    strip_sum = strip_sum + f_new
    if last_power:
        return c_sum, c_sum, strip_sum, strip_sum
    return c_new, c_sum, f_new, strip_sum


def middle_kernel(away, first, last_power, factor, step, where, strengths, *refs):
    dipole, surface, levels, pairs, thresholds, arrived, cs = refs[:7]
    rest = refs[7:]
    copies = None
    if away:
        copies = fetch(dipole, *rest[-2:])
        dipole, rest = rest[-2], rest[:-2]
    fs, ghost = rest[:2]
    rest = rest[2:]
    cs_ref, fs_ref, q_ref, a_ref, b_ref, up_ref, down_ref = rest
    c, c_sum, f, f_sum = advance(
        copies,
        first,
        last_power,
        factor,
        strengths[step],
        dipole,
        surface,
        levels,
        pairs,
        thresholds,
        arrived,
        cs,
        fs,
        ghost,
    )
    cs_ref[0:8, :] = c
    cs_ref[8:16, :] = c_sum
    fs_ref[0:32, :] = f
    fs_ref[32:64, :] = f_sum
    emit(where[0], c, f, dipole, surface, q_ref, a_ref, b_ref, up_ref, down_ref)


def last_kernel(away, factor, step, where, strengths, *refs):
    dipole, rest, copies = refs[0], refs[1:], None
    if away:
        copies = fetch(dipole, *rest[-2:])
        dipole, rest = rest[-2], rest[:-2]
    *given, bulk, c_ref, out_ref = rest
    _, c_sum, _, f_sum = advance(copies, False, True, factor, strengths[step], dipole, *given)
    c_ref[...] = c_sum
    lanes = rows_of(1, (OWN, 128))
    low = jnp.full((OWN, 128), where[1], jnp.int32) == 0
    fixed = (lanes < HALO) & low
    for part in range(2):
        corner = f_sum[part * PTS : (part + 1) * PTS]
        corner = jnp.concatenate([corner, jnp.zeros((128 - PTS, 256), F32)], axis=0).T[:OWN]
        base = part * WIDTH
        out_ref[part, :, 0:128] = jnp.where(fixed, corner, bulk[:, base : base + 128])
        out_ref[part, :, 128:512] = bulk[:, base + 128 : base + 512]


def window_kernel(where, outer, by_even, by_odd, out_ref):
    lanes = rows_of(1, (OWN, 128))
    flag = jnp.full((OWN, 128), where[1] % 2, jnp.int32) == 0
    for part in range(2):
        base = part * WIDTH
        right = jnp.where(flag, by_even[part], by_odd[part])
        left = jnp.where(flag, by_odd[part], by_even[part])
        out_ref[:, base : base + 512] = outer[part]
        out_ref[:, base + 512 : base + WIDTH] = jnp.where(
            lanes < HALO, right, jnp.where(lanes >= 128 - HALO, left, 0.0)
        )


def bulk_kernel(step, powers, where, strengths, *refs):
    begin, end = powers[0] == 1, powers[-1] == ORDER
    if begin:
        own, by_swap, by_chip, couplings, pack = refs[:5]
        refs = refs[5:]
    else:
        given, given_sum, couplings, pack = refs[:4]
        refs = refs[4:]
    if end:
        sum_ref, spare, other = refs
    else:
        other, sum_ref, spare = refs
    source, target = (spare, other) if len(powers) % 2 else (other, spare)
    if begin:
        source[160:320, :] = own[...]
        sum_ref[...] = own[...]

        @pl.when(where[0] == 0)
        def _():
            source[0:160, :] = by_chip[...]
            source[320:480, :] = by_swap[...]

        @pl.when(where[0] != 0)
        def _():
            source[0:160, :] = by_swap[...]
            source[320:480, :] = by_chip[...]
    else:
        source[...] = given[...]
        sum_ref[...] = given_sum[...]
    field = strengths[step]
    lanes = rows_of(1, (1, WIDTH))
    past = (lanes >= 512) & (lanes < 512 + 64) & (jnp.full((1, WIDTH), where[1], jnp.int32) == where[3])
    keep = jnp.where(past, 0.0, 1.0).astype(F32)
    for power in powers:
        factor = time_step / power
        ring = CH * power
        groups = [(160, 320, 120, 360)]
        if power < ORDER:
            groups += [(ring, 160, ring - CH, 200), (320, 480 - ring, 280, 480 - ring + CH)]
        for out0, out1, in0, in1 in groups:
            matrix = couplings[out0:out1, in0:in1]
            m_hi = matrix.astype(BF16)
            m_lo = (matrix - m_hi.astype(F32)).astype(BF16)
            images = []
            for part in range(2):
                cols = slice(part * WIDTH, (part + 1) * WIDTH)
                f = source[in0:in1, cols]
                f_hi = f.astype(BF16)
                f_lo = (f - f_hi.astype(F32)).astype(BF16)
                coupled = jnp.dot(m_hi, f_hi, preferred_element_type=F32)
                coupled = coupled + jnp.dot(m_hi, f_lo, preferred_element_type=F32)
                coupled = coupled + jnp.dot(m_lo, f_hi, preferred_element_type=F32)
                mine = source[out0:out1, cols]
                left = pltpu.roll(mine, 1, 1)
                right = pltpu.roll(mine, WIDTH - 1, 1)
                level = pack[out0:out1, CH : CH + 1]
                image = kinetic_scale * (2.0 * mine - left - right) + level * mine + field * coupled
                images.append(image * keep)
            new_re = factor * images[1]
            new_im = -factor * images[0]
            if power < ORDER:
                target[out0:out1, 0:WIDTH] = new_re
                target[out0:out1, WIDTH : 2 * WIDTH] = new_im
            if out0 == 160:
                sum_ref[:, 0:WIDTH] = sum_ref[:, 0:WIDTH] + new_re
                sum_ref[:, WIDTH : 2 * WIDTH] = sum_ref[:, WIDTH : 2 * WIDTH] + new_im
        if not end and power == powers[-1]:
            target[0:ring, :] = jnp.zeros((ring, 2 * WIDTH), F32)
            target[480 - ring : 480, :] = jnp.zeros((ring, 2 * WIDTH), F32)
        source, target = target, source


def pair_up(lower, upper):
    return [(a, b) for a, b in zip(lower, upper)] + [(b, a) for a, b in zip(lower, upper)]


def couplings_kernel(low, own, high, couplings_ref, pairs_ref, pack_ref):
    pack_ref[0:OWN, :] = low[...]
    pack_ref[OWN : 2 * OWN, :] = own[...]
    pack_ref[2 * OWN :, :] = high[...]
    couplings_ref[...] = jnp.zeros((3 * OWN, 3 * OWN), F32)
    pairs_ref[...] = jnp.zeros((256, 256), F32)
    for w in range(3 * LB - 1):
        here, there = slice(w * CH, (w + 1) * CH), slice((w + 1) * CH, (w + 2) * CH)
        block = pack_ref[here, 0:CH]
        couplings_ref[here, there] = block
        couplings_ref[there, here] = block.T
        n = w - LB
        if 0 <= n < LB:
            pairs_ref[n * CH : (n + 1) * CH, (n + 1) * CH : (n + 2) * CH] = block
        if -1 <= n < LB - 1:
            at = n * CH if n >= 0 else OWN + CH
            pairs_ref[(n + 1) * CH : (n + 2) * CH, at : at + CH] = block.T


def after(values, token):
    return lax.optimization_barrier((values, token))[0]


WINDOWS = {3: (0, (1, 2, 3, 4)), 7: (1, (1, 2, 3, 4))}
AWAY = (0, 1, 3, 4, 7)


def local(
    inner_state,
    outer_state,
    energies,
    dipole,
    surface,
    thresholds,
    coupling_coef,
    coupling_pattern,
    block_sizes,
    field_strength,
):
    inner_count = lax.axis_size("inner")
    outer_count = lax.axis_size("outer")
    i = lax.axis_index("inner")
    o = lax.axis_index("outer")
    parity = i % 2
    has_next = jnp.where(i < inner_count - 1, 1, 0)
    where = jnp.stack([parity, o, has_next, outer_count - 1]).astype(jnp.int32)
    swap = pair_up(range(0, inner_count, 2), range(1, inner_count, 2))
    chips = pair_up(range(1, inner_count - 1, 2), range(2, inner_count, 2))
    even = pair_up(range(0, outer_count, 2), range(1, outer_count, 2))
    odd = pair_up(range(1, outer_count - 1, 2), range(2, outer_count, 2))

    edges = (pltpu.VMEM((64, 128), F32), pltpu.VMEM((64, 128), F32))
    big = pltpu.VMEM((3 * OWN, 2 * WIDTH), F32)
    cs, fs, q, to_a, to_b, levels, surface_all, pack, strip_levels = pl.pallas_call(
        first_kernel,
        out_shape=[
            sds(16, 128),
            sds(64, 256),
            sds(16, 24, 128),
            sds(EDGE, 128),
            sds(EDGE, 128),
            sds(16, 128),
            sds(256, 128),
            sds(OWN, 128),
            sds(1, 256),
        ],
        in_specs=[SM, SM] + [HBM] * 8,
        out_specs=[VM] * 9,
        scratch_shapes=[
            *edges,
            *DIPOLE,
            pltpu.VMEM((2, LB, 128), F32),
            pltpu.VMEM((LB, 128), F32),
            pltpu.VMEM((LB, CH, 128), F32),
            pltpu.VMEM((LB, CH, CH), F32),
            pltpu.VMEM((LB, CH, CH), jnp.int32),
            pltpu.VMEM((1, OWN), F32),
            pltpu.VMEM((2, OWN, 128), F32),
            pltpu.SemaphoreType.DMA((7,)),
        ],
        compiler_params=pltpu.CompilerParams(vmem_limit_bytes=20 << 20),
    )(
        where,
        block_sizes,
        *(
            pltpu.with_memory_space_constraint(x, pltpu.HBM)
            for x in (
                inner_state,
                energies,
                surface,
                coupling_coef,
                coupling_pattern,
                thresholds.reshape(1, OWN),
                dipole,
                outer_state,
            )
        ),
    )

    for index in range(STEPS * ORDER):
        step, power = index // ORDER, index % ORDER + 1
        first = index == 0
        factor = time_step / power
        from_a = lax.ppermute(to_a, "inner", swap)
        from_b = lax.ppermute(to_b, "inner", chips)
        if first:
            q, low_pack, high_pack, ghost = call(
                functools.partial(assemble_kernel, True), [sds(16, 56, 128), sds(OWN, 128), sds(OWN, 128), sds(32, 128)]
            )(where, q, from_a, from_b, fs)
        else:
            q, ghost = call(functools.partial(assemble_kernel, False), [sds(16, 24, 128), sds(32, 128)])(
                where, q, from_a, from_b
            )
        arrived = lax.all_to_all(q, "outer", split_axis=0, concat_axis=0, tiled=True)
        token = q[0, 0, 0]

        if index == 0:
            low_pack, high_pack = after((low_pack, high_pack), token)
            couplings, pairs, packs = call(
                couplings_kernel, [sds(3 * OWN, 3 * OWN), sds(256, 256), sds(3 * OWN, 128)], smem=0
            )(low_pack, pack, high_pack)
            tail, head = after((outer_state[:, :, 384:], outer_state[:, :, :128]), token)
            is_odd = (o % 2) == 1
            by_even = lax.ppermute(jnp.where(is_odd, head, tail), "outer", even)
            by_odd = lax.ppermute(jnp.where(is_odd, tail, head), "outer", odd)
            by_even, by_odd, arrived = lax.optimization_barrier((by_even, by_odd, arrived))
        if index == 1:
            by_even, by_odd = after((by_even, by_odd), token)
            (bulk,) = call(window_kernel, [sds(OWN, 2 * WIDTH)])(where, outer_state, by_even, by_odd)
            bulk, arrived = lax.optimization_barrier((bulk, arrived))
        if index in WINDOWS:
            at, powers = WINDOWS[index]
            begin, end = powers[0] == 1, powers[-1] == ORDER
            given = (bulk, by_swap, by_chip) if begin else (window, total)
            given = after(given, token)
            outs = [sds(OWN, 2 * WIDTH)] if end else [sds(3 * OWN, 2 * WIDTH), sds(OWN, 2 * WIDTH)]
            result = call(
                functools.partial(bulk_kernel, at, powers), outs, smem=2, scratch=(big, big) if end else (big,)
            )(where, field_strength, *given, couplings, packs)
            if end:
                bulk, arrived = lax.optimization_barrier((result[0], arrived))
            else:
                window, total, arrived = lax.optimization_barrier((*result, arrived))
        if index in (1, 4):
            bulk = after(bulk, token)
            by_swap = lax.ppermute(bulk, "inner", swap)
            by_chip = lax.ppermute(bulk, "inner", chips)

        away = index in AWAY
        given = (where, field_strength, pltpu.with_memory_space_constraint(dipole, pltpu.HBM) if away else dipole, surface_all, levels, pairs, strip_levels, arrived, cs, fs, ghost)
        if index < STEPS * ORDER - 1:
            cs, fs, q, to_a, to_b = call(
                functools.partial(middle_kernel, away, first, power == ORDER, factor, step),
                [sds(16, 128), sds(64, 256), sds(16, 24, 128), sds(64, 128), sds(64, 128)],
                smem=2,
                scratch=edges + DIPOLE if away else edges,
                hbm=(2,) if away else (),
            )(*given)
        else:
            c, grid = call(
                functools.partial(last_kernel, away, factor, step),
                [sds(8, 128), sds(2, OWN, 512)],
                smem=2,
                scratch=DIPOLE if away else (),
                hbm=(2,) if away else (),
            )(*given, bulk)
    return c.reshape(2, LB, 128), grid


def solution(mesh):
    placed = (
        P(None, "inner", "outer"),
        P(None, "inner", "outer"),
        P("inner", "outer"),
        P("inner", "outer", None),
        P("inner", None, "outer"),
        P("inner"),
        P("inner", None, None),
        P("inner", None, None),
        P("inner"),
        P(),
    )
    return jax.shard_map(
        local,
        mesh=mesh,
        in_specs=placed,
        out_specs=(P(None, "inner", "outer"), P(None, "inner", "outer")),
        check_vma=False,
    )
```

time: 233 us -> 203 us (0.87)
  blocking collectives: 60.3 us -> 35.3 us
  local copies, waits for them, and re-layouts: 24.1 us -> 6.95 us
  starting transfers between devices: 55.6 us -> 67.6 us
  waiting for transfers between devices: 25.1 us -> 33.4 us
  other arithmetic: 6.24 us -> 0.11 us
    all_to_all x5 -> x3, blocking collectives: 60.3 us -> 35.3 us  [local(): lax.all_to_all(q, 'outer', split_axis=0, concat_axis=0, tiled=True)]
    all_to_all x3 -> x5, starting transfers between devices: 18.5 us -> 31.5 us  [local(): lax.all_to_all(q, 'outer', split_axis=0, concat_axis=0, tiled=True)]
    all_to_all x3 -> x5, waiting for transfers between devices: 0.01 us -> 8.14 us  [local(): lax.all_to_all(q, 'outer', split_axis=0, concat_axis=0, tiled=True)]
    unnamed x28 -> x32, local copies, waits for them, and re-layouts: 14.7 us -> 6.93 us
    add x1 -> x0, local copies, waits for them, and re-layouts: 3.34 us -> none  [coupling_matrix(): jnp.where(there == here + 1, up, 0.0)]
    ppermute x8, waiting for transfers between devices: 13.7 us -> 16.8 us  [local(): from_b = lax.ppermute(to_b, 'inner', chips)]
    slice x5 -> x0, local copies, waits for them, and re-layouts: 3.13 us -> none  [the longest x2 2.93 us: local(): own = couplings[OWN:2 * OWN]]
    select_n x3 -> x0, other arithmetic: 3.03 us -> none  [the longest x2 3.01 us: local(): high = jnp.where(is_upper, by_chip, by_swap)]
  transfers between devices with their start and end apart: 25 -> 27, of which waited for: 8 -> 11; matrix products, arithmetic and copies ran while one was open for 5% -> 0% of each run, Pallas kernels for 22% -> 18%
where the time goes in v2:
time: 203 us; the launch traced here: 199 us
  starting transfers between devices  67.6 us (33%)
  Pallas kernels  54.7 us (27%)
  blocking collectives  35.3 us (17%)
  waiting for transfers between devices  33.4 us (16%)
  local copies, waits for them, and re-layouts  6.95 us (3%)
    pallas_call x20, Pallas kernels, run(): pl.pallas_call(kernel, out_shape=outs, in_specs=[SM] * smem + [HBM if n i...  51 us
    all_to_all x3, blocking collectives, local(): lax.all_to_all(q, 'outer', split_axis=0, concat_axis=0, tiled=True)  35.3 us
    all_to_all x5, starting transfers between devices, local(): lax.all_to_all(q, 'outer', split_axis=0, concat_axis=0, tiled=True)  31.5 us
    ppermute x8, starting transfers between devices, local(): from_b = lax.ppermute(to_b, 'inner', chips)  26 us
    ppermute x8, waiting for transfers between devices, local(): from_b = lax.ppermute(to_b, 'inner', chips)  16.8 us
    ppermute x1, waiting for transfers between devices, local(): by_odd = lax.ppermute(jnp.where(is_odd, tail, head), 'outer', odd)  8.43 us
    all_to_all x5, waiting for transfers between devices, local(): lax.all_to_all(q, 'outer', split_axis=0, concat_axis=0, tiled=True)  8.14 us
    unnamed x32, local copies, waits for them, and re-layouts  6.93 us
  transfers between devices with their start and end apart: 27, of which 11 were waited for; matrix products, arithmetic and copies ran while one was open for 0% of the time, Pallas kernels for 18%

profile of v2, /device:TPU:88, one launch (start us, length us, event | category | flops | bytes accessed | tf_op | source)
XLA Modules:
  0.0 199.5 jit_solution(14426684886875082853)
XLA Ops:
  0.7 0.7 copy-done.15
  1.5 3.7 %shard_map.113 = (f32[16,128]{1,0:T(8,128)S(1)}, f32[64,256]{1,0:T(8,128)S(1)}, f32[16,24,128]{2,1,0:T(8,128)S(1)}, f32[224,128]{1,0:T(8,128)S(1)}, f32[224,128]...) custom-call(s32[4]{0:T(128)S(1)} %pad_add_fusion.where, ...), custom_call_target="tpu_custom_call" | custom-call | tf_op jit(solution)/shard_map/pallas_call | solution.py:496
  5.2 2.1 %collective-permute-start.1 = (f32[224,128]{1,0:T(8,128)S(1)}, f32[224,128]{1,0:T(8,128)S(1)}, u32[]{:S(2)}, u32[]{:S(2)}) collective-permute-start(f32[224,128]{1,0:T(8,128)S(1)} %get-tuple-element.95), channel_id=1, source_target_pairs={{16,32},{48,64},{80,96},{32,16},{64,48},{96,80},{17,33},{49,65},{8... | collective-permute-start | bytes 344072 | tf_op jit(solution)/shard_map/ppermute | solution.py:547
  7.4 4.0 %collective-permute-done.1.refs_2_ = f32[224,128]{1,0:T(8,128)S(1)} collective-permute-done((f32[224,128]{1,0:T(8,128)S(1)}, f32[224,128]{1,0:T(8,128)S(1)}, u32[]{:S(2)}, u32[]{:S(2)}) %collective-permute-start.1) | collective-permute-done | bytes 114720 | tf_op jit(solution)/shard_map/ppermute | solution.py:547
  11.3 1.4 shard_map.114
  12.7 7.2 %all-to-all-start = ((f32[16,56,128]{2,1,0:T(8,128)}), f32[16,56,128]{2,1,0:T(8,128)S(1)}, u32[]{:S(2)}, u32[]{:S(2)}) async-start(f32[16,56,128]{2,1,0:T(8,128)} %get-tuple-element.99), calls=%async_computation | async-start | bytes 917504 | tf_op jit(solution)/shard_map/all_to_all | solution.py:556
  19.9 3.4 %collective-permute-start.3 = (f32[2,160,128]{2,1,0:T(8,128)S(1)}, f32[2,160,128]{2,1,0:T(8,128)S(1)}, u32[]{:S(2)}, u32[]{:S(2)}) collective-permute-start(f32[2,160,128]{2,1,0:T(8,128)S(1)} %get-tuple-element.182), channel_id=1, source_target_pairs={{1,2},{3,4},{5,6},{7,8},{9,10},{11,12},{13,14},{2,1},{4,3},{6,5},{... | collective-permute-start | bytes 491528 | tf_op jit(solution)/shard_map/ppermute | solution.py:567
  23.4 0.3 shard_map.115
  23.7 8.4 %collective-permute-done.3.by_odd = f32[2,160,128]{2,1,0:T(8,128)S(1)} collective-permute-done((f32[2,160,128]{2,1,0:T(8,128)S(1)}, f32[2,160,128]{2,1,0:T(8,128)S(1)}, u32[]{:S(2)}, u32[]{:S(2)}) %collective-permute-start.3) | collective-permute-done | bytes 163872 | tf_op jit(solution)/shard_map/ppermute | solution.py:567
  32.2 3.8 %shard_map.116 = (f32[16,128]{1,0:T(8,128)S(1)}, f32[64,256]{1,0:T(8,128)S(1)}, f32[16,24,128]{2,1,0:T(8,128)S(1)}, f32[64,128]{1,0:T(8,128)S(1)}, f32[64,128]{1,0:T(8,128)S(1)}) custom-call(s32[4]{0:T(128)S(1)} %pad_add_fusion.where, f32[2]{0:T(128)S(1)} %copy-done.9, f32[4,128,2048]{2,1,0:T(8,128)} %refs_0_.15, f32[256,128]{1,0:T(8,128)S(1)} %get-tuple-element.91.refs_1_, ...), custom_call_target="tpu_custom_call" | custom-call | tf_op jit(solution)/shard_map/pallas_call | solution.py:39
  36.1 2.1 %collective-permute-start.5 = (f32[64,128]{1,0:T(8,128)S(1)}, f32[64,128]{1,0:T(8,128)S(1)}, u32[]{:S(2)}, u32[]{:S(2)}) collective-permute-start(f32[64,128]{1,0:T(8,128)S(1)} %get-tuple-element.114), channel_id=1, source_target_pairs={{16,32},{48,64},{80,96},{32,16},{64,48},{96,80},{17,33},{49,65},{8... | collective-permute-start | bytes 98312 | tf_op jit(solution)/shard_map/ppermute | solution.py:547
  38.2 3.1 %collective-permute-done.5.refs_2_ = f32[64,128]{1,0:T(8,128)S(1)} collective-permute-done((f32[64,128]{1,0:T(8,128)S(1)}, f32[64,128]{1,0:T(8,128)S(1)}, u32[]{:S(2)}, u32[]{:S(2)}) %collective-permute-start.5) | collective-permute-done | bytes 32800 | tf_op jit(solution)/shard_map/ppermute | solution.py:547
  41.4 1.2 shard_map.117
  42.6 5.8 %all-to-all-start.1 = ((f32[16,24,128]{2,1,0:T(8,128)}), f32[16,24,128]{2,1,0:T(8,128)S(1)}, u32[]{:S(2)}, u32[]{:S(2)}) async-start(f32[16,24,128]{2,1,0:T(8,128)} %get-tuple-element.115), calls=%async_computation.1 | async-start | bytes 393216 | tf_op jit(solution)/shard_map/all_to_all | solution.py:556
  48.4 0.9 copy-done.8
  49.3 0.6 shard_map.118.refs_0_
  49.9 4.9 %all-to-all-done.1.refs_5_ = f32[16,24,128]{2,1,0:T(8,128)S(1)} async-done(((f32[16,24,128]{2,1,0:T(8,128)}), f32[16,24,128]{2,1,0:T(8,128)S(1)}, u32[]{:S(2)}, u32[]{:S(2)}) %all-to-all-start.1) | async-done | bytes 196640 | tf_op jit(solution)/shard_map/all_to_all | solution.py:556
  54.8 2.2 %collective-permute-start.7 = (f32[160,1280]{1,0:T(8,128)S(1)}, f32[160,1280]{1,0:T(8,128)}, u32[]{:S(2)}, u32[]{:S(2)}) collective-permute-start(f32[160,1280]{1,0:T(8,128)S(1)} %shard_map.118.refs_0_), channel_id=1, source_target_pairs={{16,32},{48,64},{80,96},{32,16},{64,48},{96,80},{17,33},{49,65},{8... | collective-permute-start | bytes 2457608 | tf_op jit(solution)/shard_map/ppermute | solution.py:589
  57.0 0.3 collective-permute-start.6
  57.3 0.7 copy-done.10
  57.9 0.7 copy-done.12
  58.7 0.7 copy-done.14
  59.3 3.8 %shard_map.120 = (f32[16,128]{1,0:T(8,128)S(1)}, f32[64,256]{1,0:T(8,128)S(1)}, f32[16,24,128]{2,1,0:T(8,128)S(1)}, f32[64,128]{1,0:T(8,128)S(1)}, f32[64,128]{1,0:T(8,128)S(1)}) custom-call(s32[4]{0:T(128)S(1)} %pad_add_fusion.where, f32[2]{0:T(128)S(1)} %copy-done.10, f32[4,128,2048]{2,1,0:T(8,128)} %refs_0_.15, f32[256,128]{1,0:T(8,128)S(1)} %get-tuple-element.91.refs_1_, ...), custom_call_target="tpu_custom_call" | custom-call | tf_op jit(solution)/shard_map/pallas_call | solution.py:39
  63.2 0.4 collective-permute-start.8
  63.6 3.6 %collective-permute-start.9 = (f32[64,128]{1,0:T(8,128)S(1)}, f32[64,128]{1,0:T(8,128)S(1)}, u32[]{:S(2)}, u32[]{:S(2)}) collective-permute-start(f32[64,128]{1,0:T(8,128)S(1)} %get-tuple-element.131), channel_id=1, source_target_pairs={{16,32},{48,64},{80,96},{32,16},{64,48},{96,80},{17,33},{49,65},{8... | collective-permute-start | bytes 98312 | tf_op jit(solution)/shard_map/ppermute | solution.py:547
  67.2 1.9 collective-permute-done.9.refs_2_
  69.1 0.6 shard_map.121
  69.6 11.6 %all_to_all.40.refs_5_ = f32[16,24,128]{2,1,0:T(8,128)S(1)} all-to-all(f32[16,24,128]{2,1,0:T(8,128)S(1)} %get-tuple-element.132), channel_id=1, replica_groups=mesh['inner'=8,'outer'=16] {'outer'}, dimensions={0} | all-to-all | bytes 393216 | tf_op jit(solution)/shard_map/all_to_all | solution.py:556
  81.2 2.4 %shard_map.122 = (f32[16,128]{1,0:T(8,128)S(1)}, f32[64,256]{1,0:T(8,128)S(1)}, f32[16,24,128]{2,1,0:T(8,128)S(1)}, f32[64,128]{1,0:T(8,128)S(1)}, f32[64,128]{1,0:T(8,128)S(1)}) custom-call(s32[4]{0:T(128)S(1)} %pad_add_fusion.where, f32[2]{0:T(128)S(1)} %copy-done.10, f32[4,128,2048]{2,1,0:T(8,128)S(1)} %copy-done, ...), custom_call_target="tpu_custom_call" | custom-call | tf_op jit(solution)/shard_map/pallas_call | solution.py:39
  83.6 0.1 collective-permute-start.10
  83.7 3.7 %collective-permute-start.11 = (f32[64,128]{1,0:T(8,128)S(1)}, f32[64,128]{1,0:T(8,128)S(1)}, u32[]{:S(2)}, u32[]{:S(2)}) collective-permute-start(f32[64,128]{1,0:T(8,128)S(1)} %get-tuple-element.138), channel_id=1, source_target_pairs={{16,32},{48,64},{80,96},{32,16},{64,48},{96,80},{17,33},{49,65},{8... | collective-permute-start | bytes 98312 | tf_op jit(solution)/shard_map/ppermute | solution.py:547
  87.4 1.6 collective-permute-done.11.refs_2_
  89.0 1.2 shard_map.123
  90.2 5.7 %all-to-all-start.3 = ((f32[16,24,128]{2,1,0:T(8,128)}), f32[16,24,128]{2,1,0:T(8,128)S(1)}, u32[]{:S(2)}, u32[]{:S(2)}) async-start(f32[16,24,128]{2,1,0:T(8,128)} %get-tuple-element.139), calls=%async_computation.3 | async-start | bytes 393216 | tf_op jit(solution)/shard_map/all_to_all | solution.py:556
  95.9 1.1 copy-done.4
  97.0 7.7 %shard_map.119.refs_0_ = f32[160,1280]{1,0:T(8,128)S(1)} custom-call(s32[4]{0:T(128)S(1)} %pad_add_fusion.where, f32[2]{0:T(128)S(1)} %copy-done.10, f32[160,1280]{1,0:T(8,128)S(1)} %copy-done.4, f32[160,1280]{1,0:T(8,128)} %collective-permute-done.6.refs_1_, f32[160,1280]{1,0:T(8,128)} %collective-permute-done.7.refs_2_, ...), custom_call_target="tpu_custom_call" | custom-call | tf_op jit(solution)/shard_map/pallas_call | solution.py:39
  104.7 3.8 %shard_map.125 = (f32[16,128]{1,0:T(8,128)S(1)}, f32[64,256]{1,0:T(8,128)S(1)}, f32[16,24,128]{2,1,0:T(8,128)S(1)}, f32[64,128]{1,0:T(8,128)S(1)}, f32[64,128]{1,0:T(8,128)S(1)}) custom-call(s32[4]{0:T(128)S(1)} %pad_add_fusion.where, f32[2]{0:T(128)S(1)} %copy-done.10, f32[4,128,2048]{2,1,0:T(8,128)} %refs_0_.15, f32[256,128]{1,0:T(8,128)S(1)} %get-tuple-element.91.refs_1_, ...), custom_call_target="tpu_custom_call" | custom-call | tf_op jit(solution)/shard_map/pallas_call | solution.py:39
  108.5 0.1 collective-permute-start.14
  108.6 3.6 %collective-permute-start.15 = (f32[64,128]{1,0:T(8,128)S(1)}, f32[64,128]{1,0:T(8,128)S(1)}, u32[]{:S(2)}, u32[]{:S(2)}) collective-permute-start(f32[64,128]{1,0:T(8,128)S(1)} %get-tuple-element.150), channel_id=1, source_target_pairs={{16,32},{48,64},{80,96},{32,16},{64,48},{96,80},{17,33},{49,65},{8... | collective-permute-start | bytes 98312 | tf_op jit(solution)/shard_map/ppermute | solution.py:547
  112.3 1.6 collective-permute-done.15.refs_2_
  113.9 1.2 shard_map.126
  115.1 7.3 %all-to-all-start.4 = ((f32[16,24,128]{2,1,0:T(8,128)}), f32[16,24,128]{2,1,0:T(8,128)S(1)}, u32[]{:S(2)}, u32[]{:S(2)}) async-start(f32[16,24,128]{2,1,0:T(8,128)} %get-tuple-element.151), calls=%async_computation.4 | async-start | bytes 393216 | tf_op jit(solution)/shard_map/all_to_all | solution.py:556
  122.4 3.0 %collective-permute-start.13 = (f32[160,1280]{1,0:T(8,128)S(1)}, f32[160,1280]{1,0:T(8,128)}, u32[]{:S(2)}, u32[]{:S(2)}) collective-permute-start(f32[160,1280]{1,0:T(8,128)S(1)} %shard_map.119.refs_0_), channel_id=1, source_target_pairs={{16,32},{48,64},{80,96},{32,16},{64,48},{96,80},{17,33},{49,65},{8... | collective-permute-start | bytes 2457608 | tf_op jit(solution)/shard_map/ppermute | solution.py:589
  125.4 0.1 collective-permute-start.12
  125.5 3.2 %all-to-all-done.4.refs_5_ = f32[16,24,128]{2,1,0:T(8,128)S(1)} async-done(((f32[16,24,128]{2,1,0:T(8,128)}), f32[16,24,128]{2,1,0:T(8,128)S(1)}, u32[]{:S(2)}, u32[]{:S(2)}) %all-to-all-start.4) | async-done | bytes 196640 | tf_op jit(solution)/shard_map/all_to_all | solution.py:556
  128.8 4.1 %shard_map.127 = (f32[16,128]{1,0:T(8,128)S(1)}, f32[64,256]{1,0:T(8,128)S(1)}, f32[16,24,128]{2,1,0:T(8,128)S(1)}, f32[64,128]{1,0:T(8,128)S(1)}, f32[64,128]{1,0:T(8,128)S(1)}) custom-call(s32[4]{0:T(128)S(1)} %pad_add_fusion.where, f32[2]{0:T(128)S(1)} %copy-done.10, f32[4,128,2048]{2,1,0:T(8,128)} %refs_0_.15, f32[256,128]{1,0:T(8,128)S(1)} %get-tuple-element.91.refs_1_, ...), custom_call_target="tpu_custom_call" | custom-call | tf_op jit(solution)/shard_map/pallas_call | solution.py:39
  133.0 3.6 %collective-permute-start.17 = (f32[64,128]{1,0:T(8,128)S(1)}, f32[64,128]{1,0:T(8,128)S(1)}, u32[]{:S(2)}, u32[]{:S(2)}) collective-permute-start(f32[64,128]{1,0:T(8,128)S(1)} %get-tuple-element.157), channel_id=1, source_target_pairs={{16,32},{48,64},{80,96},{32,16},{64,48},{96,80},{17,33},{49,65},{8... | collective-permute-start | bytes 98312 | tf_op jit(solution)/shard_map/ppermute | solution.py:547
  136.6 1.6 collective-permute-done.17.refs_2_
  138.2 0.6 shard_map.128
  138.8 11.9 %all_to_all.41.refs_5_ = f32[16,24,128]{2,1,0:T(8,128)S(1)} all-to-all(f32[16,24,128]{2,1,0:T(8,128)S(1)} %get-tuple-element.158), channel_id=1, replica_groups=mesh['inner'=8,'outer'=16] {'outer'}, dimensions={0} | all-to-all | bytes 393216 | tf_op jit(solution)/shard_map/all_to_all | solution.py:556
  150.7 2.4 %shard_map.129 = (f32[16,128]{1,0:T(8,128)S(1)}, f32[64,256]{1,0:T(8,128)S(1)}, f32[16,24,128]{2,1,0:T(8,128)S(1)}, f32[64,128]{1,0:T(8,128)S(1)}, f32[64,128]{1,0:T(8,128)S(1)}) custom-call(s32[4]{0:T(128)S(1)} %pad_add_fusion.where, f32[2]{0:T(128)S(1)} %copy-done.10, f32[4,128,2048]{2,1,0:T(8,128)S(1)} %copy-done.1, ...), custom_call_target="tpu_custom_call" | custom-call | tf_op jit(solution)/shard_map/pallas_call | solution.py:39
  153.1 3.6 %collective-permute-start.19 = (f32[64,128]{1,0:T(8,128)S(1)}, f32[64,128]{1,0:T(8,128)S(1)}, u32[]{:S(2)}, u32[]{:S(2)}) collective-permute-start(f32[64,128]{1,0:T(8,128)S(1)} %get-tuple-element.164), channel_id=1, source_target_pairs={{16,32},{48,64},{80,96},{32,16},{64,48},{96,80},{17,33},{49,65},{8... | collective-permute-start | bytes 98312 | tf_op jit(solution)/shard_map/ppermute | solution.py:547
  156.8 1.6 collective-permute-done.19.refs_2_
  158.3 0.6 shard_map.130
  158.9 11.9 %all_to_all.42.refs_5_ = f32[16,24,128]{2,1,0:T(8,128)S(1)} all-to-all(f32[16,24,128]{2,1,0:T(8,128)S(1)} %get-tuple-element.165), channel_id=1, replica_groups=mesh['inner'=8,'outer'=16] {'outer'}, dimensions={0} | all-to-all | bytes 393216 | tf_op jit(solution)/shard_map/all_to_all | solution.py:556
  170.8 2.4 %shard_map.131 = (f32[16,128]{1,0:T(8,128)S(1)}, f32[64,256]{1,0:T(8,128)S(1)}, f32[16,24,128]{2,1,0:T(8,128)S(1)}, f32[64,128]{1,0:T(8,128)S(1)}, f32[64,128]{1,0:T(8,128)S(1)}) custom-call(s32[4]{0:T(128)S(1)} %pad_add_fusion.where, f32[2]{0:T(128)S(1)} %copy-done.10, f32[4,128,2048]{2,1,0:T(8,128)S(1)} %copy-done.1, ...), custom_call_target="tpu_custom_call" | custom-call | tf_op jit(solution)/shard_map/pallas_call | solution.py:39
  173.2 3.6 %collective-permute-start.21 = (f32[64,128]{1,0:T(8,128)S(1)}, f32[64,128]{1,0:T(8,128)S(1)}, u32[]{:S(2)}, u32[]{:S(2)}) collective-permute-start(f32[64,128]{1,0:T(8,128)S(1)} %get-tuple-element.171), channel_id=1, source_target_pairs={{16,32},{48,64},{80,96},{32,16},{64,48},{96,80},{17,33},{49,65},{8... | collective-permute-start | bytes 98312 | tf_op jit(solution)/shard_map/ppermute | solution.py:547
  176.9 1.6 collective-permute-done.21.refs_2_
  178.5 1.2 shard_map.132
  179.7 5.7 %all-to-all-start.7 = ((f32[16,24,128]{2,1,0:T(8,128)}), f32[16,24,128]{2,1,0:T(8,128)S(1)}, u32[]{:S(2)}, u32[]{:S(2)}) async-start(f32[16,24,128]{2,1,0:T(8,128)} %get-tuple-element.172), calls=%async_computation.7 | async-start | bytes 393216 | tf_op jit(solution)/shard_map/all_to_all | solution.py:556
  185.4 7.6 %shard_map.124.refs_9_ = f32[160,1280]{1,0:T(8,128)S(1)} custom-call(s32[4]{0:T(128)S(1)} %pad_add_fusion.where, f32[2]{0:T(128)S(1)} %copy-done.10, f32[160,1280]{1,0:T(8,128)S(1)} %shard_map.119.refs_0_, f32[160,1280]{1,0:T(8,128)} %collective-permute-done.12.refs_1_, f32[160,1280]{1,0:T(8,128)} %collective-permute-done.13.refs_2_, ...), custom_call_target="tpu_custom_call" | custom-call | tf_op jit(solution)/shard_map/pallas_call | solution.py:39
  193.0 0.9 copy-done.5
  193.9 1.1 copy-done.6
  195.1 4.2 %shard_map.133 = (f32[8,128]{1,0:T(8,128)}, f32[2,160,512]{2,1,0:T(8,128)}) custom-call(s32[4]{0:T(128)S(1)} %pad_add_fusion.where, f32[2]{0:T(128)S(1)} %copy-done.10, f32[4,128,2048]{2,1,0:T(8,128)} %refs_0_.15, f32[256,128]{1,0:T(8,128)S(1)} %get-tuple-element.91.refs_1_, f32[16,128]{1,0:T(8,128)S(1)} %get-tuple-element.92.refs_2_, ...), custom_call_target="tpu_custom_call" | custom-call | tf_op jit(solution)/shard_map/pallas_call | solution.py:39
  (49 shorter events, 0.7 us)
Async XLA Ops:
  0.6 19.2 %copy-start.2 = (f32[2,160,512]{2,1,0:T(8,128)S(1)}, f32[2,160,512]{2,1,0:T(8,128)}, u32[]{:S(2)}) copy-start(f32[2,160,512]{2,1,0:T(8,128)} %outer.3) | copy-start | bytes 1966084
  0.6 31.5 %copy-start.9 = (f32[2]{0:T(128)S(1)}, f32[2]{0:T(128)}, u32[]{:S(2)}) copy-start(f32[2]{0:T(128)} %strengths.19) | copy-start | bytes 28
  0.7 0.7 copy-start.15
  5.1 2.2 %collective-permute-start = (f32[224,128]{1,0:T(8,128)S(1)}, f32[224,128]{1,0:T(8,128)S(1)}, u32[]{:S(2)}, u32[]{:S(2)}) collective-permute-start(f32[224,128]{1,0:T(8,128)S(1)} %get-tuple-element.94), channel_id=1, source_target_pairs={{0,16},{32,48},{64,80},{96,112},{16,0},{48,32},{80,64},{112,96},{1... | collective-permute-start | bytes 344072 | tf_op jit(solution)/shard_map/ppermute | solution.py:546
  5.2 6.1 %collective-permute-start.1 = (f32[224,128]{1,0:T(8,128)S(1)}, f32[224,128]{1,0:T(8,128)S(1)}, u32[]{:S(2)}, u32[]{:S(2)}) collective-permute-start(f32[224,128]{1,0:T(8,128)S(1)} %get-tuple-element.95), channel_id=1, source_target_pairs={{16,32},{48,64},{80,96},{32,16},{64,48},{96,80},{17,33},{49,65},{8... | collective-permute-start | bytes 344072 | tf_op jit(solution)/shard_map/ppermute | solution.py:547
  12.7 19.5 %all-to-all-start = ((f32[16,56,128]{2,1,0:T(8,128)}), f32[16,56,128]{2,1,0:T(8,128)S(1)}, u32[]{:S(2)}, u32[]{:S(2)}) async-start(f32[16,56,128]{2,1,0:T(8,128)} %get-tuple-element.99), calls=%async_computation | async-start | bytes 917504 | tf_op jit(solution)/shard_map/all_to_all | solution.py:556
  19.9 12.2 %collective-permute-start.3 = (f32[2,160,128]{2,1,0:T(8,128)S(1)}, f32[2,160,128]{2,1,0:T(8,128)S(1)}, u32[]{:S(2)}, u32[]{:S(2)}) collective-permute-start(f32[2,160,128]{2,1,0:T(8,128)S(1)} %get-tuple-element.182), channel_id=1, source_target_pairs={{1,2},{3,4},{5,6},{7,8},{9,10},{11,12},{13,14},{2,1},{4,3},{6,5},{... | collective-permute-start | bytes 491528 | tf_op jit(solution)/shard_map/ppermute | solution.py:567
  23.3 8.8 %collective-permute-start.2 = (f32[2,160,128]{2,1,0:T(8,128)S(1)}, f32[2,160,128]{2,1,0:T(8,128)S(1)}, u32[]{:S(2)}, u32[]{:S(2)}) collective-permute-start(f32[2,160,128]{2,1,0:T(8,128)S(1)} %get-tuple-element.183), channel_id=1, source_target_pairs={{0,1},{2,3},{4,5},{6,7},{8,9},{10,11},{12,13},{14,15},{1,0},{3,2},... | collective-permute-start | bytes 491528 | tf_op jit(solution)/shard_map/ppermute | solution.py:566
  32.2 10.4 %copy-start.7 = (f32[2,160,128]{2,1,0:T(8,128)}, f32[2,160,128]{2,1,0:T(8,128)S(1)}, u32[]{:S(2)}) copy-start(f32[2,160,128]{2,1,0:T(8,128)S(1)} %collective-permute-done.2.by_even) | copy-start | bytes 491524
  36.0 6.6 %copy-start.13 = (f32[16,128]{1,0:T(8,128)}, f32[16,128]{1,0:T(8,128)S(1)}, u32[]{:S(2)}) copy-start(f32[16,128]{1,0:T(8,128)S(1)} %get-tuple-element.126.refs_6_) | copy-start | bytes 24580
  36.0 2.2 %collective-permute-start.4 = (f32[64,128]{1,0:T(8,128)S(1)}, f32[64,128]{1,0:T(8,128)S(1)}, u32[]{:S(2)}, u32[]{:S(2)}) collective-permute-start(f32[64,128]{1,0:T(8,128)S(1)} %get-tuple-element.113), channel_id=1, source_target_pairs={{0,16},{32,48},{64,80},{96,112},{16,0},{48,32},{80,64},{112,96},{1... | collective-permute-start | bytes 98312 | tf_op jit(solution)/shard_map/ppermute | solution.py:546
  36.1 5.2 %collective-permute-start.5 = (f32[64,128]{1,0:T(8,128)S(1)}, f32[64,128]{1,0:T(8,128)S(1)}, u32[]{:S(2)}, u32[]{:S(2)}) collective-permute-start(f32[64,128]{1,0:T(8,128)S(1)} %get-tuple-element.114), channel_id=1, source_target_pairs={{16,32},{48,64},{80,96},{32,16},{64,48},{96,80},{17,33},{49,65},{8... | collective-permute-start | bytes 98312 | tf_op jit(solution)/shard_map/ppermute | solution.py:547
  42.6 14.7 %copy-start.11 = (f32[32,128]{1,0:T(8,128)}, f32[32,128]{1,0:T(8,128)S(1)}, u32[]{:S(2)}) copy-start(f32[32,128]{1,0:T(8,128)S(1)} %get-tuple-element.128.refs_8_) | copy-start | bytes 49156
  42.6 12.2 %all-to-all-start.1 = ((f32[16,24,128]{2,1,0:T(8,128)}), f32[16,24,128]{2,1,0:T(8,128)S(1)}, u32[]{:S(2)}, u32[]{:S(2)}) async-start(f32[16,24,128]{2,1,0:T(8,128)} %get-tuple-element.115), calls=%async_computation.1 | async-start | bytes 393216 | tf_op jit(solution)/shard_map/all_to_all | solution.py:556
  48.4 0.9 copy-start.8
  49.9 33.7 %copy-start.3 = (f32[160,1280]{1,0:T(8,128)}, f32[160,1280]{1,0:T(8,128)S(1)}, u32[]{:S(2)}) copy-start(f32[160,1280]{1,0:T(8,128)S(1)} %shard_map.118.refs_0_) | copy-start | bytes 2457604
  54.8 26.4 %copy-start = (f32[4,128,2048]{2,1,0:T(8,128)S(1)}, f32[4,128,2048]{2,1,0:T(8,128)}, u32[]{:S(2)}) copy-start(f32[4,128,2048]{2,1,0:T(8,128)} %refs_0_.15) | copy-start | bytes 12582916
  54.8 41.0 %collective-permute-start.7 = (f32[160,1280]{1,0:T(8,128)S(1)}, f32[160,1280]{1,0:T(8,128)}, u32[]{:S(2)}, u32[]{:S(2)}) collective-permute-start(f32[160,1280]{1,0:T(8,128)S(1)} %shard_map.118.refs_0_), channel_id=1, source_target_pairs={{16,32},{48,64},{80,96},{32,16},{64,48},{96,80},{17,33},{49,65},{8... | collective-permute-start | bytes 2457608 | tf_op jit(solution)/shard_map/ppermute | solution.py:589
  57.0 38.9 %collective-permute-start.6 = (f32[160,1280]{1,0:T(8,128)S(1)}, f32[160,1280]{1,0:T(8,128)}, u32[]{:S(2)}, u32[]{:S(2)}) collective-permute-start(f32[160,1280]{1,0:T(8,128)S(1)} %shard_map.118.refs_0_), channel_id=1, source_target_pairs={{0,16},{32,48},{64,80},{96,112},{16,0},{48,32},{80,64},{112,96},{1... | collective-permute-start | bytes 2457608 | tf_op jit(solution)/shard_map/ppermute | solution.py:588
  57.3 0.7 copy-start.10
  57.9 0.7 copy-start.12
  58.6 0.7 copy-start.14
  63.2 4.0 %collective-permute-start.8 = (f32[64,128]{1,0:T(8,128)S(1)}, f32[64,128]{1,0:T(8,128)S(1)}, u32[]{:S(2)}, u32[]{:S(2)}) collective-permute-start(f32[64,128]{1,0:T(8,128)S(1)} %get-tuple-element.130), channel_id=1, source_target_pairs={{0,16},{32,48},{64,80},{96,112},{16,0},{48,32},{80,64},{112,96},{1... | collective-permute-start | bytes 98312 | tf_op jit(solution)/shard_map/ppermute | solution.py:546
  63.6 5.5 %collective-permute-start.9 = (f32[64,128]{1,0:T(8,128)S(1)}, f32[64,128]{1,0:T(8,128)S(1)}, u32[]{:S(2)}, u32[]{:S(2)}) collective-permute-start(f32[64,128]{1,0:T(8,128)S(1)} %get-tuple-element.131), channel_id=1, source_target_pairs={{16,32},{48,64},{80,96},{32,16},{64,48},{96,80},{17,33},{49,65},{8... | collective-permute-start | bytes 98312 | tf_op jit(solution)/shard_map/ppermute | solution.py:547
  83.6 3.8 %collective-permute-start.10 = (f32[64,128]{1,0:T(8,128)S(1)}, f32[64,128]{1,0:T(8,128)S(1)}, u32[]{:S(2)}, u32[]{:S(2)}) collective-permute-start(f32[64,128]{1,0:T(8,128)S(1)} %get-tuple-element.137), channel_id=1, source_target_pairs={{0,16},{32,48},{64,80},{96,112},{16,0},{48,32},{80,64},{112,96},{1... | collective-permute-start | bytes 98312 | tf_op jit(solution)/shard_map/ppermute | solution.py:546
  83.7 5.2 %collective-permute-start.11 = (f32[64,128]{1,0:T(8,128)S(1)}, f32[64,128]{1,0:T(8,128)S(1)}, u32[]{:S(2)}, u32[]{:S(2)}) collective-permute-start(f32[64,128]{1,0:T(8,128)S(1)} %get-tuple-element.138), channel_id=1, source_target_pairs={{16,32},{48,64},{80,96},{32,16},{64,48},{96,80},{17,33},{49,65},{8... | collective-permute-start | bytes 98312 | tf_op jit(solution)/shard_map/ppermute | solution.py:547
  90.2 14.5 %all-to-all-start.3 = ((f32[16,24,128]{2,1,0:T(8,128)}), f32[16,24,128]{2,1,0:T(8,128)S(1)}, u32[]{:S(2)}, u32[]{:S(2)}) async-start(f32[16,24,128]{2,1,0:T(8,128)} %get-tuple-element.139), calls=%async_computation.3 | async-start | bytes 393216 | tf_op jit(solution)/shard_map/all_to_all | solution.py:556
  95.9 1.1 copy-start.4
  108.5 3.7 %collective-permute-start.14 = (f32[64,128]{1,0:T(8,128)S(1)}, f32[64,128]{1,0:T(8,128)S(1)}, u32[]{:S(2)}, u32[]{:S(2)}) collective-permute-start(f32[64,128]{1,0:T(8,128)S(1)} %get-tuple-element.149), channel_id=1, source_target_pairs={{0,16},{32,48},{64,80},{96,112},{16,0},{48,32},{80,64},{112,96},{1... | collective-permute-start | bytes 98312 | tf_op jit(solution)/shard_map/ppermute | solution.py:546
  108.6 5.2 %collective-permute-start.15 = (f32[64,128]{1,0:T(8,128)S(1)}, f32[64,128]{1,0:T(8,128)S(1)}, u32[]{:S(2)}, u32[]{:S(2)}) collective-permute-start(f32[64,128]{1,0:T(8,128)S(1)} %get-tuple-element.150), channel_id=1, source_target_pairs={{16,32},{48,64},{80,96},{32,16},{64,48},{96,80},{17,33},{49,65},{8... | collective-permute-start | bytes 98312 | tf_op jit(solution)/shard_map/ppermute | solution.py:547
  115.1 13.7 %all-to-all-start.4 = ((f32[16,24,128]{2,1,0:T(8,128)}), f32[16,24,128]{2,1,0:T(8,128)S(1)}, u32[]{:S(2)}, u32[]{:S(2)}) async-start(f32[16,24,128]{2,1,0:T(8,128)} %get-tuple-element.151), calls=%async_computation.4 | async-start | bytes 393216 | tf_op jit(solution)/shard_map/all_to_all | solution.py:556
  122.4 63.0 %collective-permute-start.13 = (f32[160,1280]{1,0:T(8,128)S(1)}, f32[160,1280]{1,0:T(8,128)}, u32[]{:S(2)}, u32[]{:S(2)}) collective-permute-start(f32[160,1280]{1,0:T(8,128)S(1)} %shard_map.119.refs_0_), channel_id=1, source_target_pairs={{16,32},{48,64},{80,96},{32,16},{64,48},{96,80},{17,33},{49,65},{8... | collective-permute-start | bytes 2457608 | tf_op jit(solution)/shard_map/ppermute | solution.py:589
  125.4 60.0 %collective-permute-start.12 = (f32[160,1280]{1,0:T(8,128)S(1)}, f32[160,1280]{1,0:T(8,128)}, u32[]{:S(2)}, u32[]{:S(2)}) collective-permute-start(f32[160,1280]{1,0:T(8,128)S(1)} %shard_map.119.refs_0_), channel_id=1, source_target_pairs={{0,16},{32,48},{64,80},{96,112},{16,0},{48,32},{80,64},{112,96},{1... | collective-permute-start | bytes 2457608 | tf_op jit(solution)/shard_map/ppermute | solution.py:588
  128.8 21.9 %copy-start.1 = (f32[4,128,2048]{2,1,0:T(8,128)S(1)}, f32[4,128,2048]{2,1,0:T(8,128)}, u32[]{:S(2)}) copy-start(f32[4,128,2048]{2,1,0:T(8,128)} %refs_0_.15) | copy-start | bytes 12582916
  132.9 3.7 %collective-permute-start.16 = (f32[64,128]{1,0:T(8,128)S(1)}, f32[64,128]{1,0:T(8,128)S(1)}, u32[]{:S(2)}, u32[]{:S(2)}) collective-permute-start(f32[64,128]{1,0:T(8,128)S(1)} %get-tuple-element.156), channel_id=1, source_target_pairs={{0,16},{32,48},{64,80},{96,112},{16,0},{48,32},{80,64},{112,96},{1... | collective-permute-start | bytes 98312 | tf_op jit(solution)/shard_map/ppermute | solution.py:546
  133.0 5.2 %collective-permute-start.17 = (f32[64,128]{1,0:T(8,128)S(1)}, f32[64,128]{1,0:T(8,128)S(1)}, u32[]{:S(2)}, u32[]{:S(2)}) collective-permute-start(f32[64,128]{1,0:T(8,128)S(1)} %get-tuple-element.157), channel_id=1, source_target_pairs={{16,32},{48,64},{80,96},{32,16},{64,48},{96,80},{17,33},{49,65},{8... | collective-permute-start | bytes 98312 | tf_op jit(solution)/shard_map/ppermute | solution.py:547
  153.0 3.7 %collective-permute-start.18 = (f32[64,128]{1,0:T(8,128)S(1)}, f32[64,128]{1,0:T(8,128)S(1)}, u32[]{:S(2)}, u32[]{:S(2)}) collective-permute-start(f32[64,128]{1,0:T(8,128)S(1)} %get-tuple-element.163), channel_id=1, source_target_pairs={{0,16},{32,48},{64,80},{96,112},{16,0},{48,32},{80,64},{112,96},{1... | collective-permute-start | bytes 98312 | tf_op jit(solution)/shard_map/ppermute | solution.py:546
  153.1 5.2 %collective-permute-start.19 = (f32[64,128]{1,0:T(8,128)S(1)}, f32[64,128]{1,0:T(8,128)S(1)}, u32[]{:S(2)}, u32[]{:S(2)}) collective-permute-start(f32[64,128]{1,0:T(8,128)S(1)} %get-tuple-element.164), channel_id=1, source_target_pairs={{16,32},{48,64},{80,96},{32,16},{64,48},{96,80},{17,33},{49,65},{8... | collective-permute-start | bytes 98312 | tf_op jit(solution)/shard_map/ppermute | solution.py:547
  173.2 3.7 %collective-permute-start.20 = (f32[64,128]{1,0:T(8,128)S(1)}, f32[64,128]{1,0:T(8,128)S(1)}, u32[]{:S(2)}, u32[]{:S(2)}) collective-permute-start(f32[64,128]{1,0:T(8,128)S(1)} %get-tuple-element.170), channel_id=1, source_target_pairs={{0,16},{32,48},{64,80},{96,112},{16,0},{48,32},{80,64},{112,96},{1... | collective-permute-start | bytes 98312 | tf_op jit(solution)/shard_map/ppermute | solution.py:546
  173.2 5.2 %collective-permute-start.21 = (f32[64,128]{1,0:T(8,128)S(1)}, f32[64,128]{1,0:T(8,128)S(1)}, u32[]{:S(2)}, u32[]{:S(2)}) collective-permute-start(f32[64,128]{1,0:T(8,128)S(1)} %get-tuple-element.171), channel_id=1, source_target_pairs={{16,32},{48,64},{80,96},{32,16},{64,48},{96,80},{17,33},{49,65},{8... | collective-permute-start | bytes 98312 | tf_op jit(solution)/shard_map/ppermute | solution.py:547
  179.7 14.2 %all-to-all-start.7 = ((f32[16,24,128]{2,1,0:T(8,128)}), f32[16,24,128]{2,1,0:T(8,128)S(1)}, u32[]{:S(2)}, u32[]{:S(2)}) async-start(f32[16,24,128]{2,1,0:T(8,128)} %get-tuple-element.172), calls=%async_computation.7 | async-start | bytes 393216 | tf_op jit(solution)/shard_map/all_to_all | solution.py:556
  193.0 0.9 copy-start.5
  193.9 1.1 copy-start.6

commit v3 on v2

--- a/solution.py
+++ b/solution.py
@@ -239,22 +239,6 @@
 
 
 def advance(copies, first, last_power, factor, field, dipole, surface, levels, pairs, thresholds, arrived, cs, fs, ghost):
-    sums = []
-    for l in range(LB):
-        if copies is not None:
-            copies[l].wait()
-
-        def body(s, carry):
-            tile = dipole[l, :, pl.ds(pl.multiple_of(s * 128, 128), 128)]
-            return (
-                carry[0] + tile * arrived[s, l : l + 1, :],
-                carry[1] + tile * arrived[s, 4 + l : 5 + l, :],
-            )
-
-        zero = jnp.zeros((128, 128), F32)
-        re, im = lax.fori_loop(0, 16, body, (zero, zero), unroll=16)
-        sums.append((jnp.sum(re.T, axis=0, keepdims=True), jnp.sum(im.T, axis=0, keepdims=True)))
-    forward = jnp.concatenate([a for a, _ in sums] + [b for _, b in sums], axis=0)
     backward = arrived[0, 8:16, :]
     tail = arrived[0, 16:24, :]
     for s in range(1, 16):
@@ -279,8 +263,6 @@
         [jnp.broadcast_to(own[0:1], (4, 256)), jnp.broadcast_to(own[PTS : PTS + 1], (4, 256))], axis=0
     )
     surf = jnp.dot(edge * block_mask(), surface[...], precision=HIGHEST, preferred_element_type=F32)
-    image = levels[8:16, :] * (levels[0:8, :] * c + field * (forward + backward) - kinetic_scale * surf)
-    c_new = jnp.concatenate([factor * image[4:8], -factor * image[0:4]], axis=0)
     coupled = lax.dot_general(whole, pairs[...], NT, precision=HIGHEST, preferred_element_type=F32)
     b_re = jnp.concatenate([tail[0:1], tail[1:2]], axis=1)
     b_im = jnp.concatenate([tail[2:3], tail[3:4]], axis=1)
@@ -292,6 +274,24 @@
     grid = kinetic_scale * (2.0 * own - left - right) + thresholds[...] * own + field * coupled
     grid = jnp.where(lanes < OWN, grid, 0.0)
     f_new = jnp.concatenate([factor * grid[PTS:], -factor * grid[:PTS]], axis=0)
+    sums = []
+    for l in range(LB):
+        if copies is not None:
+            copies[l].wait()
+
+        def body(s, carry):
+            tile = dipole[l, :, pl.ds(pl.multiple_of(s * 128, 128), 128)]
+            return (
+                carry[0] + tile * arrived[s, l : l + 1, :],
+                carry[1] + tile * arrived[s, 4 + l : 5 + l, :],
+            )
+
+        zero = jnp.zeros((128, 128), F32)
+        re, im = lax.fori_loop(0, 16, body, (zero, zero), unroll=16)
+        sums.append((jnp.sum(re.T, axis=0, keepdims=True), jnp.sum(im.T, axis=0, keepdims=True)))
+    forward = jnp.concatenate([a for a, _ in sums] + [b for _, b in sums], axis=0)
+    image = levels[8:16, :] * (levels[0:8, :] * c + field * (forward + backward) - kinetic_scale * surf)
+    c_new = jnp.concatenate([factor * image[4:8], -factor * image[0:4]], axis=0)
     c_sum = c_sum + c_new
     strip_sum = strip_sum + f_new
     if last_power:
@@ -394,8 +394,8 @@
         source[...] = given[...]
         sum_ref[...] = given_sum[...]
     field = strengths[step]
-    lanes = rows_of(1, (1, WIDTH))
-    past = (lanes >= 512) & (lanes < 512 + 64) & (jnp.full((1, WIDTH), where[1], jnp.int32) == where[3])
+    lanes = rows_of(1, (1, WIDTH - 512))
+    past = (lanes < 64) & (jnp.full((1, WIDTH - 512), where[1], jnp.int32) == where[3])
     keep = jnp.where(past, 0.0, 1.0).astype(F32)
     for power in powers:
         factor = time_step / power
@@ -404,7 +404,10 @@
         if power < ORDER:
             groups += [(ring, 160, ring - CH, 200), (320, 480 - ring, 280, 480 - ring + CH)]
         for out0, out1, in0, in1 in groups:
-            matrix = couplings[out0:out1, in0:in1]
+            shape = (out1 - out0, in1 - in0)
+            level = 2.0 * kinetic_scale + pack[out0:out1, CH : CH + 1]
+            same = rows_of(0, shape) + out0 == rows_of(1, shape) + in0
+            matrix = factor * (field * couplings[out0:out1, in0:in1] + jnp.where(same, level, 0.0))
             m_hi = matrix.astype(BF16)
             m_lo = (matrix - m_hi.astype(F32)).astype(BF16)
             images = []
@@ -413,17 +416,15 @@
                 f = source[in0:in1, cols]
                 f_hi = f.astype(BF16)
                 f_lo = (f - f_hi.astype(F32)).astype(BF16)
-                coupled = jnp.dot(m_hi, f_hi, preferred_element_type=F32)
-                coupled = coupled + jnp.dot(m_hi, f_lo, preferred_element_type=F32)
-                coupled = coupled + jnp.dot(m_lo, f_hi, preferred_element_type=F32)
+                image = jnp.dot(m_hi, f_hi, preferred_element_type=F32)
+                image = image + jnp.dot(m_hi, f_lo, preferred_element_type=F32)
+                image = image + jnp.dot(m_lo, f_hi, preferred_element_type=F32)
                 mine = source[out0:out1, cols]
-                left = pltpu.roll(mine, 1, 1)
-                right = pltpu.roll(mine, WIDTH - 1, 1)
-                level = pack[out0:out1, CH : CH + 1]
-                image = kinetic_scale * (2.0 * mine - left - right) + level * mine + field * coupled
-                images.append(image * keep)
-            new_re = factor * images[1]
-            new_im = -factor * images[0]
+                beside = pltpu.roll(mine, 1, 1) + pltpu.roll(mine, WIDTH - 1, 1)
+                image = image - (factor * kinetic_scale) * beside
+                images.append(jnp.concatenate([image[:, :512], image[:, 512:] * keep], axis=1))
+            new_re = images[1]
+            new_im = -images[0]
             if power < ORDER:
                 target[out0:out1, 0:WIDTH] = new_re
                 target[out0:out1, WIDTH : 2 * WIDTH] = new_im

time: 203 us -> 202 us (level)
  transfers between devices with their start and end apart: 27 -> 27, of which waited for: 11 -> 11; matrix products, arithmetic and copies ran while one was open for 0% -> 0% of each run, Pallas kernels for 18% -> 17%
where the time goes in v3:
time: 202 us; the launch traced here: 198 us
  starting transfers between devices  67.5 us (33%)
  Pallas kernels  53.5 us (26%)
  blocking collectives  35.3 us (17%)
  waiting for transfers between devices  33.5 us (17%)
  local copies, waits for them, and re-layouts  6.95 us (3%)
    pallas_call x20, Pallas kernels, run(): pl.pallas_call(kernel, out_shape=outs, in_specs=[SM] * smem + [HBM if n i...  49.8 us
    all_to_all x3, blocking collectives, local(): lax.all_to_all(q, 'outer', split_axis=0, concat_axis=0, tiled=True)  35.3 us
    all_to_all x5, starting transfers between devices, local(): lax.all_to_all(q, 'outer', split_axis=0, concat_axis=0, tiled=True)  31.5 us
    ppermute x8, starting transfers between devices, local(): from_b = lax.ppermute(to_b, 'inner', chips)  26 us
    ppermute x8, waiting for transfers between devices, local(): from_b = lax.ppermute(to_b, 'inner', chips)  16.9 us
    ppermute x1, waiting for transfers between devices, local(): by_odd = lax.ppermute(jnp.where(is_odd, tail, head), 'outer', odd)  8.43 us
    all_to_all x5, waiting for transfers between devices, local(): lax.all_to_all(q, 'outer', split_axis=0, concat_axis=0, tiled=True)  8.17 us
    unnamed x32, local copies, waits for them, and re-layouts  6.93 us
  transfers between devices with their start and end apart: 27, of which 11 were waited for; matrix products, arithmetic and copies ran while one was open for 0% of the time, Pallas kernels for 17%

profile of v3, /device:TPU:88, one launch (start us, length us, event | category | flops | bytes accessed | tf_op | source)
XLA Modules:
  0.0 198.3 jit_solution(14337743993878993227)
XLA Ops:
  0.7 0.7 copy-done.15
  1.5 3.7 %shard_map.113 = (f32[16,128]{1,0:T(8,128)S(1)}, f32[64,256]{1,0:T(8,128)S(1)}, f32[16,24,128]{2,1,0:T(8,128)S(1)}, f32[224,128]{1,0:T(8,128)S(1)}, f32[224,128]...) custom-call(s32[4]{0:T(128)S(1)} %pad_add_fusion.where, ...), custom_call_target="tpu_custom_call" | custom-call | tf_op jit(solution)/shard_map/pallas_call | solution.py:497
  5.2 2.1 %collective-permute-start.1 = (f32[224,128]{1,0:T(8,128)S(1)}, f32[224,128]{1,0:T(8,128)S(1)}, u32[]{:S(2)}, u32[]{:S(2)}) collective-permute-start(f32[224,128]{1,0:T(8,128)S(1)} %get-tuple-element.95), channel_id=1, source_target_pairs={{16,32},{48,64},{80,96},{32,16},{64,48},{96,80},{17,33},{49,65},{8... | collective-permute-start | bytes 344072 | tf_op jit(solution)/shard_map/ppermute | solution.py:548
  7.4 4.0 %collective-permute-done.1.refs_2_ = f32[224,128]{1,0:T(8,128)S(1)} collective-permute-done((f32[224,128]{1,0:T(8,128)S(1)}, f32[224,128]{1,0:T(8,128)S(1)}, u32[]{:S(2)}, u32[]{:S(2)}) %collective-permute-start.1) | collective-permute-done | bytes 114720 | tf_op jit(solution)/shard_map/ppermute | solution.py:548
  11.3 1.4 shard_map.114
  12.7 7.2 %all-to-all-start = ((f32[16,56,128]{2,1,0:T(8,128)}), f32[16,56,128]{2,1,0:T(8,128)S(1)}, u32[]{:S(2)}, u32[]{:S(2)}) async-start(f32[16,56,128]{2,1,0:T(8,128)} %get-tuple-element.99), calls=%async_computation | async-start | bytes 917504 | tf_op jit(solution)/shard_map/all_to_all | solution.py:557
  19.9 3.4 %collective-permute-start.3 = (f32[2,160,128]{2,1,0:T(8,128)S(1)}, f32[2,160,128]{2,1,0:T(8,128)S(1)}, u32[]{:S(2)}, u32[]{:S(2)}) collective-permute-start(f32[2,160,128]{2,1,0:T(8,128)S(1)} %get-tuple-element.182), channel_id=1, source_target_pairs={{1,2},{3,4},{5,6},{7,8},{9,10},{11,12},{13,14},{2,1},{4,3},{6,5},{... | collective-permute-start | bytes 491528 | tf_op jit(solution)/shard_map/ppermute | solution.py:568
  23.3 0.1 collective-permute-start.2
  23.4 0.3 shard_map.115
  23.7 8.4 %collective-permute-done.3.by_odd = f32[2,160,128]{2,1,0:T(8,128)S(1)} collective-permute-done((f32[2,160,128]{2,1,0:T(8,128)S(1)}, f32[2,160,128]{2,1,0:T(8,128)S(1)}, u32[]{:S(2)}, u32[]{:S(2)}) %collective-permute-start.3) | collective-permute-done | bytes 163872 | tf_op jit(solution)/shard_map/ppermute | solution.py:568
  32.2 3.8 %shard_map.116 = (f32[16,128]{1,0:T(8,128)S(1)}, f32[64,256]{1,0:T(8,128)S(1)}, f32[16,24,128]{2,1,0:T(8,128)S(1)}, f32[64,128]{1,0:T(8,128)S(1)}, f32[64,128]{1,0:T(8,128)S(1)}) custom-call(s32[4]{0:T(128)S(1)} %pad_add_fusion.where, f32[2]{0:T(128)S(1)} %copy-done.9, f32[4,128,2048]{2,1,0:T(8,128)} %refs_0_.15, f32[256,128]{1,0:T(8,128)S(1)} %get-tuple-element.91.refs_1_, ...), custom_call_target="tpu_custom_call" | custom-call | tf_op jit(solution)/shard_map/pallas_call | solution.py:39
  36.1 2.1 %collective-permute-start.5 = (f32[64,128]{1,0:T(8,128)S(1)}, f32[64,128]{1,0:T(8,128)S(1)}, u32[]{:S(2)}, u32[]{:S(2)}) collective-permute-start(f32[64,128]{1,0:T(8,128)S(1)} %get-tuple-element.114), channel_id=1, source_target_pairs={{16,32},{48,64},{80,96},{32,16},{64,48},{96,80},{17,33},{49,65},{8... | collective-permute-start | bytes 98312 | tf_op jit(solution)/shard_map/ppermute | solution.py:548
  38.3 3.1 %collective-permute-done.5.refs_2_ = f32[64,128]{1,0:T(8,128)S(1)} collective-permute-done((f32[64,128]{1,0:T(8,128)S(1)}, f32[64,128]{1,0:T(8,128)S(1)}, u32[]{:S(2)}, u32[]{:S(2)}) %collective-permute-start.5) | collective-permute-done | bytes 32800 | tf_op jit(solution)/shard_map/ppermute | solution.py:548
  41.4 1.2 shard_map.117
  42.6 5.8 %all-to-all-start.1 = ((f32[16,24,128]{2,1,0:T(8,128)}), f32[16,24,128]{2,1,0:T(8,128)S(1)}, u32[]{:S(2)}, u32[]{:S(2)}) async-start(f32[16,24,128]{2,1,0:T(8,128)} %get-tuple-element.115), calls=%async_computation.1 | async-start | bytes 393216 | tf_op jit(solution)/shard_map/all_to_all | solution.py:557
  48.4 0.9 copy-done.8
  49.3 0.6 shard_map.118.refs_0_
  49.9 4.9 %all-to-all-done.1.refs_5_ = f32[16,24,128]{2,1,0:T(8,128)S(1)} async-done(((f32[16,24,128]{2,1,0:T(8,128)}), f32[16,24,128]{2,1,0:T(8,128)S(1)}, u32[]{:S(2)}, u32[]{:S(2)}) %all-to-all-start.1) | async-done | bytes 196640 | tf_op jit(solution)/shard_map/all_to_all | solution.py:557
  54.8 2.2 %collective-permute-start.7 = (f32[160,1280]{1,0:T(8,128)S(1)}, f32[160,1280]{1,0:T(8,128)}, u32[]{:S(2)}, u32[]{:S(2)}) collective-permute-start(f32[160,1280]{1,0:T(8,128)S(1)} %shard_map.118.refs_0_), channel_id=1, source_target_pairs={{16,32},{48,64},{80,96},{32,16},{64,48},{96,80},{17,33},{49,65},{8... | collective-permute-start | bytes 2457608 | tf_op jit(solution)/shard_map/ppermute | solution.py:590
  57.0 0.3 collective-permute-start.6
  57.3 0.7 copy-done.10
  57.9 0.7 copy-done.12
  58.7 0.7 copy-done.14
  59.4 3.8 %shard_map.120 = (f32[16,128]{1,0:T(8,128)S(1)}, f32[64,256]{1,0:T(8,128)S(1)}, f32[16,24,128]{2,1,0:T(8,128)S(1)}, f32[64,128]{1,0:T(8,128)S(1)}, f32[64,128]{1,0:T(8,128)S(1)}) custom-call(s32[4]{0:T(128)S(1)} %pad_add_fusion.where, f32[2]{0:T(128)S(1)} %copy-done.10, f32[4,128,2048]{2,1,0:T(8,128)} %refs_0_.15, f32[256,128]{1,0:T(8,128)S(1)} %get-tuple-element.91.refs_1_, ...), custom_call_target="tpu_custom_call" | custom-call | tf_op jit(solution)/shard_map/pallas_call | solution.py:39
  63.2 0.4 collective-permute-start.8
  63.6 3.6 %collective-permute-start.9 = (f32[64,128]{1,0:T(8,128)S(1)}, f32[64,128]{1,0:T(8,128)S(1)}, u32[]{:S(2)}, u32[]{:S(2)}) collective-permute-start(f32[64,128]{1,0:T(8,128)S(1)} %get-tuple-element.131), channel_id=1, source_target_pairs={{16,32},{48,64},{80,96},{32,16},{64,48},{96,80},{17,33},{49,65},{8... | collective-permute-start | bytes 98312 | tf_op jit(solution)/shard_map/ppermute | solution.py:548
  67.2 1.9 collective-permute-done.9.refs_2_
  69.1 0.6 shard_map.121
  69.7 11.6 %all_to_all.40.refs_5_ = f32[16,24,128]{2,1,0:T(8,128)S(1)} all-to-all(f32[16,24,128]{2,1,0:T(8,128)S(1)} %get-tuple-element.132), channel_id=1, replica_groups=mesh['inner'=8,'outer'=16] {'outer'}, dimensions={0} | all-to-all | bytes 393216 | tf_op jit(solution)/shard_map/all_to_all | solution.py:557
  81.3 2.3 %shard_map.122 = (f32[16,128]{1,0:T(8,128)S(1)}, f32[64,256]{1,0:T(8,128)S(1)}, f32[16,24,128]{2,1,0:T(8,128)S(1)}, f32[64,128]{1,0:T(8,128)S(1)}, f32[64,128]{1,0:T(8,128)S(1)}) custom-call(s32[4]{0:T(128)S(1)} %pad_add_fusion.where, f32[2]{0:T(128)S(1)} %copy-done.10, f32[4,128,2048]{2,1,0:T(8,128)S(1)} %copy-done, ...), custom_call_target="tpu_custom_call" | custom-call | tf_op jit(solution)/shard_map/pallas_call | solution.py:39
  83.7 3.6 %collective-permute-start.11 = (f32[64,128]{1,0:T(8,128)S(1)}, f32[64,128]{1,0:T(8,128)S(1)}, u32[]{:S(2)}, u32[]{:S(2)}) collective-permute-start(f32[64,128]{1,0:T(8,128)S(1)} %get-tuple-element.138), channel_id=1, source_target_pairs={{16,32},{48,64},{80,96},{32,16},{64,48},{96,80},{17,33},{49,65},{8... | collective-permute-start | bytes 98312 | tf_op jit(solution)/shard_map/ppermute | solution.py:548
  87.4 1.6 collective-permute-done.11.refs_2_
  88.9 1.2 shard_map.123
  90.2 5.7 %all-to-all-start.3 = ((f32[16,24,128]{2,1,0:T(8,128)}), f32[16,24,128]{2,1,0:T(8,128)S(1)}, u32[]{:S(2)}, u32[]{:S(2)}) async-start(f32[16,24,128]{2,1,0:T(8,128)} %get-tuple-element.139), calls=%async_computation.3 | async-start | bytes 393216 | tf_op jit(solution)/shard_map/all_to_all | solution.py:557
  95.9 1.1 copy-done.4
  97.0 7.2 %shard_map.119.refs_0_ = f32[160,1280]{1,0:T(8,128)S(1)} custom-call(s32[4]{0:T(128)S(1)} %pad_add_fusion.where, f32[2]{0:T(128)S(1)} %copy-done.10, f32[160,1280]{1,0:T(8,128)S(1)} %copy-done.4, f32[160,1280]{1,0:T(8,128)} %collective-permute-done.6.refs_1_, f32[160,1280]{1,0:T(8,128)} %collective-permute-done.7.refs_2_, ...), custom_call_target="tpu_custom_call" | custom-call | tf_op jit(solution)/shard_map/pallas_call | solution.py:39
  104.2 3.8 %shard_map.125 = (f32[16,128]{1,0:T(8,128)S(1)}, f32[64,256]{1,0:T(8,128)S(1)}, f32[16,24,128]{2,1,0:T(8,128)S(1)}, f32[64,128]{1,0:T(8,128)S(1)}, f32[64,128]{1,0:T(8,128)S(1)}) custom-call(s32[4]{0:T(128)S(1)} %pad_add_fusion.where, f32[2]{0:T(128)S(1)} %copy-done.10, f32[4,128,2048]{2,1,0:T(8,128)} %refs_0_.15, f32[256,128]{1,0:T(8,128)S(1)} %get-tuple-element.91.refs_1_, ...), custom_call_target="tpu_custom_call" | custom-call | tf_op jit(solution)/shard_map/pallas_call | solution.py:39
  108.1 0.1 collective-permute-start.14
  108.2 3.6 %collective-permute-start.15 = (f32[64,128]{1,0:T(8,128)S(1)}, f32[64,128]{1,0:T(8,128)S(1)}, u32[]{:S(2)}, u32[]{:S(2)}) collective-permute-start(f32[64,128]{1,0:T(8,128)S(1)} %get-tuple-element.150), channel_id=1, source_target_pairs={{16,32},{48,64},{80,96},{32,16},{64,48},{96,80},{17,33},{49,65},{8... | collective-permute-start | bytes 98312 | tf_op jit(solution)/shard_map/ppermute | solution.py:548
  111.8 1.6 collective-permute-done.15.refs_2_
  113.4 1.2 shard_map.126
  114.6 7.3 %all-to-all-start.4 = ((f32[16,24,128]{2,1,0:T(8,128)}), f32[16,24,128]{2,1,0:T(8,128)S(1)}, u32[]{:S(2)}, u32[]{:S(2)}) async-start(f32[16,24,128]{2,1,0:T(8,128)} %get-tuple-element.151), calls=%async_computation.4 | async-start | bytes 393216 | tf_op jit(solution)/shard_map/all_to_all | solution.py:557
  121.9 3.0 %collective-permute-start.13 = (f32[160,1280]{1,0:T(8,128)S(1)}, f32[160,1280]{1,0:T(8,128)}, u32[]{:S(2)}, u32[]{:S(2)}) collective-permute-start(f32[160,1280]{1,0:T(8,128)S(1)} %shard_map.119.refs_0_), channel_id=1, source_target_pairs={{16,32},{48,64},{80,96},{32,16},{64,48},{96,80},{17,33},{49,65},{8... | collective-permute-start | bytes 2457608 | tf_op jit(solution)/shard_map/ppermute | solution.py:590
  124.9 0.1 collective-permute-start.12
  125.0 3.3 %all-to-all-done.4.refs_5_ = f32[16,24,128]{2,1,0:T(8,128)S(1)} async-done(((f32[16,24,128]{2,1,0:T(8,128)}), f32[16,24,128]{2,1,0:T(8,128)S(1)}, u32[]{:S(2)}, u32[]{:S(2)}) %all-to-all-start.4) | async-done | bytes 196640 | tf_op jit(solution)/shard_map/all_to_all | solution.py:557
  128.3 4.1 %shard_map.127 = (f32[16,128]{1,0:T(8,128)S(1)}, f32[64,256]{1,0:T(8,128)S(1)}, f32[16,24,128]{2,1,0:T(8,128)S(1)}, f32[64,128]{1,0:T(8,128)S(1)}, f32[64,128]{1,0:T(8,128)S(1)}) custom-call(s32[4]{0:T(128)S(1)} %pad_add_fusion.where, f32[2]{0:T(128)S(1)} %copy-done.10, f32[4,128,2048]{2,1,0:T(8,128)} %refs_0_.15, f32[256,128]{1,0:T(8,128)S(1)} %get-tuple-element.91.refs_1_, ...), custom_call_target="tpu_custom_call" | custom-call | tf_op jit(solution)/shard_map/pallas_call | solution.py:39
  132.5 3.6 %collective-permute-start.17 = (f32[64,128]{1,0:T(8,128)S(1)}, f32[64,128]{1,0:T(8,128)S(1)}, u32[]{:S(2)}, u32[]{:S(2)}) collective-permute-start(f32[64,128]{1,0:T(8,128)S(1)} %get-tuple-element.157), channel_id=1, source_target_pairs={{16,32},{48,64},{80,96},{32,16},{64,48},{96,80},{17,33},{49,65},{8... | collective-permute-start | bytes 98312 | tf_op jit(solution)/shard_map/ppermute | solution.py:548
  136.2 1.6 collective-permute-done.17.refs_2_
  137.8 0.6 shard_map.128
  138.3 11.9 %all_to_all.41.refs_5_ = f32[16,24,128]{2,1,0:T(8,128)S(1)} all-to-all(f32[16,24,128]{2,1,0:T(8,128)S(1)} %get-tuple-element.158), channel_id=1, replica_groups=mesh['inner'=8,'outer'=16] {'outer'}, dimensions={0} | all-to-all | bytes 393216 | tf_op jit(solution)/shard_map/all_to_all | solution.py:557
  150.2 2.3 %shard_map.129 = (f32[16,128]{1,0:T(8,128)S(1)}, f32[64,256]{1,0:T(8,128)S(1)}, f32[16,24,128]{2,1,0:T(8,128)S(1)}, f32[64,128]{1,0:T(8,128)S(1)}, f32[64,128]{1,0:T(8,128)S(1)}) custom-call(s32[4]{0:T(128)S(1)} %pad_add_fusion.where, f32[2]{0:T(128)S(1)} %copy-done.10, f32[4,128,2048]{2,1,0:T(8,128)S(1)} %copy-done.1, ...), custom_call_target="tpu_custom_call" | custom-call | tf_op jit(solution)/shard_map/pallas_call | solution.py:39
  152.7 3.6 %collective-permute-start.19 = (f32[64,128]{1,0:T(8,128)S(1)}, f32[64,128]{1,0:T(8,128)S(1)}, u32[]{:S(2)}, u32[]{:S(2)}) collective-permute-start(f32[64,128]{1,0:T(8,128)S(1)} %get-tuple-element.164), channel_id=1, source_target_pairs={{16,32},{48,64},{80,96},{32,16},{64,48},{96,80},{17,33},{49,65},{8... | collective-permute-start | bytes 98312 | tf_op jit(solution)/shard_map/ppermute | solution.py:548
  156.3 1.6 collective-permute-done.19.refs_2_
  157.9 0.6 shard_map.130
  158.5 11.9 %all_to_all.42.refs_5_ = f32[16,24,128]{2,1,0:T(8,128)S(1)} all-to-all(f32[16,24,128]{2,1,0:T(8,128)S(1)} %get-tuple-element.165), channel_id=1, replica_groups=mesh['inner'=8,'outer'=16] {'outer'}, dimensions={0} | all-to-all | bytes 393216 | tf_op jit(solution)/shard_map/all_to_all | solution.py:557
  170.4 2.3 %shard_map.131 = (f32[16,128]{1,0:T(8,128)S(1)}, f32[64,256]{1,0:T(8,128)S(1)}, f32[16,24,128]{2,1,0:T(8,128)S(1)}, f32[64,128]{1,0:T(8,128)S(1)}, f32[64,128]{1,0:T(8,128)S(1)}) custom-call(s32[4]{0:T(128)S(1)} %pad_add_fusion.where, f32[2]{0:T(128)S(1)} %copy-done.10, f32[4,128,2048]{2,1,0:T(8,128)S(1)} %copy-done.1, ...), custom_call_target="tpu_custom_call" | custom-call | tf_op jit(solution)/shard_map/pallas_call | solution.py:39
  172.8 3.6 %collective-permute-start.21 = (f32[64,128]{1,0:T(8,128)S(1)}, f32[64,128]{1,0:T(8,128)S(1)}, u32[]{:S(2)}, u32[]{:S(2)}) collective-permute-start(f32[64,128]{1,0:T(8,128)S(1)} %get-tuple-element.171), channel_id=1, source_target_pairs={{16,32},{48,64},{80,96},{32,16},{64,48},{96,80},{17,33},{49,65},{8... | collective-permute-start | bytes 98312 | tf_op jit(solution)/shard_map/ppermute | solution.py:548
  176.4 1.6 collective-permute-done.21.refs_2_
  178.0 1.2 shard_map.132
  179.3 5.7 %all-to-all-start.7 = ((f32[16,24,128]{2,1,0:T(8,128)}), f32[16,24,128]{2,1,0:T(8,128)S(1)}, u32[]{:S(2)}, u32[]{:S(2)}) async-start(f32[16,24,128]{2,1,0:T(8,128)} %get-tuple-element.172), calls=%async_computation.7 | async-start | bytes 393216 | tf_op jit(solution)/shard_map/all_to_all | solution.py:557
  184.9 7.1 %shard_map.124.refs_9_ = f32[160,1280]{1,0:T(8,128)S(1)} custom-call(s32[4]{0:T(128)S(1)} %pad_add_fusion.where, f32[2]{0:T(128)S(1)} %copy-done.10, f32[160,1280]{1,0:T(8,128)S(1)} %shard_map.119.refs_0_, f32[160,1280]{1,0:T(8,128)} %collective-permute-done.12.refs_1_, f32[160,1280]{1,0:T(8,128)} %collective-permute-done.13.refs_2_, ...), custom_call_target="tpu_custom_call" | custom-call | tf_op jit(solution)/shard_map/pallas_call | solution.py:39
  192.1 0.9 copy-done.5
  193.0 1.1 copy-done.6
  194.2 3.9 %shard_map.133 = (f32[8,128]{1,0:T(8,128)}, f32[2,160,512]{2,1,0:T(8,128)}) custom-call(s32[4]{0:T(128)S(1)} %pad_add_fusion.where, f32[2]{0:T(128)S(1)} %copy-done.10, f32[4,128,2048]{2,1,0:T(8,128)} %refs_0_.15, f32[256,128]{1,0:T(8,128)S(1)} %get-tuple-element.91.refs_1_, f32[16,128]{1,0:T(8,128)S(1)} %get-tuple-element.92.refs_2_, ...), custom_call_target="tpu_custom_call" | custom-call | tf_op jit(solution)/shard_map/pallas_call | solution.py:39
  (49 shorter events, 0.7 us)
Async XLA Ops:
  0.6 19.2 %copy-start.2 = (f32[2,160,512]{2,1,0:T(8,128)S(1)}, f32[2,160,512]{2,1,0:T(8,128)}, u32[]{:S(2)}) copy-start(f32[2,160,512]{2,1,0:T(8,128)} %outer.3) | copy-start | bytes 1966084
  0.6 31.5 %copy-start.9 = (f32[2]{0:T(128)S(1)}, f32[2]{0:T(128)}, u32[]{:S(2)}) copy-start(f32[2]{0:T(128)} %strengths.19) | copy-start | bytes 28
  0.7 0.7 copy-start.15
  5.1 2.2 %collective-permute-start = (f32[224,128]{1,0:T(8,128)S(1)}, f32[224,128]{1,0:T(8,128)S(1)}, u32[]{:S(2)}, u32[]{:S(2)}) collective-permute-start(f32[224,128]{1,0:T(8,128)S(1)} %get-tuple-element.94), channel_id=1, source_target_pairs={{0,16},{32,48},{64,80},{96,112},{16,0},{48,32},{80,64},{112,96},{1... | collective-permute-start | bytes 344072 | tf_op jit(solution)/shard_map/ppermute | solution.py:547
  5.2 6.1 %collective-permute-start.1 = (f32[224,128]{1,0:T(8,128)S(1)}, f32[224,128]{1,0:T(8,128)S(1)}, u32[]{:S(2)}, u32[]{:S(2)}) collective-permute-start(f32[224,128]{1,0:T(8,128)S(1)} %get-tuple-element.95), channel_id=1, source_target_pairs={{16,32},{48,64},{80,96},{32,16},{64,48},{96,80},{17,33},{49,65},{8... | collective-permute-start | bytes 344072 | tf_op jit(solution)/shard_map/ppermute | solution.py:548
  12.7 19.5 %all-to-all-start = ((f32[16,56,128]{2,1,0:T(8,128)}), f32[16,56,128]{2,1,0:T(8,128)S(1)}, u32[]{:S(2)}, u32[]{:S(2)}) async-start(f32[16,56,128]{2,1,0:T(8,128)} %get-tuple-element.99), calls=%async_computation | async-start | bytes 917504 | tf_op jit(solution)/shard_map/all_to_all | solution.py:557
  19.9 12.2 %collective-permute-start.3 = (f32[2,160,128]{2,1,0:T(8,128)S(1)}, f32[2,160,128]{2,1,0:T(8,128)S(1)}, u32[]{:S(2)}, u32[]{:S(2)}) collective-permute-start(f32[2,160,128]{2,1,0:T(8,128)S(1)} %get-tuple-element.182), channel_id=1, source_target_pairs={{1,2},{3,4},{5,6},{7,8},{9,10},{11,12},{13,14},{2,1},{4,3},{6,5},{... | collective-permute-start | bytes 491528 | tf_op jit(solution)/shard_map/ppermute | solution.py:568
  23.3 8.8 %collective-permute-start.2 = (f32[2,160,128]{2,1,0:T(8,128)S(1)}, f32[2,160,128]{2,1,0:T(8,128)S(1)}, u32[]{:S(2)}, u32[]{:S(2)}) collective-permute-start(f32[2,160,128]{2,1,0:T(8,128)S(1)} %get-tuple-element.183), channel_id=1, source_target_pairs={{0,1},{2,3},{4,5},{6,7},{8,9},{10,11},{12,13},{14,15},{1,0},{3,2},... | collective-permute-start | bytes 491528 | tf_op jit(solution)/shard_map/ppermute | solution.py:567
  32.2 10.4 %copy-start.7 = (f32[2,160,128]{2,1,0:T(8,128)}, f32[2,160,128]{2,1,0:T(8,128)S(1)}, u32[]{:S(2)}) copy-start(f32[2,160,128]{2,1,0:T(8,128)S(1)} %collective-permute-done.2.by_even) | copy-start | bytes 491524
  36.0 6.6 %copy-start.13 = (f32[16,128]{1,0:T(8,128)}, f32[16,128]{1,0:T(8,128)S(1)}, u32[]{:S(2)}) copy-start(f32[16,128]{1,0:T(8,128)S(1)} %get-tuple-element.126.refs_6_) | copy-start | bytes 24580
  36.0 2.2 %collective-permute-start.4 = (f32[64,128]{1,0:T(8,128)S(1)}, f32[64,128]{1,0:T(8,128)S(1)}, u32[]{:S(2)}, u32[]{:S(2)}) collective-permute-start(f32[64,128]{1,0:T(8,128)S(1)} %get-tuple-element.113), channel_id=1, source_target_pairs={{0,16},{32,48},{64,80},{96,112},{16,0},{48,32},{80,64},{112,96},{1... | collective-permute-start | bytes 98312 | tf_op jit(solution)/shard_map/ppermute | solution.py:547
  36.1 5.2 %collective-permute-start.5 = (f32[64,128]{1,0:T(8,128)S(1)}, f32[64,128]{1,0:T(8,128)S(1)}, u32[]{:S(2)}, u32[]{:S(2)}) collective-permute-start(f32[64,128]{1,0:T(8,128)S(1)} %get-tuple-element.114), channel_id=1, source_target_pairs={{16,32},{48,64},{80,96},{32,16},{64,48},{96,80},{17,33},{49,65},{8... | collective-permute-start | bytes 98312 | tf_op jit(solution)/shard_map/ppermute | solution.py:548
  42.6 14.7 %copy-start.11 = (f32[32,128]{1,0:T(8,128)}, f32[32,128]{1,0:T(8,128)S(1)}, u32[]{:S(2)}) copy-start(f32[32,128]{1,0:T(8,128)S(1)} %get-tuple-element.128.refs_8_) | copy-start | bytes 49156
  42.6 12.2 %all-to-all-start.1 = ((f32[16,24,128]{2,1,0:T(8,128)}), f32[16,24,128]{2,1,0:T(8,128)S(1)}, u32[]{:S(2)}, u32[]{:S(2)}) async-start(f32[16,24,128]{2,1,0:T(8,128)} %get-tuple-element.115), calls=%async_computation.1 | async-start | bytes 393216 | tf_op jit(solution)/shard_map/all_to_all | solution.py:557
  48.4 0.9 copy-start.8
  49.9 33.7 %copy-start.3 = (f32[160,1280]{1,0:T(8,128)}, f32[160,1280]{1,0:T(8,128)S(1)}, u32[]{:S(2)}) copy-start(f32[160,1280]{1,0:T(8,128)S(1)} %shard_map.118.refs_0_) | copy-start | bytes 2457604
  54.8 26.4 %copy-start = (f32[4,128,2048]{2,1,0:T(8,128)S(1)}, f32[4,128,2048]{2,1,0:T(8,128)}, u32[]{:S(2)}) copy-start(f32[4,128,2048]{2,1,0:T(8,128)} %refs_0_.15) | copy-start | bytes 12582916
  54.8 41.0 %collective-permute-start.7 = (f32[160,1280]{1,0:T(8,128)S(1)}, f32[160,1280]{1,0:T(8,128)}, u32[]{:S(2)}, u32[]{:S(2)}) collective-permute-start(f32[160,1280]{1,0:T(8,128)S(1)} %shard_map.118.refs_0_), channel_id=1, source_target_pairs={{16,32},{48,64},{80,96},{32,16},{64,48},{96,80},{17,33},{49,65},{8... | collective-permute-start | bytes 2457608 | tf_op jit(solution)/shard_map/ppermute | solution.py:590
  57.0 38.8 %collective-permute-start.6 = (f32[160,1280]{1,0:T(8,128)S(1)}, f32[160,1280]{1,0:T(8,128)}, u32[]{:S(2)}, u32[]{:S(2)}) collective-permute-start(f32[160,1280]{1,0:T(8,128)S(1)} %shard_map.118.refs_0_), channel_id=1, source_target_pairs={{0,16},{32,48},{64,80},{96,112},{16,0},{48,32},{80,64},{112,96},{1... | collective-permute-start | bytes 2457608 | tf_op jit(solution)/shard_map/ppermute | solution.py:589
  57.3 0.7 copy-start.10
  57.9 0.7 copy-start.12
  58.7 0.7 copy-start.14
  63.2 4.0 %collective-permute-start.8 = (f32[64,128]{1,0:T(8,128)S(1)}, f32[64,128]{1,0:T(8,128)S(1)}, u32[]{:S(2)}, u32[]{:S(2)}) collective-permute-start(f32[64,128]{1,0:T(8,128)S(1)} %get-tuple-element.130), channel_id=1, source_target_pairs={{0,16},{32,48},{64,80},{96,112},{16,0},{48,32},{80,64},{112,96},{1... | collective-permute-start | bytes 98312 | tf_op jit(solution)/shard_map/ppermute | solution.py:547
  63.6 5.5 %collective-permute-start.9 = (f32[64,128]{1,0:T(8,128)S(1)}, f32[64,128]{1,0:T(8,128)S(1)}, u32[]{:S(2)}, u32[]{:S(2)}) collective-permute-start(f32[64,128]{1,0:T(8,128)S(1)} %get-tuple-element.131), channel_id=1, source_target_pairs={{16,32},{48,64},{80,96},{32,16},{64,48},{96,80},{17,33},{49,65},{8... | collective-permute-start | bytes 98312 | tf_op jit(solution)/shard_map/ppermute | solution.py:548
  83.6 3.7 %collective-permute-start.10 = (f32[64,128]{1,0:T(8,128)S(1)}, f32[64,128]{1,0:T(8,128)S(1)}, u32[]{:S(2)}, u32[]{:S(2)}) collective-permute-start(f32[64,128]{1,0:T(8,128)S(1)} %get-tuple-element.137), channel_id=1, source_target_pairs={{0,16},{32,48},{64,80},{96,112},{16,0},{48,32},{80,64},{112,96},{1... | collective-permute-start | bytes 98312 | tf_op jit(solution)/shard_map/ppermute | solution.py:547
  83.7 5.2 %collective-permute-start.11 = (f32[64,128]{1,0:T(8,128)S(1)}, f32[64,128]{1,0:T(8,128)S(1)}, u32[]{:S(2)}, u32[]{:S(2)}) collective-permute-start(f32[64,128]{1,0:T(8,128)S(1)} %get-tuple-element.138), channel_id=1, source_target_pairs={{16,32},{48,64},{80,96},{32,16},{64,48},{96,80},{17,33},{49,65},{8... | collective-permute-start | bytes 98312 | tf_op jit(solution)/shard_map/ppermute | solution.py:548
  90.2 14.1 %all-to-all-start.3 = ((f32[16,24,128]{2,1,0:T(8,128)}), f32[16,24,128]{2,1,0:T(8,128)S(1)}, u32[]{:S(2)}, u32[]{:S(2)}) async-start(f32[16,24,128]{2,1,0:T(8,128)} %get-tuple-element.139), calls=%async_computation.3 | async-start | bytes 393216 | tf_op jit(solution)/shard_map/all_to_all | solution.py:557
  95.9 1.1 copy-start.4
  108.1 3.7 %collective-permute-start.14 = (f32[64,128]{1,0:T(8,128)S(1)}, f32[64,128]{1,0:T(8,128)S(1)}, u32[]{:S(2)}, u32[]{:S(2)}) collective-permute-start(f32[64,128]{1,0:T(8,128)S(1)} %get-tuple-element.149), channel_id=1, source_target_pairs={{0,16},{32,48},{64,80},{96,112},{16,0},{48,32},{80,64},{112,96},{1... | collective-permute-start | bytes 98312 | tf_op jit(solution)/shard_map/ppermute | solution.py:547
  108.2 5.2 %collective-permute-start.15 = (f32[64,128]{1,0:T(8,128)S(1)}, f32[64,128]{1,0:T(8,128)S(1)}, u32[]{:S(2)}, u32[]{:S(2)}) collective-permute-start(f32[64,128]{1,0:T(8,128)S(1)} %get-tuple-element.150), channel_id=1, source_target_pairs={{16,32},{48,64},{80,96},{32,16},{64,48},{96,80},{17,33},{49,65},{8... | collective-permute-start | bytes 98312 | tf_op jit(solution)/shard_map/ppermute | solution.py:548
  114.6 13.7 %all-to-all-start.4 = ((f32[16,24,128]{2,1,0:T(8,128)}), f32[16,24,128]{2,1,0:T(8,128)S(1)}, u32[]{:S(2)}, u32[]{:S(2)}) async-start(f32[16,24,128]{2,1,0:T(8,128)} %get-tuple-element.151), calls=%async_computation.4 | async-start | bytes 393216 | tf_op jit(solution)/shard_map/all_to_all | solution.py:557
  121.9 63.0 %collective-permute-start.13 = (f32[160,1280]{1,0:T(8,128)S(1)}, f32[160,1280]{1,0:T(8,128)}, u32[]{:S(2)}, u32[]{:S(2)}) collective-permute-start(f32[160,1280]{1,0:T(8,128)S(1)} %shard_map.119.refs_0_), channel_id=1, source_target_pairs={{16,32},{48,64},{80,96},{32,16},{64,48},{96,80},{17,33},{49,65},{8... | collective-permute-start | bytes 2457608 | tf_op jit(solution)/shard_map/ppermute | solution.py:590
  124.9 60.0 %collective-permute-start.12 = (f32[160,1280]{1,0:T(8,128)S(1)}, f32[160,1280]{1,0:T(8,128)}, u32[]{:S(2)}, u32[]{:S(2)}) collective-permute-start(f32[160,1280]{1,0:T(8,128)S(1)} %shard_map.119.refs_0_), channel_id=1, source_target_pairs={{0,16},{32,48},{64,80},{96,112},{16,0},{48,32},{80,64},{112,96},{1... | collective-permute-start | bytes 2457608 | tf_op jit(solution)/shard_map/ppermute | solution.py:589
  128.3 21.9 %copy-start.1 = (f32[4,128,2048]{2,1,0:T(8,128)S(1)}, f32[4,128,2048]{2,1,0:T(8,128)}, u32[]{:S(2)}) copy-start(f32[4,128,2048]{2,1,0:T(8,128)} %refs_0_.15) | copy-start | bytes 12582916
  132.4 3.7 %collective-permute-start.16 = (f32[64,128]{1,0:T(8,128)S(1)}, f32[64,128]{1,0:T(8,128)S(1)}, u32[]{:S(2)}, u32[]{:S(2)}) collective-permute-start(f32[64,128]{1,0:T(8,128)S(1)} %get-tuple-element.156), channel_id=1, source_target_pairs={{0,16},{32,48},{64,80},{96,112},{16,0},{48,32},{80,64},{112,96},{1... | collective-permute-start | bytes 98312 | tf_op jit(solution)/shard_map/ppermute | solution.py:547
  132.5 5.2 %collective-permute-start.17 = (f32[64,128]{1,0:T(8,128)S(1)}, f32[64,128]{1,0:T(8,128)S(1)}, u32[]{:S(2)}, u32[]{:S(2)}) collective-permute-start(f32[64,128]{1,0:T(8,128)S(1)} %get-tuple-element.157), channel_id=1, source_target_pairs={{16,32},{48,64},{80,96},{32,16},{64,48},{96,80},{17,33},{49,65},{8... | collective-permute-start | bytes 98312 | tf_op jit(solution)/shard_map/ppermute | solution.py:548
  152.6 3.7 %collective-permute-start.18 = (f32[64,128]{1,0:T(8,128)S(1)}, f32[64,128]{1,0:T(8,128)S(1)}, u32[]{:S(2)}, u32[]{:S(2)}) collective-permute-start(f32[64,128]{1,0:T(8,128)S(1)} %get-tuple-element.163), channel_id=1, source_target_pairs={{0,16},{32,48},{64,80},{96,112},{16,0},{48,32},{80,64},{112,96},{1... | collective-permute-start | bytes 98312 | tf_op jit(solution)/shard_map/ppermute | solution.py:547
  152.7 5.2 %collective-permute-start.19 = (f32[64,128]{1,0:T(8,128)S(1)}, f32[64,128]{1,0:T(8,128)S(1)}, u32[]{:S(2)}, u32[]{:S(2)}) collective-permute-start(f32[64,128]{1,0:T(8,128)S(1)} %get-tuple-element.164), channel_id=1, source_target_pairs={{16,32},{48,64},{80,96},{32,16},{64,48},{96,80},{17,33},{49,65},{8... | collective-permute-start | bytes 98312 | tf_op jit(solution)/shard_map/ppermute | solution.py:548
  172.7 3.7 %collective-permute-start.20 = (f32[64,128]{1,0:T(8,128)S(1)}, f32[64,128]{1,0:T(8,128)S(1)}, u32[]{:S(2)}, u32[]{:S(2)}) collective-permute-start(f32[64,128]{1,0:T(8,128)S(1)} %get-tuple-element.170), channel_id=1, source_target_pairs={{0,16},{32,48},{64,80},{96,112},{16,0},{48,32},{80,64},{112,96},{1... | collective-permute-start | bytes 98312 | tf_op jit(solution)/shard_map/ppermute | solution.py:547
  172.8 5.2 %collective-permute-start.21 = (f32[64,128]{1,0:T(8,128)S(1)}, f32[64,128]{1,0:T(8,128)S(1)}, u32[]{:S(2)}, u32[]{:S(2)}) collective-permute-start(f32[64,128]{1,0:T(8,128)S(1)} %get-tuple-element.171), channel_id=1, source_target_pairs={{16,32},{48,64},{80,96},{32,16},{64,48},{96,80},{17,33},{49,65},{8... | collective-permute-start | bytes 98312 | tf_op jit(solution)/shard_map/ppermute | solution.py:548
  179.3 13.8 %all-to-all-start.7 = ((f32[16,24,128]{2,1,0:T(8,128)}), f32[16,24,128]{2,1,0:T(8,128)S(1)}, u32[]{:S(2)}, u32[]{:S(2)}) async-start(f32[16,24,128]{2,1,0:T(8,128)} %get-tuple-element.172), calls=%async_computation.7 | async-start | bytes 393216 | tf_op jit(solution)/shard_map/all_to_all | solution.py:557
  192.1 0.9 copy-start.5
  193.0 1.1 copy-start.6

commit v4 on v3

--- a/solution.py
+++ b/solution.py
@@ -332,13 +332,17 @@
     emit(where[0], c, f, dipole, surface, q_ref, a_ref, b_ref, up_ref, down_ref)
 
 
-def last_kernel(away, factor, step, where, strengths, *refs):
-    dipole, rest, copies = refs[0], refs[1:], None
-    if away:
-        copies = fetch(dipole, *rest[-2:])
-        dipole, rest = rest[-2], rest[:-2]
-    *given, bulk, c_ref, out_ref = rest
-    _, c_sum, _, f_sum = advance(copies, False, True, factor, strengths[step], dipole, *given)
+def last_kernel(factor, step, where, strengths, *refs):
+    *rest, dipole_ref, dipole_arrivals, bulk_arrivals = refs
+    dipole, *given, bulk, c_ref, out_ref = rest
+    copies = fetch(dipole, dipole_ref, dipole_arrivals)
+    moves = [
+        pltpu.make_async_copy(bulk.at[:, pl.ds(part * WIDTH, 512)], out_ref.at[part], bulk_arrivals.at[part])
+        for part in range(2)
+    ]
+    for move in moves:
+        move.start()
+    _, c_sum, _, f_sum = advance(copies, False, True, factor, strengths[step], dipole_ref, *given)
     c_ref[...] = c_sum
     lanes = rows_of(1, (OWN, 128))
     low = jnp.full((OWN, 128), where[1], jnp.int32) == 0
@@ -346,9 +350,8 @@
     for part in range(2):
         corner = f_sum[part * PTS : (part + 1) * PTS]
         corner = jnp.concatenate([corner, jnp.zeros((128 - PTS, 256), F32)], axis=0).T[:OWN]
-        base = part * WIDTH
-        out_ref[part, :, 0:128] = jnp.where(fixed, corner, bulk[:, base : base + 128])
-        out_ref[part, :, 128:512] = bulk[:, base + 128 : base + 512]
+        moves[part].wait()
+        out_ref[part, :, 0:128] = jnp.where(fixed, corner, out_ref[part, :, 0:128])
 
 
 def window_kernel(where, outer, by_even, by_odd, out_ref):
@@ -601,12 +604,12 @@
             )(*given)
         else:
             c, grid = call(
-                functools.partial(last_kernel, away, factor, step),
+                functools.partial(last_kernel, factor, step),
                 [sds(8, 128), sds(2, OWN, 512)],
                 smem=2,
-                scratch=DIPOLE if away else (),
-                hbm=(2,) if away else (),
-            )(*given, bulk)
+                scratch=(*DIPOLE, pltpu.SemaphoreType.DMA((2,))),
+                hbm=(2, len(given)),
+            )(*given, pltpu.with_memory_space_constraint(bulk, pltpu.HBM))
     return c.reshape(2, LB, 128), grid
 
 

time: 202 us -> 201 us (level)
    unnamed x32 -> x30, local copies, waits for them, and re-layouts: 6.93 us -> 5.79 us
where the time goes in v4:
time: 201 us; the launch traced here: 197 us
  starting transfers between devices  67.5 us (34%)
  Pallas kernels  53.8 us (27%)
  blocking collectives  35.3 us (18%)
  waiting for transfers between devices  33.5 us (17%)
  local copies, waits for them, and re-layouts  5.81 us (3%)
    pallas_call x20, Pallas kernels, run(): pl.pallas_call(kernel, out_shape=outs, in_specs=[SM] * smem + [HBM if n i...  50.1 us
    all_to_all x3, blocking collectives, local(): lax.all_to_all(q, 'outer', split_axis=0, concat_axis=0, tiled=True)  35.3 us
    all_to_all x5, starting transfers between devices, local(): lax.all_to_all(q, 'outer', split_axis=0, concat_axis=0, tiled=True)  31.5 us
    ppermute x8, starting transfers between devices, local(): from_b = lax.ppermute(to_b, 'inner', chips)  26 us
    ppermute x8, waiting for transfers between devices, local(): from_b = lax.ppermute(to_b, 'inner', chips)  16.9 us
    ppermute x1, waiting for transfers between devices, local(): by_odd = lax.ppermute(jnp.where(is_odd, tail, head), 'outer', odd)  8.43 us
    all_to_all x5, waiting for transfers between devices, local(): lax.all_to_all(q, 'outer', split_axis=0, concat_axis=0, tiled=True)  8.17 us
    unnamed x30, local copies, waits for them, and re-layouts  5.79 us
  transfers between devices with their start and end apart: 27, of which 11 were waited for; matrix products, arithmetic and copies ran while one was open for 0% of the time, Pallas kernels for 17%

profile of v4, /device:TPU:88, one launch (start us, length us, event | category | flops | bytes accessed | tf_op | source)
XLA Modules:
  0.0 197.4 jit_solution(17844979925990878997)
XLA Ops:
  0.7 0.7 copy-done.14
  1.5 3.7 %shard_map.113 = (f32[16,128]{1,0:T(8,128)S(1)}, f32[64,256]{1,0:T(8,128)S(1)}, f32[16,24,128]{2,1,0:T(8,128)S(1)}, f32[224,128]{1,0:T(8,128)S(1)}, f32[224,128]...) custom-call(s32[4]{0:T(128)S(1)} %pad_add_fusion.where, ...), custom_call_target="tpu_custom_call" | custom-call | tf_op jit(solution)/shard_map/pallas_call | solution.py:500
  5.2 2.1 %collective-permute-start.1 = (f32[224,128]{1,0:T(8,128)S(1)}, f32[224,128]{1,0:T(8,128)S(1)}, u32[]{:S(2)}, u32[]{:S(2)}) collective-permute-start(f32[224,128]{1,0:T(8,128)S(1)} %get-tuple-element.95), channel_id=1, source_target_pairs={{16,32},{48,64},{80,96},{32,16},{64,48},{96,80},{17,33},{49,65},{8... | collective-permute-start | bytes 344072 | tf_op jit(solution)/shard_map/ppermute | solution.py:551
  7.4 4.0 %collective-permute-done.1.refs_2_ = f32[224,128]{1,0:T(8,128)S(1)} collective-permute-done((f32[224,128]{1,0:T(8,128)S(1)}, f32[224,128]{1,0:T(8,128)S(1)}, u32[]{:S(2)}, u32[]{:S(2)}) %collective-permute-start.1) | collective-permute-done | bytes 114720 | tf_op jit(solution)/shard_map/ppermute | solution.py:551
  11.3 1.4 shard_map.114
  12.7 7.2 %all-to-all-start = ((f32[16,56,128]{2,1,0:T(8,128)}), f32[16,56,128]{2,1,0:T(8,128)S(1)}, u32[]{:S(2)}, u32[]{:S(2)}) async-start(f32[16,56,128]{2,1,0:T(8,128)} %get-tuple-element.99), calls=%async_computation | async-start | bytes 917504 | tf_op jit(solution)/shard_map/all_to_all | solution.py:560
  19.9 3.4 %collective-permute-start.3 = (f32[2,160,128]{2,1,0:T(8,128)S(1)}, f32[2,160,128]{2,1,0:T(8,128)S(1)}, u32[]{:S(2)}, u32[]{:S(2)}) collective-permute-start(f32[2,160,128]{2,1,0:T(8,128)S(1)} %get-tuple-element.182), channel_id=1, source_target_pairs={{1,2},{3,4},{5,6},{7,8},{9,10},{11,12},{13,14},{2,1},{4,3},{6,5},{... | collective-permute-start | bytes 491528 | tf_op jit(solution)/shard_map/ppermute | solution.py:571
  23.3 0.1 collective-permute-start.2
  23.4 0.3 shard_map.115
  23.7 8.4 %collective-permute-done.3.by_odd = f32[2,160,128]{2,1,0:T(8,128)S(1)} collective-permute-done((f32[2,160,128]{2,1,0:T(8,128)S(1)}, f32[2,160,128]{2,1,0:T(8,128)S(1)}, u32[]{:S(2)}, u32[]{:S(2)}) %collective-permute-start.3) | collective-permute-done | bytes 163872 | tf_op jit(solution)/shard_map/ppermute | solution.py:571
  32.2 3.8 %shard_map.116 = (f32[16,128]{1,0:T(8,128)S(1)}, f32[64,256]{1,0:T(8,128)S(1)}, f32[16,24,128]{2,1,0:T(8,128)S(1)}, f32[64,128]{1,0:T(8,128)S(1)}, f32[64,128]{1,0:T(8,128)S(1)}) custom-call(s32[4]{0:T(128)S(1)} %pad_add_fusion.where, f32[2]{0:T(128)S(1)} %copy-done.8, f32[4,128,2048]{2,1,0:T(8,128)} %refs_0_.15, f32[256,128]{1,0:T(8,128)S(1)} %get-tuple-element.91.refs_1_, ...), custom_call_target="tpu_custom_call" | custom-call | tf_op jit(solution)/shard_map/pallas_call | solution.py:39
  36.1 2.1 %collective-permute-start.5 = (f32[64,128]{1,0:T(8,128)S(1)}, f32[64,128]{1,0:T(8,128)S(1)}, u32[]{:S(2)}, u32[]{:S(2)}) collective-permute-start(f32[64,128]{1,0:T(8,128)S(1)} %get-tuple-element.114), channel_id=1, source_target_pairs={{16,32},{48,64},{80,96},{32,16},{64,48},{96,80},{17,33},{49,65},{8... | collective-permute-start | bytes 98312 | tf_op jit(solution)/shard_map/ppermute | solution.py:551
  38.3 3.1 %collective-permute-done.5.refs_2_ = f32[64,128]{1,0:T(8,128)S(1)} collective-permute-done((f32[64,128]{1,0:T(8,128)S(1)}, f32[64,128]{1,0:T(8,128)S(1)}, u32[]{:S(2)}, u32[]{:S(2)}) %collective-permute-start.5) | collective-permute-done | bytes 32800 | tf_op jit(solution)/shard_map/ppermute | solution.py:551
  41.4 1.2 shard_map.117
  42.6 5.8 %all-to-all-start.1 = ((f32[16,24,128]{2,1,0:T(8,128)}), f32[16,24,128]{2,1,0:T(8,128)S(1)}, u32[]{:S(2)}, u32[]{:S(2)}) async-start(f32[16,24,128]{2,1,0:T(8,128)} %get-tuple-element.115), calls=%async_computation.1 | async-start | bytes 393216 | tf_op jit(solution)/shard_map/all_to_all | solution.py:560
  48.4 0.9 copy-done.7
  49.3 0.6 shard_map.118.refs_0_
  49.9 4.9 %all-to-all-done.1.refs_5_ = f32[16,24,128]{2,1,0:T(8,128)S(1)} async-done(((f32[16,24,128]{2,1,0:T(8,128)}), f32[16,24,128]{2,1,0:T(8,128)S(1)}, u32[]{:S(2)}, u32[]{:S(2)}) %all-to-all-start.1) | async-done | bytes 196640 | tf_op jit(solution)/shard_map/all_to_all | solution.py:560
  54.8 2.2 %collective-permute-start.7 = (f32[160,1280]{1,0:T(8,128)S(1)}, f32[160,1280]{1,0:T(8,128)}, u32[]{:S(2)}, u32[]{:S(2)}) collective-permute-start(f32[160,1280]{1,0:T(8,128)S(1)} %shard_map.118.refs_0_), channel_id=1, source_target_pairs={{16,32},{48,64},{80,96},{32,16},{64,48},{96,80},{17,33},{49,65},{8... | collective-permute-start | bytes 2457608 | tf_op jit(solution)/shard_map/ppermute | solution.py:593
  57.0 0.3 collective-permute-start.6
  57.3 0.7 copy-done.9
  57.9 0.7 copy-done.11
  58.7 0.7 copy-done.13
  59.4 3.8 %shard_map.120 = (f32[16,128]{1,0:T(8,128)S(1)}, f32[64,256]{1,0:T(8,128)S(1)}, f32[16,24,128]{2,1,0:T(8,128)S(1)}, f32[64,128]{1,0:T(8,128)S(1)}, f32[64,128]{1,0:T(8,128)S(1)}) custom-call(s32[4]{0:T(128)S(1)} %pad_add_fusion.where, f32[2]{0:T(128)S(1)} %copy-done.9, f32[4,128,2048]{2,1,0:T(8,128)} %refs_0_.15, f32[256,128]{1,0:T(8,128)S(1)} %get-tuple-element.91.refs_1_, ...), custom_call_target="tpu_custom_call" | custom-call | tf_op jit(solution)/shard_map/pallas_call | solution.py:39
  63.2 0.4 collective-permute-start.8
  63.6 3.6 %collective-permute-start.9 = (f32[64,128]{1,0:T(8,128)S(1)}, f32[64,128]{1,0:T(8,128)S(1)}, u32[]{:S(2)}, u32[]{:S(2)}) collective-permute-start(f32[64,128]{1,0:T(8,128)S(1)} %get-tuple-element.131), channel_id=1, source_target_pairs={{16,32},{48,64},{80,96},{32,16},{64,48},{96,80},{17,33},{49,65},{8... | collective-permute-start | bytes 98312 | tf_op jit(solution)/shard_map/ppermute | solution.py:551
  67.2 1.9 collective-permute-done.9.refs_2_
  69.1 0.6 shard_map.121
  69.7 11.6 %all_to_all.40.refs_5_ = f32[16,24,128]{2,1,0:T(8,128)S(1)} all-to-all(f32[16,24,128]{2,1,0:T(8,128)S(1)} %get-tuple-element.132), channel_id=1, replica_groups=mesh['inner'=8,'outer'=16] {'outer'}, dimensions={0} | all-to-all | bytes 393216 | tf_op jit(solution)/shard_map/all_to_all | solution.py:560
  81.3 2.3 %shard_map.122 = (f32[16,128]{1,0:T(8,128)S(1)}, f32[64,256]{1,0:T(8,128)S(1)}, f32[16,24,128]{2,1,0:T(8,128)S(1)}, f32[64,128]{1,0:T(8,128)S(1)}, f32[64,128]{1,0:T(8,128)S(1)}) custom-call(s32[4]{0:T(128)S(1)} %pad_add_fusion.where, f32[2]{0:T(128)S(1)} %copy-done.9, f32[4,128,2048]{2,1,0:T(8,128)S(1)} %copy-done, ...), custom_call_target="tpu_custom_call" | custom-call | tf_op jit(solution)/shard_map/pallas_call | solution.py:39
  83.6 0.1 collective-permute-start.10
  83.7 3.6 %collective-permute-start.11 = (f32[64,128]{1,0:T(8,128)S(1)}, f32[64,128]{1,0:T(8,128)S(1)}, u32[]{:S(2)}, u32[]{:S(2)}) collective-permute-start(f32[64,128]{1,0:T(8,128)S(1)} %get-tuple-element.138), channel_id=1, source_target_pairs={{16,32},{48,64},{80,96},{32,16},{64,48},{96,80},{17,33},{49,65},{8... | collective-permute-start | bytes 98312 | tf_op jit(solution)/shard_map/ppermute | solution.py:551
  87.4 1.6 collective-permute-done.11.refs_2_
  88.9 1.2 shard_map.123
  90.2 5.7 %all-to-all-start.3 = ((f32[16,24,128]{2,1,0:T(8,128)}), f32[16,24,128]{2,1,0:T(8,128)S(1)}, u32[]{:S(2)}, u32[]{:S(2)}) async-start(f32[16,24,128]{2,1,0:T(8,128)} %get-tuple-element.139), calls=%async_computation.3 | async-start | bytes 393216 | tf_op jit(solution)/shard_map/all_to_all | solution.py:560
  95.9 1.1 copy-done.4
  97.0 7.2 %shard_map.119.refs_0_ = f32[160,1280]{1,0:T(8,128)S(1)} custom-call(s32[4]{0:T(128)S(1)} %pad_add_fusion.where, f32[2]{0:T(128)S(1)} %copy-done.9, f32[160,1280]{1,0:T(8,128)S(1)} %copy-done.4, f32[160,1280]{1,0:T(8,128)} %collective-permute-done.6.refs_1_, f32[160,1280]{1,0:T(8,128)} %collective-permute-done.7.refs_2_, ...), custom_call_target="tpu_custom_call" | custom-call | tf_op jit(solution)/shard_map/pallas_call | solution.py:39
  104.2 3.8 %shard_map.125 = (f32[16,128]{1,0:T(8,128)S(1)}, f32[64,256]{1,0:T(8,128)S(1)}, f32[16,24,128]{2,1,0:T(8,128)S(1)}, f32[64,128]{1,0:T(8,128)S(1)}, f32[64,128]{1,0:T(8,128)S(1)}) custom-call(s32[4]{0:T(128)S(1)} %pad_add_fusion.where, f32[2]{0:T(128)S(1)} %copy-done.9, f32[4,128,2048]{2,1,0:T(8,128)} %refs_0_.15, f32[256,128]{1,0:T(8,128)S(1)} %get-tuple-element.91.refs_1_, ...), custom_call_target="tpu_custom_call" | custom-call | tf_op jit(solution)/shard_map/pallas_call | solution.py:39
  108.1 0.1 collective-permute-start.14
  108.2 3.6 %collective-permute-start.15 = (f32[64,128]{1,0:T(8,128)S(1)}, f32[64,128]{1,0:T(8,128)S(1)}, u32[]{:S(2)}, u32[]{:S(2)}) collective-permute-start(f32[64,128]{1,0:T(8,128)S(1)} %get-tuple-element.150), channel_id=1, source_target_pairs={{16,32},{48,64},{80,96},{32,16},{64,48},{96,80},{17,33},{49,65},{8... | collective-permute-start | bytes 98312 | tf_op jit(solution)/shard_map/ppermute | solution.py:551
  111.8 1.6 collective-permute-done.15.refs_2_
  113.4 1.2 shard_map.126
  114.6 7.3 %all-to-all-start.4 = ((f32[16,24,128]{2,1,0:T(8,128)}), f32[16,24,128]{2,1,0:T(8,128)S(1)}, u32[]{:S(2)}, u32[]{:S(2)}) async-start(f32[16,24,128]{2,1,0:T(8,128)} %get-tuple-element.151), calls=%async_computation.4 | async-start | bytes 393216 | tf_op jit(solution)/shard_map/all_to_all | solution.py:560
  121.9 3.0 %collective-permute-start.13 = (f32[160,1280]{1,0:T(8,128)S(1)}, f32[160,1280]{1,0:T(8,128)}, u32[]{:S(2)}, u32[]{:S(2)}) collective-permute-start(f32[160,1280]{1,0:T(8,128)S(1)} %shard_map.119.refs_0_), channel_id=1, source_target_pairs={{16,32},{48,64},{80,96},{32,16},{64,48},{96,80},{17,33},{49,65},{8... | collective-permute-start | bytes 2457608 | tf_op jit(solution)/shard_map/ppermute | solution.py:593
  124.9 0.1 collective-permute-start.12
  125.0 3.3 %all-to-all-done.4.refs_5_ = f32[16,24,128]{2,1,0:T(8,128)S(1)} async-done(((f32[16,24,128]{2,1,0:T(8,128)}), f32[16,24,128]{2,1,0:T(8,128)S(1)}, u32[]{:S(2)}, u32[]{:S(2)}) %all-to-all-start.4) | async-done | bytes 196640 | tf_op jit(solution)/shard_map/all_to_all | solution.py:560
  128.3 4.1 %shard_map.127 = (f32[16,128]{1,0:T(8,128)S(1)}, f32[64,256]{1,0:T(8,128)S(1)}, f32[16,24,128]{2,1,0:T(8,128)S(1)}, f32[64,128]{1,0:T(8,128)S(1)}, f32[64,128]{1,0:T(8,128)S(1)}) custom-call(s32[4]{0:T(128)S(1)} %pad_add_fusion.where, f32[2]{0:T(128)S(1)} %copy-done.9, f32[4,128,2048]{2,1,0:T(8,128)} %refs_0_.15, f32[256,128]{1,0:T(8,128)S(1)} %get-tuple-element.91.refs_1_, ...), custom_call_target="tpu_custom_call" | custom-call | tf_op jit(solution)/shard_map/pallas_call | solution.py:39
  132.5 3.6 %collective-permute-start.17 = (f32[64,128]{1,0:T(8,128)S(1)}, f32[64,128]{1,0:T(8,128)S(1)}, u32[]{:S(2)}, u32[]{:S(2)}) collective-permute-start(f32[64,128]{1,0:T(8,128)S(1)} %get-tuple-element.157), channel_id=1, source_target_pairs={{16,32},{48,64},{80,96},{32,16},{64,48},{96,80},{17,33},{49,65},{8... | collective-permute-start | bytes 98312 | tf_op jit(solution)/shard_map/ppermute | solution.py:551
  136.2 1.6 collective-permute-done.17.refs_2_
  137.8 0.6 shard_map.128
  138.3 11.9 %all_to_all.41.refs_5_ = f32[16,24,128]{2,1,0:T(8,128)S(1)} all-to-all(f32[16,24,128]{2,1,0:T(8,128)S(1)} %get-tuple-element.158), channel_id=1, replica_groups=mesh['inner'=8,'outer'=16] {'outer'}, dimensions={0} | all-to-all | bytes 393216 | tf_op jit(solution)/shard_map/all_to_all | solution.py:560
  150.2 2.3 %shard_map.129 = (f32[16,128]{1,0:T(8,128)S(1)}, f32[64,256]{1,0:T(8,128)S(1)}, f32[16,24,128]{2,1,0:T(8,128)S(1)}, f32[64,128]{1,0:T(8,128)S(1)}, f32[64,128]{1,0:T(8,128)S(1)}) custom-call(s32[4]{0:T(128)S(1)} %pad_add_fusion.where, f32[2]{0:T(128)S(1)} %copy-done.9, f32[4,128,2048]{2,1,0:T(8,128)S(1)} %copy-done.1, ...), custom_call_target="tpu_custom_call" | custom-call | tf_op jit(solution)/shard_map/pallas_call | solution.py:39
  152.7 3.6 %collective-permute-start.19 = (f32[64,128]{1,0:T(8,128)S(1)}, f32[64,128]{1,0:T(8,128)S(1)}, u32[]{:S(2)}, u32[]{:S(2)}) collective-permute-start(f32[64,128]{1,0:T(8,128)S(1)} %get-tuple-element.164), channel_id=1, source_target_pairs={{16,32},{48,64},{80,96},{32,16},{64,48},{96,80},{17,33},{49,65},{8... | collective-permute-start | bytes 98312 | tf_op jit(solution)/shard_map/ppermute | solution.py:551
  156.3 1.6 collective-permute-done.19.refs_2_
  157.9 0.6 shard_map.130
  158.5 11.9 %all_to_all.42.refs_5_ = f32[16,24,128]{2,1,0:T(8,128)S(1)} all-to-all(f32[16,24,128]{2,1,0:T(8,128)S(1)} %get-tuple-element.165), channel_id=1, replica_groups=mesh['inner'=8,'outer'=16] {'outer'}, dimensions={0} | all-to-all | bytes 393216 | tf_op jit(solution)/shard_map/all_to_all | solution.py:560
  170.4 2.3 %shard_map.131 = (f32[16,128]{1,0:T(8,128)S(1)}, f32[64,256]{1,0:T(8,128)S(1)}, f32[16,24,128]{2,1,0:T(8,128)S(1)}, f32[64,128]{1,0:T(8,128)S(1)}, f32[64,128]{1,0:T(8,128)S(1)}) custom-call(s32[4]{0:T(128)S(1)} %pad_add_fusion.where, f32[2]{0:T(128)S(1)} %copy-done.9, f32[4,128,2048]{2,1,0:T(8,128)S(1)} %copy-done.1, ...), custom_call_target="tpu_custom_call" | custom-call | tf_op jit(solution)/shard_map/pallas_call | solution.py:39
  172.8 3.6 %collective-permute-start.21 = (f32[64,128]{1,0:T(8,128)S(1)}, f32[64,128]{1,0:T(8,128)S(1)}, u32[]{:S(2)}, u32[]{:S(2)}) collective-permute-start(f32[64,128]{1,0:T(8,128)S(1)} %get-tuple-element.171), channel_id=1, source_target_pairs={{16,32},{48,64},{80,96},{32,16},{64,48},{96,80},{17,33},{49,65},{8... | collective-permute-start | bytes 98312 | tf_op jit(solution)/shard_map/ppermute | solution.py:551
  176.4 1.6 collective-permute-done.21.refs_2_
  178.0 1.2 shard_map.132
  179.3 5.7 %all-to-all-start.7 = ((f32[16,24,128]{2,1,0:T(8,128)}), f32[16,24,128]{2,1,0:T(8,128)S(1)}, u32[]{:S(2)}, u32[]{:S(2)}) async-start(f32[16,24,128]{2,1,0:T(8,128)} %get-tuple-element.172), calls=%async_computation.7 | async-start | bytes 393216 | tf_op jit(solution)/shard_map/all_to_all | solution.py:560
  184.9 7.1 %shard_map.124.refs_9_ = f32[160,1280]{1,0:T(8,128)S(1)} custom-call(s32[4]{0:T(128)S(1)} %pad_add_fusion.where, f32[2]{0:T(128)S(1)} %copy-done.9, f32[160,1280]{1,0:T(8,128)S(1)} %shard_map.119.refs_0_, f32[160,1280]{1,0:T(8,128)} %collective-permute-done.12.refs_1_, f32[160,1280]{1,0:T(8,128)} %collective-permute-done.13.refs_2_, ...), custom_call_target="tpu_custom_call" | custom-call | tf_op jit(solution)/shard_map/pallas_call | solution.py:39
  192.1 0.9 copy-done.5
  193.0 4.2 %shard_map.133 = (f32[8,128]{1,0:T(8,128)}, f32[2,160,512]{2,1,0:T(8,128)}) custom-call(s32[4]{0:T(128)S(1)} %pad_add_fusion.where, f32[2]{0:T(128)S(1)} %copy-done.9, f32[4,128,2048]{2,1,0:T(8,128)} %refs_0_.15, f32[256,128]{1,0:T(8,128)S(1)} %get-tuple-element.91.refs_1_, f32[16,128]{1,0:T(8,128)S(1)} %get-tuple-element.92.refs_2_, ...), custom_call_target="tpu_custom_call" | custom-call | tf_op jit(solution)/shard_map/pallas_call | solution.py:39
  (47 shorter events, 0.7 us)
Async XLA Ops:
  0.6 19.2 %copy-start.2 = (f32[2,160,512]{2,1,0:T(8,128)S(1)}, f32[2,160,512]{2,1,0:T(8,128)}, u32[]{:S(2)}) copy-start(f32[2,160,512]{2,1,0:T(8,128)} %outer.3) | copy-start | bytes 1966084
  0.6 31.5 %copy-start.8 = (f32[2]{0:T(128)S(1)}, f32[2]{0:T(128)}, u32[]{:S(2)}) copy-start(f32[2]{0:T(128)} %strengths.19) | copy-start | bytes 28
  0.7 0.7 copy-start.14
  5.1 2.2 %collective-permute-start = (f32[224,128]{1,0:T(8,128)S(1)}, f32[224,128]{1,0:T(8,128)S(1)}, u32[]{:S(2)}, u32[]{:S(2)}) collective-permute-start(f32[224,128]{1,0:T(8,128)S(1)} %get-tuple-element.94), channel_id=1, source_target_pairs={{0,16},{32,48},{64,80},{96,112},{16,0},{48,32},{80,64},{112,96},{1... | collective-permute-start | bytes 344072 | tf_op jit(solution)/shard_map/ppermute | solution.py:550
  5.2 6.1 %collective-permute-start.1 = (f32[224,128]{1,0:T(8,128)S(1)}, f32[224,128]{1,0:T(8,128)S(1)}, u32[]{:S(2)}, u32[]{:S(2)}) collective-permute-start(f32[224,128]{1,0:T(8,128)S(1)} %get-tuple-element.95), channel_id=1, source_target_pairs={{16,32},{48,64},{80,96},{32,16},{64,48},{96,80},{17,33},{49,65},{8... | collective-permute-start | bytes 344072 | tf_op jit(solution)/shard_map/ppermute | solution.py:551
  12.7 19.5 %all-to-all-start = ((f32[16,56,128]{2,1,0:T(8,128)}), f32[16,56,128]{2,1,0:T(8,128)S(1)}, u32[]{:S(2)}, u32[]{:S(2)}) async-start(f32[16,56,128]{2,1,0:T(8,128)} %get-tuple-element.99), calls=%async_computation | async-start | bytes 917504 | tf_op jit(solution)/shard_map/all_to_all | solution.py:560
  19.9 12.2 %collective-permute-start.3 = (f32[2,160,128]{2,1,0:T(8,128)S(1)}, f32[2,160,128]{2,1,0:T(8,128)S(1)}, u32[]{:S(2)}, u32[]{:S(2)}) collective-permute-start(f32[2,160,128]{2,1,0:T(8,128)S(1)} %get-tuple-element.182), channel_id=1, source_target_pairs={{1,2},{3,4},{5,6},{7,8},{9,10},{11,12},{13,14},{2,1},{4,3},{6,5},{... | collective-permute-start | bytes 491528 | tf_op jit(solution)/shard_map/ppermute | solution.py:571
  23.3 8.8 %collective-permute-start.2 = (f32[2,160,128]{2,1,0:T(8,128)S(1)}, f32[2,160,128]{2,1,0:T(8,128)S(1)}, u32[]{:S(2)}, u32[]{:S(2)}) collective-permute-start(f32[2,160,128]{2,1,0:T(8,128)S(1)} %get-tuple-element.183), channel_id=1, source_target_pairs={{0,1},{2,3},{4,5},{6,7},{8,9},{10,11},{12,13},{14,15},{1,0},{3,2},... | collective-permute-start | bytes 491528 | tf_op jit(solution)/shard_map/ppermute | solution.py:570
  32.2 10.4 %copy-start.6 = (f32[2,160,128]{2,1,0:T(8,128)}, f32[2,160,128]{2,1,0:T(8,128)S(1)}, u32[]{:S(2)}) copy-start(f32[2,160,128]{2,1,0:T(8,128)S(1)} %collective-permute-done.2.by_even) | copy-start | bytes 491524
  36.0 6.6 %copy-start.12 = (f32[16,128]{1,0:T(8,128)}, f32[16,128]{1,0:T(8,128)S(1)}, u32[]{:S(2)}) copy-start(f32[16,128]{1,0:T(8,128)S(1)} %get-tuple-element.126.refs_6_) | copy-start | bytes 24580
  36.0 2.2 %collective-permute-start.4 = (f32[64,128]{1,0:T(8,128)S(1)}, f32[64,128]{1,0:T(8,128)S(1)}, u32[]{:S(2)}, u32[]{:S(2)}) collective-permute-start(f32[64,128]{1,0:T(8,128)S(1)} %get-tuple-element.113), channel_id=1, source_target_pairs={{0,16},{32,48},{64,80},{96,112},{16,0},{48,32},{80,64},{112,96},{1... | collective-permute-start | bytes 98312 | tf_op jit(solution)/shard_map/ppermute | solution.py:550
  36.1 5.2 %collective-permute-start.5 = (f32[64,128]{1,0:T(8,128)S(1)}, f32[64,128]{1,0:T(8,128)S(1)}, u32[]{:S(2)}, u32[]{:S(2)}) collective-permute-start(f32[64,128]{1,0:T(8,128)S(1)} %get-tuple-element.114), channel_id=1, source_target_pairs={{16,32},{48,64},{80,96},{32,16},{64,48},{96,80},{17,33},{49,65},{8... | collective-permute-start | bytes 98312 | tf_op jit(solution)/shard_map/ppermute | solution.py:551
  42.6 14.7 %copy-start.10 = (f32[32,128]{1,0:T(8,128)}, f32[32,128]{1,0:T(8,128)S(1)}, u32[]{:S(2)}) copy-start(f32[32,128]{1,0:T(8,128)S(1)} %get-tuple-element.128.refs_8_) | copy-start | bytes 49156
  42.6 12.2 %all-to-all-start.1 = ((f32[16,24,128]{2,1,0:T(8,128)}), f32[16,24,128]{2,1,0:T(8,128)S(1)}, u32[]{:S(2)}, u32[]{:S(2)}) async-start(f32[16,24,128]{2,1,0:T(8,128)} %get-tuple-element.115), calls=%async_computation.1 | async-start | bytes 393216 | tf_op jit(solution)/shard_map/all_to_all | solution.py:560
  48.4 0.9 copy-start.7
  49.9 33.7 %copy-start.3 = (f32[160,1280]{1,0:T(8,128)}, f32[160,1280]{1,0:T(8,128)S(1)}, u32[]{:S(2)}) copy-start(f32[160,1280]{1,0:T(8,128)S(1)} %shard_map.118.refs_0_) | copy-start | bytes 2457604
  54.8 26.4 %copy-start = (f32[4,128,2048]{2,1,0:T(8,128)S(1)}, f32[4,128,2048]{2,1,0:T(8,128)}, u32[]{:S(2)}) copy-start(f32[4,128,2048]{2,1,0:T(8,128)} %refs_0_.15) | copy-start | bytes 12582916
  54.8 41.0 %collective-permute-start.7 = (f32[160,1280]{1,0:T(8,128)S(1)}, f32[160,1280]{1,0:T(8,128)}, u32[]{:S(2)}, u32[]{:S(2)}) collective-permute-start(f32[160,1280]{1,0:T(8,128)S(1)} %shard_map.118.refs_0_), channel_id=1, source_target_pairs={{16,32},{48,64},{80,96},{32,16},{64,48},{96,80},{17,33},{49,65},{8... | collective-permute-start | bytes 2457608 | tf_op jit(solution)/shard_map/ppermute | solution.py:593
  57.0 38.8 %collective-permute-start.6 = (f32[160,1280]{1,0:T(8,128)S(1)}, f32[160,1280]{1,0:T(8,128)}, u32[]{:S(2)}, u32[]{:S(2)}) collective-permute-start(f32[160,1280]{1,0:T(8,128)S(1)} %shard_map.118.refs_0_), channel_id=1, source_target_pairs={{0,16},{32,48},{64,80},{96,112},{16,0},{48,32},{80,64},{112,96},{1... | collective-permute-start | bytes 2457608 | tf_op jit(solution)/shard_map/ppermute | solution.py:592
  57.3 0.7 copy-start.9
  57.9 0.7 copy-start.11
  58.7 0.7 copy-start.13
  63.2 4.0 %collective-permute-start.8 = (f32[64,128]{1,0:T(8,128)S(1)}, f32[64,128]{1,0:T(8,128)S(1)}, u32[]{:S(2)}, u32[]{:S(2)}) collective-permute-start(f32[64,128]{1,0:T(8,128)S(1)} %get-tuple-element.130), channel_id=1, source_target_pairs={{0,16},{32,48},{64,80},{96,112},{16,0},{48,32},{80,64},{112,96},{1... | collective-permute-start | bytes 98312 | tf_op jit(solution)/shard_map/ppermute | solution.py:550
  63.6 5.5 %collective-permute-start.9 = (f32[64,128]{1,0:T(8,128)S(1)}, f32[64,128]{1,0:T(8,128)S(1)}, u32[]{:S(2)}, u32[]{:S(2)}) collective-permute-start(f32[64,128]{1,0:T(8,128)S(1)} %get-tuple-element.131), channel_id=1, source_target_pairs={{16,32},{48,64},{80,96},{32,16},{64,48},{96,80},{17,33},{49,65},{8... | collective-permute-start | bytes 98312 | tf_op jit(solution)/shard_map/ppermute | solution.py:551
  83.6 3.7 %collective-permute-start.10 = (f32[64,128]{1,0:T(8,128)S(1)}, f32[64,128]{1,0:T(8,128)S(1)}, u32[]{:S(2)}, u32[]{:S(2)}) collective-permute-start(f32[64,128]{1,0:T(8,128)S(1)} %get-tuple-element.137), channel_id=1, source_target_pairs={{0,16},{32,48},{64,80},{96,112},{16,0},{48,32},{80,64},{112,96},{1... | collective-permute-start | bytes 98312 | tf_op jit(solution)/shard_map/ppermute | solution.py:550
  83.7 5.2 %collective-permute-start.11 = (f32[64,128]{1,0:T(8,128)S(1)}, f32[64,128]{1,0:T(8,128)S(1)}, u32[]{:S(2)}, u32[]{:S(2)}) collective-permute-start(f32[64,128]{1,0:T(8,128)S(1)} %get-tuple-element.138), channel_id=1, source_target_pairs={{16,32},{48,64},{80,96},{32,16},{64,48},{96,80},{17,33},{49,65},{8... | collective-permute-start | bytes 98312 | tf_op jit(solution)/shard_map/ppermute | solution.py:551
  90.2 14.1 %all-to-all-start.3 = ((f32[16,24,128]{2,1,0:T(8,128)}), f32[16,24,128]{2,1,0:T(8,128)S(1)}, u32[]{:S(2)}, u32[]{:S(2)}) async-start(f32[16,24,128]{2,1,0:T(8,128)} %get-tuple-element.139), calls=%async_computation.3 | async-start | bytes 393216 | tf_op jit(solution)/shard_map/all_to_all | solution.py:560
  95.9 1.1 copy-start.4
  108.1 3.7 %collective-permute-start.14 = (f32[64,128]{1,0:T(8,128)S(1)}, f32[64,128]{1,0:T(8,128)S(1)}, u32[]{:S(2)}, u32[]{:S(2)}) collective-permute-start(f32[64,128]{1,0:T(8,128)S(1)} %get-tuple-element.149), channel_id=1, source_target_pairs={{0,16},{32,48},{64,80},{96,112},{16,0},{48,32},{80,64},{112,96},{1... | collective-permute-start | bytes 98312 | tf_op jit(solution)/shard_map/ppermute | solution.py:550
  108.2 5.2 %collective-permute-start.15 = (f32[64,128]{1,0:T(8,128)S(1)}, f32[64,128]{1,0:T(8,128)S(1)}, u32[]{:S(2)}, u32[]{:S(2)}) collective-permute-start(f32[64,128]{1,0:T(8,128)S(1)} %get-tuple-element.150), channel_id=1, source_target_pairs={{16,32},{48,64},{80,96},{32,16},{64,48},{96,80},{17,33},{49,65},{8... | collective-permute-start | bytes 98312 | tf_op jit(solution)/shard_map/ppermute | solution.py:551
  114.6 13.7 %all-to-all-start.4 = ((f32[16,24,128]{2,1,0:T(8,128)}), f32[16,24,128]{2,1,0:T(8,128)S(1)}, u32[]{:S(2)}, u32[]{:S(2)}) async-start(f32[16,24,128]{2,1,0:T(8,128)} %get-tuple-element.151), calls=%async_computation.4 | async-start | bytes 393216 | tf_op jit(solution)/shard_map/all_to_all | solution.py:560
  121.9 63.0 %collective-permute-start.13 = (f32[160,1280]{1,0:T(8,128)S(1)}, f32[160,1280]{1,0:T(8,128)}, u32[]{:S(2)}, u32[]{:S(2)}) collective-permute-start(f32[160,1280]{1,0:T(8,128)S(1)} %shard_map.119.refs_0_), channel_id=1, source_target_pairs={{16,32},{48,64},{80,96},{32,16},{64,48},{96,80},{17,33},{49,65},{8... | collective-permute-start | bytes 2457608 | tf_op jit(solution)/shard_map/ppermute | solution.py:593
  124.9 60.0 %collective-permute-start.12 = (f32[160,1280]{1,0:T(8,128)S(1)}, f32[160,1280]{1,0:T(8,128)}, u32[]{:S(2)}, u32[]{:S(2)}) collective-permute-start(f32[160,1280]{1,0:T(8,128)S(1)} %shard_map.119.refs_0_), channel_id=1, source_target_pairs={{0,16},{32,48},{64,80},{96,112},{16,0},{48,32},{80,64},{112,96},{1... | collective-permute-start | bytes 2457608 | tf_op jit(solution)/shard_map/ppermute | solution.py:592
  128.3 21.9 %copy-start.1 = (f32[4,128,2048]{2,1,0:T(8,128)S(1)}, f32[4,128,2048]{2,1,0:T(8,128)}, u32[]{:S(2)}) copy-start(f32[4,128,2048]{2,1,0:T(8,128)} %refs_0_.15) | copy-start | bytes 12582916
  132.4 3.7 %collective-permute-start.16 = (f32[64,128]{1,0:T(8,128)S(1)}, f32[64,128]{1,0:T(8,128)S(1)}, u32[]{:S(2)}, u32[]{:S(2)}) collective-permute-start(f32[64,128]{1,0:T(8,128)S(1)} %get-tuple-element.156), channel_id=1, source_target_pairs={{0,16},{32,48},{64,80},{96,112},{16,0},{48,32},{80,64},{112,96},{1... | collective-permute-start | bytes 98312 | tf_op jit(solution)/shard_map/ppermute | solution.py:550
  132.5 5.2 %collective-permute-start.17 = (f32[64,128]{1,0:T(8,128)S(1)}, f32[64,128]{1,0:T(8,128)S(1)}, u32[]{:S(2)}, u32[]{:S(2)}) collective-permute-start(f32[64,128]{1,0:T(8,128)S(1)} %get-tuple-element.157), channel_id=1, source_target_pairs={{16,32},{48,64},{80,96},{32,16},{64,48},{96,80},{17,33},{49,65},{8... | collective-permute-start | bytes 98312 | tf_op jit(solution)/shard_map/ppermute | solution.py:551
  152.6 3.7 %collective-permute-start.18 = (f32[64,128]{1,0:T(8,128)S(1)}, f32[64,128]{1,0:T(8,128)S(1)}, u32[]{:S(2)}, u32[]{:S(2)}) collective-permute-start(f32[64,128]{1,0:T(8,128)S(1)} %get-tuple-element.163), channel_id=1, source_target_pairs={{0,16},{32,48},{64,80},{96,112},{16,0},{48,32},{80,64},{112,96},{1... | collective-permute-start | bytes 98312 | tf_op jit(solution)/shard_map/ppermute | solution.py:550
  152.7 5.2 %collective-permute-start.19 = (f32[64,128]{1,0:T(8,128)S(1)}, f32[64,128]{1,0:T(8,128)S(1)}, u32[]{:S(2)}, u32[]{:S(2)}) collective-permute-start(f32[64,128]{1,0:T(8,128)S(1)} %get-tuple-element.164), channel_id=1, source_target_pairs={{16,32},{48,64},{80,96},{32,16},{64,48},{96,80},{17,33},{49,65},{8... | collective-permute-start | bytes 98312 | tf_op jit(solution)/shard_map/ppermute | solution.py:551
  172.7 3.7 %collective-permute-start.20 = (f32[64,128]{1,0:T(8,128)S(1)}, f32[64,128]{1,0:T(8,128)S(1)}, u32[]{:S(2)}, u32[]{:S(2)}) collective-permute-start(f32[64,128]{1,0:T(8,128)S(1)} %get-tuple-element.170), channel_id=1, source_target_pairs={{0,16},{32,48},{64,80},{96,112},{16,0},{48,32},{80,64},{112,96},{1... | collective-permute-start | bytes 98312 | tf_op jit(solution)/shard_map/ppermute | solution.py:550
  172.8 5.2 %collective-permute-start.21 = (f32[64,128]{1,0:T(8,128)S(1)}, f32[64,128]{1,0:T(8,128)S(1)}, u32[]{:S(2)}, u32[]{:S(2)}) collective-permute-start(f32[64,128]{1,0:T(8,128)S(1)} %get-tuple-element.171), channel_id=1, source_target_pairs={{16,32},{48,64},{80,96},{32,16},{64,48},{96,80},{17,33},{49,65},{8... | collective-permute-start | bytes 98312 | tf_op jit(solution)/shard_map/ppermute | solution.py:551
  179.3 13.8 %all-to-all-start.7 = ((f32[16,24,128]{2,1,0:T(8,128)}), f32[16,24,128]{2,1,0:T(8,128)S(1)}, u32[]{:S(2)}, u32[]{:S(2)}) async-start(f32[16,24,128]{2,1,0:T(8,128)} %get-tuple-element.172), calls=%async_computation.7 | async-start | bytes 393216 | tf_op jit(solution)/shard_map/all_to_all | solution.py:560
  192.1 0.9 copy-start.5
